TPU v7x, 32 devices: a whole 2x2x4 slice. The times are simulated.
32 devices in a mesh: ctx: 8 (over z, y), fsdp: 4 (over x, core).
Axes of the slice: x: 2, y: 2, z: 4, core: 2. Of those that a mesh axis runs over, the one named last changes fastest.
Arguments:
- tokens: int32 [4096], P('ctx'), may hold values from 0 to 511
- embedding: bfloat16 [512, 4096], P(None, 'fsdp'), may hold values from -6 to 6
- norm_gain: float32 [4096], replicated, may hold values from 0.1 to 1.9
- in_weight: bfloat16 [4096, 3, 2048], P('ctx', None, 'fsdp'), may hold values from -0.09375 to 0.09375
- short_taps: float32 [7, 3, 2048], P(None, None, 'fsdp'), may hold values from -2 to 2
- decay_rates: float32 [16, 128], P(None, 'fsdp'), may hold values from 0.00012207031 to 0.1
- residue: float32 [16, 128], P(None, 'fsdp'), may hold values from -0.15625 to 0.15625
- skip_weight: float32 [2048], P('fsdp'), may hold values from -4 to 4
- out_weight: bfloat16 [2048, 4096], P('fsdp', 'ctx'), may hold values from -0.125 to 0.125
Outputs:
- mixed: bfloat16 [4096, 4096], P('ctx', 'fsdp')
All inputs are finite; a program needn't handle non-finite values.
Results may differ from a plain program's by a relative error of at most 0.018.
Values may be sent and summed in bfloat16 or wider, within the bound.
No kernel may reach another device: no remote copies, remote signals or barrier semaphores. Data moves between devices by JAX's collectives and lax.ppermute only.
A program may use at most 64 MiB of HBM per device.

v0:
```python
import functools

import jax
import jax.numpy as jnp
from jax import lax
from jax.experimental import pallas as pl
from jax.experimental.pallas import tpu as pltpu
from jax.sharding import PartitionSpec as P


GROUP = 16
CHUNK = 256
TILE = 512
EXTRA = 16
BASE = 16
AXES = ("ctx", "fsdp")
BF16 = jnp.bfloat16
F32 = jnp.float32


def send(value, ctx_count, fsdp_count, target):
    pairs = []
    for i in range(ctx_count):
        for j in range(fsdp_count):
            to = target(i, j)
            if to is not None:
                pairs.append((i * fsdp_count + j, to[0] * fsdp_count + to[1]))
    return lax.ppermute(value, AXES, pairs)


def after(values, *others):
    return lax.optimization_barrier((tuple(values), others))[0]


def split_high_low(value):
    high = value.astype(BF16)
    return high, (value - high.astype(F32)).astype(BF16)


def filter_body(decay_ref, residue_ref, decay_col_ref, residue_col_ref, near_ref, into_ref, outof_ref, step_ref):
    groups, modes = decay_ref.shape
    rows = lax.broadcasted_iota(jnp.int32, (CHUNK, CHUNK), 0)
    cols = lax.broadcasted_iota(jnp.int32, (CHUNK, CHUNK), 1)
    lag = (cols - rows).astype(F32)
    clipped = jnp.maximum(lag, 0.0)
    back = (CHUNK - 1 - lax.broadcasted_iota(jnp.int32, (CHUNK, modes), 0)).astype(F32)
    ahead = (1 + lax.broadcasted_iota(jnp.int32, (modes, CHUNK), 1)).astype(F32)
    for group in range(groups):
        total = jnp.zeros((CHUNK, CHUNK), F32)
        for mode in range(modes):
            total += residue_ref[group, mode] * jnp.exp(-decay_ref[group, mode] * clipped)
        near_ref[group] = jnp.where(lag >= 0.0, total, 0.0).astype(BF16)
        rate_row = decay_col_ref[group, 0:1, :]
        into_high, into_low = split_high_low(jnp.exp(-rate_row * back))
        into_ref[group] = jnp.concatenate([into_high, into_low], axis=1)
        rate_col = jnp.swapaxes(jnp.broadcast_to(rate_row, (8, modes)), 0, 1)[:, 0:1]
        residue_row = residue_col_ref[group, 0:1, :]
        residue_col = jnp.swapaxes(jnp.broadcast_to(residue_row, (8, modes)), 0, 1)[:, 0:1]
        outof_high, outof_low = split_high_low(residue_col * jnp.exp(-rate_col * ahead))
        outof_ref[group] = jnp.concatenate([outof_high, outof_high, outof_low], axis=0)
        step_ref[group] = jnp.exp(-rate_row * CHUNK)


def make_filters(decay, residue):
    groups, modes = decay.shape
    smem = pl.BlockSpec(memory_space=pltpu.SMEM)
    vmem = pl.BlockSpec(memory_space=pltpu.VMEM)
    return pl.pallas_call(
        filter_body,
        in_specs=[smem, smem, vmem, vmem],
        out_specs=[vmem] * 4,
        out_shape=[
            jax.ShapeDtypeStruct((groups, CHUNK, CHUNK), BF16),
            jax.ShapeDtypeStruct((groups, CHUNK, 2 * modes), BF16),
            jax.ShapeDtypeStruct((groups, 3 * modes, CHUNK), BF16),
            jax.ShapeDtypeStruct((groups, 1, modes), F32),
        ],
        name="filters",
    )(decay, residue, decay[:, None, :], residue[:, None, :])


def table_body(place_ref, own_ref, across_ref, beside_ref, gain_ref, *refs):
    out_ref, raw_ref, scaled_ref, extra_ref = refs[-4:]
    count = (len(refs) - 4) // 2
    weight_refs, token_refs = refs[:count], refs[count:2 * count]
    vocab, columns = own_ref.shape
    width = columns // count
    pieces, rows, _ = out_ref.shape
    low_at, origin = place_ref[0], place_ref[1]

    @pl.when(origin == 0)
    def _():
        raw_ref[...] = own_ref[...].astype(F32)

    @pl.when(origin == 1)
    def _():
        raw_ref[...] = across_ref[...].astype(F32)

    @pl.when(origin == 2)
    def _():
        raw_ref[...] = beside_ref[...].astype(F32)

    raw = raw_ref[...]
    scaled_ref[...] = (raw * gain_ref[...]).astype(BF16)
    extra_ref[...] = jnp.zeros_like(extra_ref)
    squares = jnp.broadcast_to(jnp.sum(raw * raw, axis=1, keepdims=True), (vocab, 128))
    squares = jnp.swapaxes(squares, 0, 1)[0:1, :]
    for row in range(3):
        rounded = squares.astype(BF16).astype(F32)
        extra_ref[row:row + 1, :] = rounded
        squares = squares - rounded
    for shift, token_ref in enumerate(token_refs):
        low = lax.rem(low_at + shift, count)
        extra_ref[pl.ds(3 + low, 1), :] = (token_ref[...] // BASE).astype(F32)
        extra_ref[pl.ds(3 + count + low, 1), :] = (token_ref[...] % BASE).astype(F32)
    extra = extra_ref[...].astype(BF16)
    each = (rows - EXTRA) // 3
    for piece in range(pieces):
        out_ref[piece, :EXTRA, :] = extra
    for kind in range(3):
        total = None
        for shift, weight_ref in enumerate(weight_refs):
            start = pl.multiple_of(lax.rem(low_at + shift, count) * width, width)
            part = jnp.dot(scaled_ref[:, pl.ds(start, width)], weight_ref[kind], preferred_element_type=F32)
            total = part if total is None else total + part
        flipped = jnp.swapaxes(total, 0, 1).astype(BF16)
        for piece in range(pieces):
            out_ref[piece, EXTRA + kind * each:EXTRA + (kind + 1) * each, :] = flipped[piece * each:(piece + 1) * each]


def make_table(place, own, across, beside, gain, weights, tokens, pieces):
    vocab = own.shape[0]
    channels = weights[0].shape[2]
    vmem = pl.BlockSpec(memory_space=pltpu.VMEM)
    return pl.pallas_call(
        table_body,
        in_specs=[pl.BlockSpec(memory_space=pltpu.SMEM)] + [vmem] * (4 + len(weights) + len(tokens)),
        out_specs=vmem,
        out_shape=jax.ShapeDtypeStruct((pieces, EXTRA + 3 * channels // pieces, vocab), BF16),
        scratch_shapes=[
            pltpu.VMEM(own.shape, F32),
            pltpu.VMEM(own.shape, BF16),
            pltpu.VMEM((EXTRA, vocab), F32),
        ],
        name="table",
    )(place, own, across, beside, gain, *weights, *tokens)


def mixer_body(width, place_ref, taps_ref, skip_ref, near_ref, into_ref, outof_ref, step_ref, *refs):
    piece_refs = refs[:-5]
    out_ref, query_ref, drive_ref, conv_ref, token_ref = refs[-5:]
    rows, vocab = piece_refs[0].shape
    rows -= EXTRA
    channels = rows // 3
    blocks, _, block = token_ref.shape
    length = blocks * block
    count = len(piece_refs)
    lows = blocks // count
    taps = taps_ref.shape[1]
    total = None
    squares = None
    for shift, ref in enumerate(piece_refs):
        head = ref[:EXTRA, :].astype(F32)
        summed = head[0:1] + head[1:2] + head[2:3]
        squares = summed if squares is None else squares + summed
        high = lax.rem(place_ref[0] // lows - shift + count, count)
        for low in range(lows):
            ids = head[3 + low:4 + low] * BASE + head[3 + lows + low:4 + lows + low]
            token_ref[high * lows + low] = ids[:, :block].astype(jnp.int32)
        part = ref[EXTRA:, :].astype(F32)
        total = part if total is None else total + part
    table = (total * lax.rsqrt(squares * (1.0 / width) + 1e-05)).astype(BF16)
    ids = lax.broadcasted_iota(jnp.int32, (vocab, TILE), 0)
    halo = jnp.zeros((rows, 128), F32)
    for tile in range(length // TILE):
        at = tile * TILE
        inside = at % block
        tokens = token_ref[at // block][:, inside:inside + TILE]
        hot = jnp.where(ids == tokens, 1.0, 0.0).astype(BF16)
        projected = jnp.dot(table, hot, preferred_element_type=F32)
        extended = jnp.concatenate([halo, projected], axis=1)
        halo = projected[:, TILE - 128:]
        short = taps_ref[:, 0:1] * projected
        for lag in range(1, taps):
            short += taps_ref[:, lag:lag + 1] * pltpu.roll(extended, lag, 1)[:, 128:]
        query_ref[:, at:at + TILE] = short[:channels]
        drive_ref[:, at:at + TILE] = short[channels:2 * channels] * short[2 * channels:]
    groups = near_ref.shape[0]
    per = channels // groups
    modes = step_ref.shape[2]
    chunks = length // CHUNK
    for group in range(groups):
        base = group * per
        stacked = jnp.concatenate(
            [drive_ref[base:base + per, n * CHUNK:(n + 1) * CHUNK] for n in range(chunks)], axis=0
        ).astype(BF16)
        both = jnp.dot(stacked, into_ref[group], preferred_element_type=F32)
        ends = both[:, :modes] + both[:, modes:]
        step = step_ref[group]
        state = jnp.zeros((per, modes), F32)
        starts = []
        for n in range(chunks):
            starts.append(state)
            state = state * step + ends[n * per:(n + 1) * per]
        high, low = split_high_low(jnp.concatenate(starts, axis=0))
        conv_ref[...] = jnp.dot(stacked, near_ref[group], preferred_element_type=F32) + jnp.dot(
            jnp.concatenate([high, low, high], axis=1), outof_ref[group], preferred_element_type=F32
        )
        for n in range(chunks):
            here = slice(n * CHUNK, (n + 1) * CHUNK)
            response = conv_ref[n * per:(n + 1) * per, :] + skip_ref[base:base + per, :] * drive_ref[base:base + per, here]
            out_ref[base:base + per, here] = (query_ref[base:base + per, here] * response).astype(BF16)


def make_mixer(place, width, block, taps, skip, filters, pieces, blocks):
    rows = pieces[0].shape[0] - EXTRA
    channels = rows // 3
    length = block * blocks
    groups = filters[0].shape[0]
    vmem = pl.BlockSpec(memory_space=pltpu.VMEM)
    return pl.pallas_call(
        functools.partial(mixer_body, width),
        in_specs=[pl.BlockSpec(memory_space=pltpu.SMEM)] + [vmem] * (6 + len(pieces)),
        out_specs=vmem,
        out_shape=jax.ShapeDtypeStruct((channels, length), BF16),
        scratch_shapes=[
            pltpu.VMEM((channels, length), F32),
            pltpu.VMEM((channels, length), F32),
            pltpu.VMEM((length // CHUNK * (channels // groups), CHUNK), F32),
            pltpu.VMEM((blocks, 1, block), jnp.int32),
        ],
        name="mixer",
    )(place, taps, skip, *filters, *pieces)


def order_body(place_ref, *refs):
    piece_refs, out_ref, stage_ref = refs[:-2], refs[-2], refs[-1]
    count = len(piece_refs)
    rows = piece_refs[0].shape[0]
    lows = place_ref[1]
    for shift, ref in enumerate(piece_refs):
        source = lax.rem(place_ref[0] - shift + count, count)
        start = pl.multiple_of((lax.rem(source, lows) * (count // lows) + source // lows) * rows, rows)
        stage_ref[pl.ds(start, rows), :] = ref[...].astype(F32)
    out_ref[...] = jnp.swapaxes(stage_ref[...], 0, 1).astype(BF16)


def make_order(place, pieces):
    rows, length = pieces[0].shape
    vmem = pl.BlockSpec(memory_space=pltpu.VMEM)
    return pl.pallas_call(
        order_body,
        in_specs=[pl.BlockSpec(memory_space=pltpu.SMEM)] + [vmem] * len(pieces),
        out_specs=vmem,
        out_shape=jax.ShapeDtypeStruct((length, rows * len(pieces)), BF16),
        scratch_shapes=[pltpu.VMEM((rows * len(pieces), length), F32)],
        name="order",
    )(place, *pieces)


def product_body(order, flips_ref, lows_ref, *refs):
    side_refs = refs[:len(order)]
    block_refs = refs[len(order):-3]
    out_ref, sides_ref, sum_ref = refs[-3:]
    for flip, ref in zip(order, side_refs):
        sides_ref[flip] = ref[...]
    full, cols = block_refs[0].shape
    sum_ref[...] = jnp.zeros_like(sum_ref)
    for at, ref in enumerate(block_refs):
        first = full // 2 if at == len(block_refs) - 1 else 0
        side = sides_ref[flips_ref[at], :, first:first + ref.shape[0]]
        sum_ref[lows_ref[at]] += jnp.dot(side, ref[...], preferred_element_type=F32)
    for low in range(sum_ref.shape[0]):
        out_ref[:, low * cols:(low + 1) * cols] = sum_ref[low].astype(BF16)


def make_product(flips, lows_at, order, sides, blocks, lows):
    length, full = sides[0].shape
    cols = blocks[0].shape[1]
    smem = pl.BlockSpec(memory_space=pltpu.SMEM)
    vmem = pl.BlockSpec(memory_space=pltpu.VMEM)
    return pl.pallas_call(
        functools.partial(product_body, order),
        in_specs=[smem, smem] + [vmem] * (len(sides) + len(blocks)),
        out_specs=vmem,
        out_shape=jax.ShapeDtypeStruct((length, lows * cols), BF16),
        scratch_shapes=[
            pltpu.VMEM((len(sides), length, full), BF16),
            pltpu.VMEM((lows, length, cols), F32),
        ],
        name="product",
    )(flips, lows_at, *sides, *blocks)


def reverse_bits(value, count):
    result = 0
    while count > 1:
        result, value, count = result * 2 + value % 2, value // 2, count // 2
    return result


def cycle_of(highs, lows):
    walk = [(high, 0) for high in range(highs)]
    for at in range(highs - 1, -1, -1):
        lows_at = range(1, lows) if (highs - 1 - at) % 2 == 0 else range(lows - 1, 0, -1)
        walk += [(at, low) for low in lows_at]
    return [high * lows + low for high, low in walk]


def body(
    tokens,
    embedding,
    norm_gain,
    in_weight,
    short_taps,
    decay_rates,
    residue,
    skip_weight,
    out_weight,
):
    ctx_count = lax.axis_size("ctx")
    fsdp_count = lax.axis_size("fsdp")
    lows = ctx_count // fsdp_count
    ctx_at = lax.axis_index("ctx")
    fsdp_at = lax.axis_index("fsdp")
    high_at, low_at = ctx_at // lows, ctx_at % lows
    tok_count = tokens.shape[0]
    _, columns = embedding.shape
    local_channels = in_weight.shape[2]
    part = local_channels // lows
    own = local_channels // ctx_count

    def move(value, target):
        return send(value, ctx_count, fsdp_count, target)

    by_kind = jnp.swapaxes(in_weight, 0, 1)
    weights = [lax.dynamic_slice_in_dim(by_kind, low_at * part, part, 2)]
    ids = [tokens[None, :]]
    for shift in range(1, lows):
        def neighbour(i, j):
            return (i // lows * lows + (i % lows - shift) % lows, j)

        going = lax.dynamic_slice_in_dim(by_kind, (low_at - shift) % lows * part, part, 2)
        weights.append(move(going, neighbour))
        ids.append(move(tokens[None, :], neighbour))

    chips = fsdp_count // 2
    across = None
    for shift in range(1, chips):
        got = move(
            embedding, lambda i, j: (i, (j + 2 * shift) % fsdp_count) if j == i // lows else None
        )
        across = got if across is None else across + got
    channel_at = low_at * part + high_at * own
    per_group = min(GROUP, own)
    group_count = own // per_group
    decay = lax.dynamic_slice_in_dim(decay_rates.T, channel_at // GROUP, group_count, 0)
    weight = lax.dynamic_slice_in_dim(residue.T, channel_at // GROUP, group_count, 0)
    filters = make_filters(decay, weight)
    taps = lax.dynamic_slice_in_dim(short_taps, channel_at, own, 2)
    taps = taps.reshape(taps.shape[0], 3 * own).T
    skip = lax.dynamic_slice_in_dim(skip_weight, channel_at, own, 0)[:, None]
    (across,) = after((across,), taps, skip, *filters)
    holder = jnp.where(fsdp_at == high_at, embedding, across)
    beside = move(holder, lambda i, j: (i, j ^ 1) if j % 2 == i // lows % 2 else None)
    gain = lax.dynamic_slice_in_dim(norm_gain, high_at * columns, columns, 0)[None, :]

    cycle = cycle_of(fsdp_count, lows)
    spot = {ctx: at for at, ctx in enumerate(cycle)}
    moved = move(
        out_weight,
        lambda i, j: ((reverse_bits(j, fsdp_count) ^ i // lows) * lows + i % lows, i // lows),
    )
    ahead, behind = [moved], [moved]
    rounds = (ctx_count - 1) // 2

    def turn(*others):
        low, high = after((ahead[-1], behind[-1]), *others)
        ahead.append(move(low, lambda i, j: (cycle[(spot[i] + 1) % ctx_count], j)))
        behind.append(move(high, lambda i, j: (cycle[(spot[i] - 1) % ctx_count], j)))

    turn()
    origin = jnp.where(fsdp_at == high_at, 0, jnp.where((fsdp_at - high_at) % 2 == 0, 1, 2))
    partial = make_table(
        jnp.stack([low_at, origin]), embedding, across, beside, gain, weights, ids, fsdp_count
    )
    pieces = [lax.dynamic_index_in_dim(partial, high_at, 0, keepdims=False)]
    for shift in range(1, fsdp_count):
        going = lax.dynamic_index_in_dim(partial, (high_at + shift) % fsdp_count, 0, keepdims=False)
        pieces.append(move(going, lambda i, j: ((i // lows + shift) % fsdp_count * lows + i % lows, j)))

    for _ in range(1, rounds - 1):
        pieces = list(after(pieces, ahead[-1], behind[-1]))
        turn(*pieces)
    ctx_place = jnp.stack([ctx_at, jnp.int32(lows)])
    gated = make_mixer(
        ctx_place, columns * fsdp_count, tok_count, taps, skip, filters, pieces, ctx_count
    )

    pieces = [lax.dynamic_slice_in_dim(gated, ctx_at * tok_count, tok_count, 1)]
    for shift in range(1, ctx_count):
        going = lax.dynamic_slice_in_dim(gated, (ctx_at + shift) % ctx_count * tok_count, tok_count, 1)
        pieces.append(move(going, lambda i, j: ((i + shift) % ctx_count, j)))
    turn(pieces[-1])
    middle = out_weight.shape[0] // 2
    last_ahead = move(ahead[-1][:middle], lambda i, j: (cycle[(spot[i] + 1) % ctx_count], j))
    last_behind = move(behind[-1][middle:], lambda i, j: (cycle[(spot[i] - 1) % ctx_count], j))
    blocks = ahead + behind[1:] + [last_ahead, last_behind]
    steps = list(range(len(ahead))) + [-at for at in range(1, len(behind))] + [len(ahead)] * 2
    from_ctx = [[cycle[(spot[ctx] - step) % ctx_count] for step in steps] for ctx in range(ctx_count)]
    sources = jnp.array(from_ctx, jnp.int32)[ctx_at]
    lows_from = sources % lows
    to_flip = [
        [reverse_bits(high ^ j, fsdp_count) ^ j for high in range(fsdp_count)] for j in range(fsdp_count)
    ]
    flips = jnp.array(to_flip, jnp.int32)[fsdp_at][sources // lows]

    ordered = make_order(ctx_place, pieces)
    sides, order = [ordered], [0]
    reach = fsdp_count // 2
    while reach:
        sides = sides + [move(side, lambda i, j: (i, j ^ reach)) for side in sides]
        order = order + [at ^ reach for at in order]
        reach //= 2
    return make_product(flips, lows_from, tuple(order), sides, blocks, lows)


def solution(mesh):
    placed = (
        P("ctx"),
        P(None, "fsdp"),
        P(),
        P("ctx", None, "fsdp"),
        P(None, None, "fsdp"),
        P(None, "fsdp"),
        P(None, "fsdp"),
        P("fsdp"),
        P("fsdp", "ctx"),
    )
    return jax.shard_map(body, mesh=mesh, in_specs=placed, out_specs=P("ctx", "fsdp"), check_vma=False)
```

profile of v0, /device:TPU:0, one launch (start us, length us, event | category | flops | bytes accessed | tf_op | source)
XLA Modules:
  0.0 146.0 jit_solution(11694686683950439812)
XLA Ops:
  0.0 5.1 %collective-permute-start = (bf16[512,1024]{1,0:T(8,128)(2,1)}, bf16[512,1024]{1,0:T(8,128)(2,1)S(1)}, u32[]{:S(2)}, u32[]{:S(2)}) collective-permute-start(bf16[512,1024]{1,0:T(8,128)(2,1)} %own_ref.1), channel_id=1, source_target_pairs={{0,2},{4,6},{9,11},{13,15},{18,16},{22,20},{27,25},{31,29}} | collective-permute-start | bytes 3145736 | tf_op jit(solution)/shard_map/ppermute | solution.py:28
  8.1 5.1 %filters.1 = (bf16[4,256,256]{2,1,0:T(8,128)(2,1)}, bf16[4,256,32]{2,1,0:T(8,128)(2,1)}, bf16[4,48,256]{2,1,0:T(8,128)(2,1)}, f32[4,1,16]{2,1,0:T(1,128)}) custom-call(f32[4,16]{1,0:T(4,128)} %bitcast.51, f32[4,16]{1,0:T(4,128)} %bitcast.49, f32[4,1,16]{2,1,0:T(1,128)} %bitcast.52, f32[4,1,16]{2,1,0:T(1,128)} %bitcast.50), custom_call_target="tpu_custom_call" | custom-call | tf_op jit(solution)/shard_map/filters/pallas_call | solution.py:68
  13.9 3.7 %collective-permute-done.across_ref = bf16[512,1024]{1,0:T(8,128)(2,1)S(1)} collective-permute-done((bf16[512,1024]{1,0:T(8,128)(2,1)}, bf16[512,1024]{1,0:T(8,128)(2,1)S(1)}, u32[]{:S(2)}, u32[]{:S(2)}) %collective-permute-start) | collective-permute-done | bytes 1048608 | tf_op jit(solution)/shard_map/ppermute | solution.py:28
  17.6 2.7 %broadcast_select_fusion = bf16[512,1024]{1,0:T(8,128)(2,1)} fusion(bf16[512,1024]{1,0:T(8,128)(2,1)} %own_ref.1, bf16[512,1024]{1,0:T(8,128)(2,1)S(1)} %collective-permute-done.across_ref, pred[]{:T(512)S(6)} %eq.23), kind=kLoop, calls=%fused_computation.1 | loop fusion | flops 524288 | bytes 3145729 | tf_op jit(solution)/shard_map/jit(_where)/select_n | solution.py:364
  20.4 2.3 %collective-permute-start.1 = (bf16[512,1024]{1,0:T(8,128)(2,1)}, bf16[512,1024]{1,0:T(8,128)(2,1)}, u32[]{:S(2)}, u32[]{:S(2)}) collective-permute-start(bf16[512,1024]{1,0:T(8,128)(2,1)} %broadcast_select_fusion), channel_id=1, source_target_pairs={{0,1},{2,3},{4,5},{6,7},{9,8},{11,10},{13,12},{15,14},{16,17},{18,... | collective-permute-start | bytes 3145736 | tf_op jit(solution)/shard_map/ppermute | solution.py:28
  23.7 1.5 %collective-permute-start.2 = (bf16[3,512,256]{2,1,0:T(8,128)(2,1)S(1)}, bf16[3,512,256]{2,1,0:T(8,128)(2,1)S(1)}, u32[]{:S(2)}, u32[]{:S(2)}) collective-permute-start(bf16[3,512,256]{2,1,0:T(8,128)(2,1)S(1)} %get-tuple-element.35), channel_id=1, source_target_pairs={{0,4},{1,5},{2,6},{3,7},{4,0},{5,1},{6,2},{7,3},{8,12},{9,13},{10,... | collective-permute-start | bytes 2359304 | tf_op jit(solution)/shard_map/ppermute | solution.py:28
  25.9 11.1 %collective-permute-start.8 = (bf16[512,512]{1,0:T(8,128)(2,1)S(1)}, bf16[512,512]{1,0:T(8,128)(2,1)S(1)}, u32[]{:S(2)}, u32[]{:S(2)}) collective-permute-start(bf16[512,512]{1,0:T(8,128)(2,1)S(1)} %collective-permute-done.7.refs_4_), channel_id=1, source_target_pairs={{0,8},{1,9},{2,10},{3,11},{4,0},{5,1},{6,2},{7,3},{8,16},{9,17},{1... | collective-permute-start | bytes 1572872 | tf_op jit(solution)/shard_map/ppermute | solution.py:28
  38.1 1.3 dynamic_slice.70
  39.3 7.4 %collective-permute-done.3.refs_3_ = s32[1,512]{1,0:T(1,128)S(1)} collective-permute-done((s32[1,512]{1,0:T(1,128)S(1)}, s32[1,512]{1,0:T(1,128)S(1)}, u32[]{:S(2)}, u32[]{:S(2)}) %collective-permute-start.3) | collective-permute-done | bytes 2080 | tf_op jit(solution)/shard_map/ppermute | solution.py:28
  47.7 4.7 %table.1 = bf16[4,208,512]{2,1,0:T(8,128)(2,1)} custom-call(s32[2]{0:T(128)} %pad_add_fusion.1.place_ref, bf16[512,1024]{1,0:T(8,128)(2,1)} %own_ref.1, bf16[512,1024]{1,0:T(8,128)(2,1)} %copy-done.1, bf16[512,1024]{1,0:T(8,128)(2,1)} %collective-permute-done.1.beside_ref, f32[1,1024]{1,0:T(1,128)} %bitcast.53, ...), custom_call_target="tpu_custom_call" | custom-call | tf_op jit(solution)/shard_map/table/pallas_call | solution.py:135
  52.4 2.0 %dynamic-slice_bitcast_fusion.2 = (bf16[208,512]{1,0:T(8,128)(2,1)S(1)}, bf16[208,512]{1,0:T(8,128)(2,1)S(1)}, bf16[208,512]{1,0:T(8,128)(2,1)S(1)}, bf16[208,512]{1,0:T(8,128)(2,1)}) fusion(bf16[4,208,512]{2,1,0:T(8,128)(2,1)} %table.1, s32[]{:T(128)S(6)} %select_n.192, s32[]{:T(128)S(6)} %select_n.190, s32[]{:T(128)S(6)} %select_n.188, s32[]{:T(128)S(6)} %select_n.186), kind=kLoop, calls=%fused_computation.4 | loop fusion | bytes 1703952 | tf_op jit(solution)/shard_map/jit(dynamic_index_in_dim)/squeeze | solution.py:389
  54.4 3.0 %collective-permute-start.6 = (bf16[208,512]{1,0:T(8,128)(2,1)S(1)}, bf16[208,512]{1,0:T(8,128)(2,1)S(1)}, u32[]{:S(2)}, u32[]{:S(2)}) collective-permute-start(bf16[208,512]{1,0:T(8,128)(2,1)S(1)} %get-tuple-element.37), channel_id=1, source_target_pairs={{0,24},{1,25},{2,26},{3,27},{4,28},{5,29},{6,30},{7,31},{8,0},{9,1... | collective-permute-start | bytes 638984 | tf_op jit(solution)/shard_map/ppermute | solution.py:28
  58.0 2.8 %collective-permute-done.6.refs_3_ = bf16[208,512]{1,0:T(8,128)(2,1)S(1)} collective-permute-done((bf16[208,512]{1,0:T(8,128)(2,1)S(1)}, bf16[208,512]{1,0:T(8,128)(2,1)S(1)}, u32[]{:S(2)}, u32[]{:S(2)}) %collective-permute-start.6) | collective-permute-done | bytes 213024 | tf_op jit(solution)/shard_map/ppermute | solution.py:28
  60.8 13.0 %collective-permute-done.5.refs_2_ = bf16[208,512]{1,0:T(8,128)(2,1)S(1)} collective-permute-done((bf16[208,512]{1,0:T(8,128)(2,1)S(1)}, bf16[208,512]{1,0:T(8,128)(2,1)S(1)}, u32[]{:S(2)}, u32[]{:S(2)}) %collective-permute-start.5) | collective-permute-done | bytes 213024 | tf_op jit(solution)/shard_map/ppermute | solution.py:28
  73.8 2.6 %collective-permute-start.20 = (bf16[512,512]{1,0:T(8,128)(2,1)S(1)}, bf16[512,512]{1,0:T(8,128)(2,1)}, u32[]{:S(2)}, u32[]{:S(2)}) collective-permute-start(bf16[512,512]{1,0:T(8,128)(2,1)S(1)} %collective-permute-done.8.refs_5_), channel_id=1, source_target_pairs={{0,8},{1,9},{2,10},{3,11},{4,0},{5,1},{6,2},{7,3},{8,16},{9,17},{1... | collective-permute-start | bytes 1572872 | tf_op jit(solution)/shard_map/ppermute | solution.py:28
  77.7 12.2 %mixer.1 = bf16[64,4096]{1,0:T(8,128)(2,1)} custom-call(s32[2]{0:T(128)} %pad_add_fusion.place_ref, f32[192,7]{1,0:T(8,128)} %bitcast.48, f32[64,1]{1,0:T(8,128)} %copy.23.skip_ref, bf16[4,256,256]{2,1,0:T(8,128)(2,1)} %get-tuple-element.20.near_ref, bf16[4,256,32]{2,1,0:T(8,128)(2,1)} %get-tuple-element.21.into_ref, ...), custom_call_target="tpu_custom_call" | custom-call | tf_op jit(solution)/shard_map/mixer/pallas_call | solution.py:221
  89.9 1.7 %constant_dynamic-slice_fusion = (bf16[64,512]{1,0:T(8,128)(2,1)S(1)}, bf16[64,512]{1,0:T(8,128)(2,1)S(1)}, bf16[64,512]{1,0:T(8,128)(2,1)S(1)}, bf16[64,512]{1,...) fusion(bf16[64,4096]{1,0:T(8,128)(2,1)} %mixer.1, ...), kind=kLoop, calls=%fused_computation.8 | loop fusion | bytes 1048608 | tf_op jit(solution)/shard_map/dynamic_slice | solution.py:402
  91.6 4.3 %collective-permute-start.16 = (bf16[64,512]{1,0:T(8,128)(2,1)S(1)}, bf16[64,512]{1,0:T(8,128)(2,1)S(1)}, u32[]{:S(2)}, u32[]{:S(2)}) collective-permute-start(bf16[64,512]{1,0:T(8,128)(2,1)S(1)} %get-tuple-element.41), channel_id=1, source_target_pairs={{0,28},{1,29},{2,30},{3,31},{4,0},{5,1},{6,2},{7,3},{8,4},{9,5},{1... | collective-permute-start | bytes 196616 | tf_op jit(solution)/shard_map/ppermute | solution.py:28
  95.9 2.0 %collective-permute-start.15 = (bf16[64,512]{1,0:T(8,128)(2,1)S(1)}, bf16[64,512]{1,0:T(8,128)(2,1)S(1)}, u32[]{:S(2)}, u32[]{:S(2)}) collective-permute-start(bf16[64,512]{1,0:T(8,128)(2,1)S(1)} %get-tuple-element.42), channel_id=1, source_target_pairs={{0,24},{1,25},{2,26},{3,27},{4,28},{5,29},{6,30},{7,31},{8,0},{9,1... | collective-permute-start | bytes 196616 | tf_op jit(solution)/shard_map/ppermute | solution.py:28
  98.0 1.9 %collective-permute-start.13 = (bf16[64,512]{1,0:T(8,128)(2,1)S(1)}, bf16[64,512]{1,0:T(8,128)(2,1)S(1)}, u32[]{:S(2)}, u32[]{:S(2)}) collective-permute-start(bf16[64,512]{1,0:T(8,128)(2,1)S(1)} %get-tuple-element.44), channel_id=1, source_target_pairs={{0,16},{1,17},{2,18},{3,19},{4,20},{5,21},{6,22},{7,23},{8,24},{9,... | collective-permute-start | bytes 196616 | tf_op jit(solution)/shard_map/ppermute | solution.py:28
  100.4 3.5 %collective-permute-start.12 = (bf16[64,512]{1,0:T(8,128)(2,1)S(1)}, bf16[64,512]{1,0:T(8,128)(2,1)S(1)}, u32[]{:S(2)}, u32[]{:S(2)}) collective-permute-start(bf16[64,512]{1,0:T(8,128)(2,1)S(1)} %get-tuple-element.45), channel_id=1, source_target_pairs={{0,12},{1,13},{2,14},{3,15},{4,16},{5,17},{6,18},{7,19},{8,20},{9,... | collective-permute-start | bytes 196616 | tf_op jit(solution)/shard_map/ppermute | solution.py:28
  106.0 1.5 collective-permute-start.10
  107.6 2.3 %collective-permute-done.11.refs_2_ = bf16[64,512]{1,0:T(8,128)(2,1)S(1)} collective-permute-done((bf16[64,512]{1,0:T(8,128)(2,1)S(1)}, bf16[64,512]{1,0:T(8,128)(2,1)S(1)}, u32[]{:S(2)}, u32[]{:S(2)}) %collective-permute-start.11) | collective-permute-done | bytes 65568 | tf_op jit(solution)/shard_map/ppermute | solution.py:28
  109.9 3.1 %collective-permute-done.10.refs_1_ = bf16[64,512]{1,0:T(8,128)(2,1)S(1)} collective-permute-done((bf16[64,512]{1,0:T(8,128)(2,1)S(1)}, bf16[64,512]{1,0:T(8,128)(2,1)S(1)}, u32[]{:S(2)}, u32[]{:S(2)}) %collective-permute-start.10) | collective-permute-done | bytes 65568 | tf_op jit(solution)/shard_map/ppermute | solution.py:28
  113.6 2.2 %order.1.refs_0_ = bf16[512,512]{1,0:T(8,128)(2,1)} custom-call(s32[2]{0:T(128)} %pad_add_fusion.place_ref, bf16[64,512]{1,0:T(8,128)(2,1)} %get-tuple-element.48.refs_0_, bf16[64,512]{1,0:T(8,128)(2,1)} %copy-done.23, bf16[64,512]{1,0:T(8,128)(2,1)} %copy-done.22, bf16[64,512]{1,0:T(8,128)(2,1)} %copy-done.21, bf16[64,512]{1,0:T(8,128)(2,1)} %copy-done.20, ...), custom_call_target="tpu_custom_call" | custom-call | tf_op jit(solution)/shard_map/order/pallas_call | solution.py:251
  116.8 2.0 %collective-permute-start.23 = (bf16[512,512]{1,0:T(8,128)(2,1)}, bf16[512,512]{1,0:T(8,128)(2,1)S(1)}, u32[]{:S(2)}, u32[]{:S(2)}) collective-permute-start(bf16[512,512]{1,0:T(8,128)(2,1)} %collective-permute-done.21.refs_9_), channel_id=1, source_target_pairs={{0,4},{1,5},{2,6},{3,7},{4,12},{5,13},{6,14},{7,15},{8,0},{9,1},{1... | collective-permute-start | bytes 1572872 | tf_op jit(solution)/shard_map/ppermute | solution.py:28
  118.8 9.4 %collective-permute-done.17.refs_1_ = bf16[512,512]{1,0:T(8,128)(2,1)S(1)} collective-permute-done((bf16[512,512]{1,0:T(8,128)(2,1)}, bf16[512,512]{1,0:T(8,128)(2,1)S(1)}, u32[]{:S(2)}, u32[]{:S(2)}) %collective-permute-start.17) | collective-permute-done | bytes 524320 | tf_op jit(solution)/shard_map/ppermute | solution.py:28
  129.9 1.9 %collective-permute-start.25 = (bf16[256,512]{1,0:T(8,128)(2,1)}, bf16[256,512]{1,0:T(8,128)(2,1)S(1)}, u32[]{:S(2)}, u32[]{:S(2)}) collective-permute-start(bf16[256,512]{1,0:T(8,128)(2,1)} %slice.11), channel_id=1, source_target_pairs={{0,4},{1,5},{2,6},{3,7},{4,12},{5,13},{6,14},{7,15},{8,0},{9,1},{1... | collective-permute-start | bytes 786440 | tf_op jit(solution)/shard_map/ppermute | solution.py:28
  132.6 1.2 gather_fusion
  133.8 1.2 and_select_fusion.lows_ref
  135.0 2.8 %collective-permute-done.24.refs_11_ = bf16[256,512]{1,0:T(8,128)(2,1)S(1)} collective-permute-done((bf16[256,512]{1,0:T(8,128)(2,1)S(1)}, bf16[256,512]{1,0:T(8,128)(2,1)S(1)}, u32[]{:S(2)}, u32[]{:S(2)}) %collective-permute-start.24) | collective-permute-done | bytes 262176 | tf_op jit(solution)/shard_map/ppermute | solution.py:28
  139.6 6.4 %product.1 = bf16[512,1024]{1,0:T(8,128)(2,1)} custom-call(s32[9]{0:T(128)} %gather_fusion, s32[9]{0:T(128)} %and_select_fusion.lows_ref, bf16[512,512]{1,0:T(8,128)(2,1)} %order.1.refs_0_, bf16[512,512]{1,0:T(8,128)(2,1)} %copy-done.9, bf16[512,512]{1,0:T(8,128)(2,1)} %copy-done.10, bf16[512,512]{1,0:T(8,128)(2,1)} %copy-done.11, ...), custom_call_target="tpu_custom_call" | custom-call | tf_op jit(solution)/shard_map/product/pallas_call | solution.py:282
  (100 shorter events, 18.0 us)
Async XLA Ops:
  0.0 17.6 %collective-permute-start = (bf16[512,1024]{1,0:T(8,128)(2,1)}, bf16[512,1024]{1,0:T(8,128)(2,1)S(1)}, u32[]{:S(2)}, u32[]{:S(2)}) collective-permute-start(bf16[512,1024]{1,0:T(8,128)(2,1)} %own_ref.1), channel_id=1, source_target_pairs={{0,2},{4,6},{9,11},{13,15},{18,16},{22,20},{27,25},{31,29}} | collective-permute-start | bytes 3145736 | tf_op jit(solution)/shard_map/ppermute | solution.py:28
  20.4 26.4 %collective-permute-start.1 = (bf16[512,1024]{1,0:T(8,128)(2,1)}, bf16[512,1024]{1,0:T(8,128)(2,1)}, u32[]{:S(2)}, u32[]{:S(2)}) collective-permute-start(bf16[512,1024]{1,0:T(8,128)(2,1)} %broadcast_select_fusion), channel_id=1, source_target_pairs={{0,1},{2,3},{4,5},{6,7},{9,8},{11,10},{13,12},{15,14},{16,17},{18,... | collective-permute-start | bytes 3145736 | tf_op jit(solution)/shard_map/ppermute | solution.py:28
  22.7 14.3 %copy-start.24 = (s32[512]{0:T(512)S(1)}, s32[512]{0:T(512)}, u32[]{:S(2)}) copy-start(s32[512]{0:T(512)} %param.11) | copy-start | bytes 6148
  23.7 23.1 %collective-permute-start.2 = (bf16[3,512,256]{2,1,0:T(8,128)(2,1)S(1)}, bf16[3,512,256]{2,1,0:T(8,128)(2,1)S(1)}, u32[]{:S(2)}, u32[]{:S(2)}) collective-permute-start(bf16[3,512,256]{2,1,0:T(8,128)(2,1)S(1)} %get-tuple-element.35), channel_id=1, source_target_pairs={{0,4},{1,5},{2,6},{3,7},{4,0},{5,1},{6,2},{7,3},{8,12},{9,13},{10,... | collective-permute-start | bytes 2359304 | tf_op jit(solution)/shard_map/ppermute | solution.py:28
  25.2 0.7 collective-permute-start.7
  25.9 64.0 %copy-start.6 = (bf16[512,512]{1,0:T(8,128)(2,1)}, bf16[512,512]{1,0:T(8,128)(2,1)S(1)}, u32[]{:S(2)}) copy-start(bf16[512,512]{1,0:T(8,128)(2,1)S(1)} %collective-permute-done.7.refs_4_) | copy-start | bytes 1572868
  25.9 32.0 %collective-permute-start.8 = (bf16[512,512]{1,0:T(8,128)(2,1)S(1)}, bf16[512,512]{1,0:T(8,128)(2,1)S(1)}, u32[]{:S(2)}, u32[]{:S(2)}) collective-permute-start(bf16[512,512]{1,0:T(8,128)(2,1)S(1)} %collective-permute-done.7.refs_4_), channel_id=1, source_target_pairs={{0,8},{1,9},{2,10},{3,11},{4,0},{5,1},{6,2},{7,3},{8,16},{9,17},{1... | collective-permute-start | bytes 1572872 | tf_op jit(solution)/shard_map/ppermute | solution.py:28
  37.0 20.9 %collective-permute-start.9 = (bf16[512,512]{1,0:T(8,128)(2,1)S(1)}, bf16[512,512]{1,0:T(8,128)(2,1)S(1)}, u32[]{:S(2)}, u32[]{:S(2)}) collective-permute-start(bf16[512,512]{1,0:T(8,128)(2,1)S(1)} %collective-permute-done.7.refs_4_), channel_id=1, source_target_pairs={{0,4},{1,5},{2,6},{3,7},{4,12},{5,13},{6,14},{7,15},{8,0},{9,1},{1... | collective-permute-start | bytes 1572872 | tf_op jit(solution)/shard_map/ppermute | solution.py:28
  37.0 9.8 %collective-permute-start.3 = (s32[1,512]{1,0:T(1,128)S(1)}, s32[1,512]{1,0:T(1,128)S(1)}, u32[]{:S(2)}, u32[]{:S(2)}) collective-permute-start(s32[1,512]{1,0:T(1,128)S(1)} %bitcast.55), channel_id=1, source_target_pairs={{0,4},{1,5},{2,6},{3,7},{4,0},{5,1},{6,2},{7,3},{8,12},{9,13},{10,... | collective-permute-start | bytes 6152 | tf_op jit(solution)/shard_map/ppermute | solution.py:28
  54.4 6.4 %collective-permute-start.6 = (bf16[208,512]{1,0:T(8,128)(2,1)S(1)}, bf16[208,512]{1,0:T(8,128)(2,1)S(1)}, u32[]{:S(2)}, u32[]{:S(2)}) collective-permute-start(bf16[208,512]{1,0:T(8,128)(2,1)S(1)} %get-tuple-element.37), channel_id=1, source_target_pairs={{0,24},{1,25},{2,26},{3,27},{4,28},{5,29},{6,30},{7,31},{8,0},{9,1... | collective-permute-start | bytes 638984 | tf_op jit(solution)/shard_map/ppermute | solution.py:28
  57.4 16.4 %collective-permute-start.5 = (bf16[208,512]{1,0:T(8,128)(2,1)S(1)}, bf16[208,512]{1,0:T(8,128)(2,1)S(1)}, u32[]{:S(2)}, u32[]{:S(2)}) collective-permute-start(bf16[208,512]{1,0:T(8,128)(2,1)S(1)} %get-tuple-element.38), channel_id=1, source_target_pairs={{0,16},{1,17},{2,18},{3,19},{4,20},{5,21},{6,22},{7,23},{8,24},{9,... | collective-permute-start | bytes 638984 | tf_op jit(solution)/shard_map/ppermute | solution.py:28
  57.4 16.4 %collective-permute-start.4 = (bf16[208,512]{1,0:T(8,128)(2,1)S(1)}, bf16[208,512]{1,0:T(8,128)(2,1)S(1)}, u32[]{:S(2)}, u32[]{:S(2)}) collective-permute-start(bf16[208,512]{1,0:T(8,128)(2,1)S(1)} %get-tuple-element.39), channel_id=1, source_target_pairs={{0,8},{1,9},{2,10},{3,11},{4,12},{5,13},{6,14},{7,15},{8,16},{9,17... | collective-permute-start | bytes 638984 | tf_op jit(solution)/shard_map/ppermute | solution.py:28
  57.9 33.7 %copy-start.7 = (bf16[512,512]{1,0:T(8,128)(2,1)}, bf16[512,512]{1,0:T(8,128)(2,1)S(1)}, u32[]{:S(2)}) copy-start(bf16[512,512]{1,0:T(8,128)(2,1)S(1)} %collective-permute-done.8.refs_5_) | copy-start | bytes 1572868
  57.9 33.7 %copy-start.8 = (bf16[512,512]{1,0:T(8,128)(2,1)}, bf16[512,512]{1,0:T(8,128)(2,1)S(1)}, u32[]{:S(2)}) copy-start(bf16[512,512]{1,0:T(8,128)(2,1)S(1)} %collective-permute-done.9.refs_8_) | copy-start | bytes 1572868
  60.8 16.9 %copy-start.14 = (bf16[208,512]{1,0:T(8,128)(2,1)}, bf16[208,512]{1,0:T(8,128)(2,1)S(1)}, u32[]{:S(2)}) copy-start(bf16[208,512]{1,0:T(8,128)(2,1)S(1)} %collective-permute-done.6.refs_3_) | copy-start | bytes 638980
  73.8 43.1 %collective-permute-start.20 = (bf16[512,512]{1,0:T(8,128)(2,1)S(1)}, bf16[512,512]{1,0:T(8,128)(2,1)}, u32[]{:S(2)}, u32[]{:S(2)}) collective-permute-start(bf16[512,512]{1,0:T(8,128)(2,1)S(1)} %collective-permute-done.8.refs_5_), channel_id=1, source_target_pairs={{0,8},{1,9},{2,10},{3,11},{4,0},{5,1},{6,2},{7,3},{8,16},{9,17},{1... | collective-permute-start | bytes 1572872 | tf_op jit(solution)/shard_map/ppermute | solution.py:28
  76.3 40.5 %collective-permute-start.21 = (bf16[512,512]{1,0:T(8,128)(2,1)S(1)}, bf16[512,512]{1,0:T(8,128)(2,1)}, u32[]{:S(2)}, u32[]{:S(2)}) collective-permute-start(bf16[512,512]{1,0:T(8,128)(2,1)S(1)} %collective-permute-done.9.refs_8_), channel_id=1, source_target_pairs={{0,4},{1,5},{2,6},{3,7},{4,12},{5,13},{6,14},{7,15},{8,0},{9,1},{1... | collective-permute-start | bytes 1572872 | tf_op jit(solution)/shard_map/ppermute | solution.py:28
  91.6 6.4 %collective-permute-start.16 = (bf16[64,512]{1,0:T(8,128)(2,1)S(1)}, bf16[64,512]{1,0:T(8,128)(2,1)S(1)}, u32[]{:S(2)}, u32[]{:S(2)}) collective-permute-start(bf16[64,512]{1,0:T(8,128)(2,1)S(1)} %get-tuple-element.41), channel_id=1, source_target_pairs={{0,28},{1,29},{2,30},{3,31},{4,0},{5,1},{6,2},{7,3},{8,4},{9,5},{1... | collective-permute-start | bytes 196616 | tf_op jit(solution)/shard_map/ppermute | solution.py:28
  95.9 4.5 %collective-permute-start.15 = (bf16[64,512]{1,0:T(8,128)(2,1)S(1)}, bf16[64,512]{1,0:T(8,128)(2,1)S(1)}, u32[]{:S(2)}, u32[]{:S(2)}) collective-permute-start(bf16[64,512]{1,0:T(8,128)(2,1)S(1)} %get-tuple-element.42), channel_id=1, source_target_pairs={{0,24},{1,25},{2,26},{3,27},{4,28},{5,29},{6,30},{7,31},{8,0},{9,1... | collective-permute-start | bytes 196616 | tf_op jit(solution)/shard_map/ppermute | solution.py:28
  97.9 5.9 %collective-permute-start.14 = (bf16[64,512]{1,0:T(8,128)(2,1)S(1)}, bf16[64,512]{1,0:T(8,128)(2,1)S(1)}, u32[]{:S(2)}, u32[]{:S(2)}) collective-permute-start(bf16[64,512]{1,0:T(8,128)(2,1)S(1)} %get-tuple-element.43), channel_id=1, source_target_pairs={{0,20},{1,21},{2,22},{3,23},{4,24},{5,25},{6,26},{7,27},{8,28},{9,... | collective-permute-start | bytes 196616 | tf_op jit(solution)/shard_map/ppermute | solution.py:28
  98.0 15.0 %copy-start.17 = (bf16[64,512]{1,0:T(8,128)(2,1)}, bf16[64,512]{1,0:T(8,128)(2,1)S(1)}, u32[]{:S(2)}) copy-start(bf16[64,512]{1,0:T(8,128)(2,1)S(1)} %collective-permute-done.16.refs_7_) | copy-start | bytes 196612
  98.0 8.0 %collective-permute-start.13 = (bf16[64,512]{1,0:T(8,128)(2,1)S(1)}, bf16[64,512]{1,0:T(8,128)(2,1)S(1)}, u32[]{:S(2)}, u32[]{:S(2)}) collective-permute-start(bf16[64,512]{1,0:T(8,128)(2,1)S(1)} %get-tuple-element.44), channel_id=1, source_target_pairs={{0,16},{1,17},{2,18},{3,19},{4,20},{5,21},{6,22},{7,23},{8,24},{9,... | collective-permute-start | bytes 196616 | tf_op jit(solution)/shard_map/ppermute | solution.py:28
  100.4 7.3 %collective-permute-start.12 = (bf16[64,512]{1,0:T(8,128)(2,1)S(1)}, bf16[64,512]{1,0:T(8,128)(2,1)S(1)}, u32[]{:S(2)}, u32[]{:S(2)}) collective-permute-start(bf16[64,512]{1,0:T(8,128)(2,1)S(1)} %get-tuple-element.45), channel_id=1, source_target_pairs={{0,12},{1,13},{2,14},{3,15},{4,16},{5,17},{6,18},{7,19},{8,20},{9,... | collective-permute-start | bytes 196616 | tf_op jit(solution)/shard_map/ppermute | solution.py:28
  103.9 6.1 %collective-permute-start.11 = (bf16[64,512]{1,0:T(8,128)(2,1)S(1)}, bf16[64,512]{1,0:T(8,128)(2,1)S(1)}, u32[]{:S(2)}, u32[]{:S(2)}) collective-permute-start(bf16[64,512]{1,0:T(8,128)(2,1)S(1)} %get-tuple-element.46), channel_id=1, source_target_pairs={{0,8},{1,9},{2,10},{3,11},{4,12},{5,13},{6,14},{7,15},{8,16},{9,17... | collective-permute-start | bytes 196616 | tf_op jit(solution)/shard_map/ppermute | solution.py:28
  106.0 7.0 %collective-permute-start.10 = (bf16[64,512]{1,0:T(8,128)(2,1)S(1)}, bf16[64,512]{1,0:T(8,128)(2,1)S(1)}, u32[]{:S(2)}, u32[]{:S(2)}) collective-permute-start(bf16[64,512]{1,0:T(8,128)(2,1)S(1)} %get-tuple-element.47), channel_id=1, source_target_pairs={{0,4},{1,5},{2,6},{3,7},{4,8},{5,9},{6,10},{7,11},{8,12},{9,13},{1... | collective-permute-start | bytes 196616 | tf_op jit(solution)/shard_map/ppermute | solution.py:28
  115.8 12.5 %collective-permute-start.17 = (bf16[512,512]{1,0:T(8,128)(2,1)}, bf16[512,512]{1,0:T(8,128)(2,1)S(1)}, u32[]{:S(2)}, u32[]{:S(2)}) collective-permute-start(bf16[512,512]{1,0:T(8,128)(2,1)} %order.1.refs_0_), channel_id=1, source_target_pairs={{0,2},{1,3},{2,0},{3,1},{4,6},{5,7},{6,4},{7,5},{8,10},{9,11},{10,... | collective-permute-start | bytes 1572872 | tf_op jit(solution)/shard_map/ppermute | solution.py:28
  116.8 12.2 %collective-permute-start.22 = (bf16[512,512]{1,0:T(8,128)(2,1)}, bf16[512,512]{1,0:T(8,128)(2,1)S(1)}, u32[]{:S(2)}, u32[]{:S(2)}) collective-permute-start(bf16[512,512]{1,0:T(8,128)(2,1)} %collective-permute-done.20.refs_6_), channel_id=1, source_target_pairs={{0,8},{1,9},{2,10},{3,11},{4,0},{5,1},{6,2},{7,3},{8,16},{9,17},{1... | collective-permute-start | bytes 1572872 | tf_op jit(solution)/shard_map/ppermute | solution.py:28
  116.8 12.3 %collective-permute-start.23 = (bf16[512,512]{1,0:T(8,128)(2,1)}, bf16[512,512]{1,0:T(8,128)(2,1)S(1)}, u32[]{:S(2)}, u32[]{:S(2)}) collective-permute-start(bf16[512,512]{1,0:T(8,128)(2,1)} %collective-permute-done.21.refs_9_), channel_id=1, source_target_pairs={{0,4},{1,5},{2,6},{3,7},{4,12},{5,13},{6,14},{7,15},{8,0},{9,1},{1... | collective-permute-start | bytes 1572872 | tf_op jit(solution)/shard_map/ppermute | solution.py:28
  118.8 16.1 %collective-permute-start.18 = (bf16[512,512]{1,0:T(8,128)(2,1)}, bf16[512,512]{1,0:T(8,128)(2,1)S(1)}, u32[]{:S(2)}, u32[]{:S(2)}) collective-permute-start(bf16[512,512]{1,0:T(8,128)(2,1)} %order.1.refs_0_), channel_id=1, source_target_pairs={{0,1},{1,0},{2,3},{3,2},{4,5},{5,4},{6,7},{7,6},{8,9},{9,8},{10,11... | collective-permute-start | bytes 1572872 | tf_op jit(solution)/shard_map/ppermute | solution.py:28
  128.3 6.7 %collective-permute-start.19 = (bf16[512,512]{1,0:T(8,128)(2,1)S(1)}, bf16[512,512]{1,0:T(8,128)(2,1)S(1)}, u32[]{:S(2)}, u32[]{:S(2)}) collective-permute-start(bf16[512,512]{1,0:T(8,128)(2,1)S(1)} %collective-permute-done.17.refs_1_), channel_id=1, source_target_pairs={{0,1},{1,0},{2,3},{3,2},{4,5},{5,4},{6,7},{7,6},{8,9},{9,8},{10,11... | collective-permute-start | bytes 1572872 | tf_op jit(solution)/shard_map/ppermute | solution.py:28
  129.0 8.8 %collective-permute-start.24 = (bf16[256,512]{1,0:T(8,128)(2,1)S(1)}, bf16[256,512]{1,0:T(8,128)(2,1)S(1)}, u32[]{:S(2)}, u32[]{:S(2)}) collective-permute-start(bf16[256,512]{1,0:T(8,128)(2,1)S(1)} %slice.10), channel_id=1, source_target_pairs={{0,8},{1,9},{2,10},{3,11},{4,0},{5,1},{6,2},{7,3},{8,16},{9,17},{1... | collective-permute-start | bytes 786440 | tf_op jit(solution)/shard_map/ppermute | solution.py:28
  129.9 8.9 %collective-permute-start.25 = (bf16[256,512]{1,0:T(8,128)(2,1)}, bf16[256,512]{1,0:T(8,128)(2,1)S(1)}, u32[]{:S(2)}, u32[]{:S(2)}) collective-permute-start(bf16[256,512]{1,0:T(8,128)(2,1)} %slice.11), channel_id=1, source_target_pairs={{0,4},{1,5},{2,6},{3,7},{4,12},{5,13},{6,14},{7,15},{8,0},{9,1},{1... | collective-permute-start | bytes 786440 | tf_op jit(solution)/shard_map/ppermute | solution.py:28
  (21 other events, 104.7 us)
where the time goes:
time: 147 us; the launch traced here: 146 us
  waiting for transfers between devices  47.5 us (32%)
  starting transfers between devices  46.4 us (32%)
  Pallas kernels  30.5 us (21%)
  local copies, waits for them, and re-layouts  15.4 us (10%)
  other arithmetic  5.88 us (4%)
    ppermute x26, waiting for transfers between devices, send(): return lax.ppermute(value, AXES, pairs)  47.5 us
    ppermute x26, starting transfers between devices, send(): return lax.ppermute(value, AXES, pairs)  46.4 us
    pallas_call x1, Pallas kernels, make_mixer(): pl.pallas_call(functools.partial(mixer_body, width), in_specs=[pl.BlockSp...  12.2 us
    pallas_call x1, Pallas kernels, make_product(): pl.pallas_call(functools.partial(product_body, order), in_specs=[smem, sm...  6.35 us
    pallas_call x1, Pallas kernels, make_filters(): pl.pallas_call(filter_body, in_specs=[smem, smem, vmem, vmem], out_specs=...  5.07 us
    pallas_call x1, Pallas kernels, make_table(): pl.pallas_call(table_body, in_specs=[pl.BlockSpec(memory_space=pltpu.SMEM...  4.7 us
    unnamed x56, local copies, waits for them, and re-layouts  3.56 us
  transfers between devices with their start and end apart: 26, of which 13 were waited for; matrix products, arithmetic and copies ran while one was open for 11% of the time, Pallas kernels for 17%

commit v1 on v0

--- a/solution.py
+++ b/solution.py
@@ -12,6 +12,7 @@
 CHUNK = 256
 TILE = 512
 EXTRA = 16
+PLACES = 4
 BASE = 16
 AXES = ("ctx", "fsdp")
 BF16 = jnp.bfloat16
@@ -37,7 +38,13 @@
     return high, (value - high.astype(F32)).astype(BF16)
 
 
-def filter_body(decay_ref, residue_ref, decay_col_ref, residue_col_ref, near_ref, into_ref, outof_ref, step_ref):
+def filter_body(
+    decay_ref, residue_ref, decay_col_ref, residue_col_ref, taps_ref, skip_ref,
+    near_ref, into_ref, outof_ref, step_ref, side_ref,
+):
+    count = taps_ref.shape[1]
+    side_ref[:, :count] = taps_ref[...]
+    side_ref[:skip_ref.shape[0], count:count + 1] = skip_ref[...]
     groups, modes = decay_ref.shape
     rows = lax.broadcasted_iota(jnp.int32, (CHUNK, CHUNK), 0)
     cols = lax.broadcasted_iota(jnp.int32, (CHUNK, CHUNK), 1)
@@ -61,32 +68,32 @@
         step_ref[group] = jnp.exp(-rate_row * CHUNK)
 
 
-def make_filters(decay, residue):
+def make_filters(decay, residue, taps, skip):
     groups, modes = decay.shape
     smem = pl.BlockSpec(memory_space=pltpu.SMEM)
     vmem = pl.BlockSpec(memory_space=pltpu.VMEM)
     return pl.pallas_call(
         filter_body,
-        in_specs=[smem, smem, vmem, vmem],
-        out_specs=[vmem] * 4,
+        in_specs=[smem, smem] + [vmem] * 4,
+        out_specs=[vmem] * 5,
         out_shape=[
             jax.ShapeDtypeStruct((groups, CHUNK, CHUNK), BF16),
             jax.ShapeDtypeStruct((groups, CHUNK, 2 * modes), BF16),
             jax.ShapeDtypeStruct((groups, 3 * modes, CHUNK), BF16),
             jax.ShapeDtypeStruct((groups, 1, modes), F32),
+            jax.ShapeDtypeStruct((taps.shape[0], 128), F32),
         ],
         name="filters",
-    )(decay, residue, decay[:, None, :], residue[:, None, :])
-
-
-def table_body(place_ref, own_ref, across_ref, beside_ref, gain_ref, *refs):
-    out_ref, raw_ref, scaled_ref, extra_ref = refs[-4:]
-    count = (len(refs) - 4) // 2
-    weight_refs, token_refs = refs[:count], refs[count:2 * count]
+    )(decay, residue, decay[:, None, :], residue[:, None, :], taps, skip)
+
+
+def table_body(count, place_ref, own_ref, across_ref, beside_ref, gain_ref, *refs):
+    raw_ref, scaled_ref, extra_ref, flip_ref = refs[-4:]
+    weight_refs, token_refs, out_refs = refs[:count], refs[count:2 * count], refs[2 * count:-4]
     vocab, columns = own_ref.shape
     width = columns // count
-    pieces, rows, _ = out_ref.shape
-    low_at, origin = place_ref[0], place_ref[1]
+    pieces, rows = len(out_refs), out_refs[0].shape[0]
+    low_at, origin, high_at = place_ref[0], place_ref[1], place_ref[3]
 
     @pl.when(origin == 0)
     def _():
@@ -115,17 +122,18 @@
         extra_ref[pl.ds(3 + count + low, 1), :] = (token_ref[...] % BASE).astype(F32)
     extra = extra_ref[...].astype(BF16)
     each = (rows - EXTRA) // 3
-    for piece in range(pieces):
-        out_ref[piece, :EXTRA, :] = extra
+    for out_ref in out_refs:
+        out_ref[:EXTRA, :] = extra
     for kind in range(3):
         total = None
         for shift, weight_ref in enumerate(weight_refs):
             start = pl.multiple_of(lax.rem(low_at + shift, count) * width, width)
             part = jnp.dot(scaled_ref[:, pl.ds(start, width)], weight_ref[kind], preferred_element_type=F32)
             total = part if total is None else total + part
-        flipped = jnp.swapaxes(total, 0, 1).astype(BF16)
-        for piece in range(pieces):
-            out_ref[piece, EXTRA + kind * each:EXTRA + (kind + 1) * each, :] = flipped[piece * each:(piece + 1) * each]
+        flip_ref[...] = jnp.swapaxes(total, 0, 1)
+        for shift, out_ref in enumerate(out_refs):
+            start = pl.multiple_of(lax.rem(high_at + shift, pieces) * each, each)
+            out_ref[EXTRA + kind * each:EXTRA + (kind + 1) * each, :] = flip_ref[pl.ds(start, each), :].astype(BF16)
 
 
 def make_table(place, own, across, beside, gain, weights, tokens, pieces):
@@ -133,22 +141,25 @@
     channels = weights[0].shape[2]
     vmem = pl.BlockSpec(memory_space=pltpu.VMEM)
     return pl.pallas_call(
-        table_body,
+        functools.partial(table_body, len(weights)),
         in_specs=[pl.BlockSpec(memory_space=pltpu.SMEM)] + [vmem] * (4 + len(weights) + len(tokens)),
-        out_specs=vmem,
-        out_shape=jax.ShapeDtypeStruct((pieces, EXTRA + 3 * channels // pieces, vocab), BF16),
+        out_specs=[vmem] * pieces,
+        out_shape=[jax.ShapeDtypeStruct((EXTRA + 3 * channels // pieces, vocab), BF16)] * pieces,
         scratch_shapes=[
             pltpu.VMEM(own.shape, F32),
             pltpu.VMEM(own.shape, BF16),
             pltpu.VMEM((EXTRA, vocab), F32),
+            pltpu.VMEM((channels, vocab), F32),
         ],
         name="table",
     )(place, own, across, beside, gain, *weights, *tokens)
 
 
-def mixer_body(width, place_ref, taps_ref, skip_ref, near_ref, into_ref, outof_ref, step_ref, *refs):
-    piece_refs = refs[:-5]
-    out_ref, query_ref, drive_ref, conv_ref, token_ref = refs[-5:]
+def mixer_body(width, taps, place_ref, near_ref, into_ref, outof_ref, step_ref, taps_ref, *refs):
+    query_ref, drive_ref, conv_ref, token_ref, stage_ref = refs[-5:]
+    ctx_at = place_ref[2]
+    out_refs = refs[-5 - token_ref.shape[0]:-5]
+    piece_refs = refs[:-5 - token_ref.shape[0]]
     rows, vocab = piece_refs[0].shape
     rows -= EXTRA
     channels = rows // 3
@@ -156,14 +167,13 @@
     length = blocks * block
     count = len(piece_refs)
     lows = blocks // count
-    taps = taps_ref.shape[1]
     total = None
     squares = None
     for shift, ref in enumerate(piece_refs):
         head = ref[:EXTRA, :].astype(F32)
         summed = head[0:1] + head[1:2] + head[2:3]
         squares = summed if squares is None else squares + summed
-        high = lax.rem(place_ref[0] // lows - shift + count, count)
+        high = lax.rem(ctx_at // lows - shift + count, count)
         for low in range(lows):
             ids = head[3 + low:4 + low] * BASE + head[3 + lows + low:4 + lows + low]
             token_ref[high * lows + low] = ids[:, :block].astype(jnp.int32)
@@ -208,48 +218,53 @@
         )
         for n in range(chunks):
             here = slice(n * CHUNK, (n + 1) * CHUNK)
-            response = conv_ref[n * per:(n + 1) * per, :] + skip_ref[base:base + per, :] * drive_ref[base:base + per, here]
-            out_ref[base:base + per, here] = (query_ref[base:base + per, here] * response).astype(BF16)
-
-
-def make_mixer(place, width, block, taps, skip, filters, pieces, blocks):
+            response = conv_ref[n * per:(n + 1) * per, :] + taps_ref[base:base + per, taps:taps + 1] * drive_ref[base:base + per, here]
+            at = n * CHUNK
+            stage_ref[at // block, base:base + per, at % block:at % block + CHUNK] = (
+                query_ref[base:base + per, here] * response
+            ).astype(BF16)
+    for shift, out_ref in enumerate(out_refs):
+        out_ref[...] = stage_ref[lax.rem(ctx_at + shift, blocks)]
+
+
+def make_mixer(place, width, taps, block, filters, pieces, blocks):
     rows = pieces[0].shape[0] - EXTRA
     channels = rows // 3
     length = block * blocks
     groups = filters[0].shape[0]
     vmem = pl.BlockSpec(memory_space=pltpu.VMEM)
     return pl.pallas_call(
-        functools.partial(mixer_body, width),
-        in_specs=[pl.BlockSpec(memory_space=pltpu.SMEM)] + [vmem] * (6 + len(pieces)),
-        out_specs=vmem,
-        out_shape=jax.ShapeDtypeStruct((channels, length), BF16),
+        functools.partial(mixer_body, width, taps),
+        in_specs=[pl.BlockSpec(memory_space=pltpu.SMEM)] + [vmem] * (5 + len(pieces)),
+        out_specs=[vmem] * blocks,
+        out_shape=[jax.ShapeDtypeStruct((channels, block), BF16)] * blocks,
         scratch_shapes=[
             pltpu.VMEM((channels, length), F32),
             pltpu.VMEM((channels, length), F32),
             pltpu.VMEM((length // CHUNK * (channels // groups), CHUNK), F32),
             pltpu.VMEM((blocks, 1, block), jnp.int32),
+            pltpu.VMEM((blocks, channels, block), BF16),
         ],
         name="mixer",
-    )(place, taps, skip, *filters, *pieces)
-
-
-def order_body(place_ref, *refs):
+    )(place, *filters, *pieces)
+
+
+def order_body(lows, place_ref, *refs):
     piece_refs, out_ref, stage_ref = refs[:-2], refs[-2], refs[-1]
     count = len(piece_refs)
     rows = piece_refs[0].shape[0]
-    lows = place_ref[1]
     for shift, ref in enumerate(piece_refs):
-        source = lax.rem(place_ref[0] - shift + count, count)
+        source = lax.rem(place_ref[2] - shift + count, count)
         start = pl.multiple_of((lax.rem(source, lows) * (count // lows) + source // lows) * rows, rows)
         stage_ref[pl.ds(start, rows), :] = ref[...].astype(F32)
     out_ref[...] = jnp.swapaxes(stage_ref[...], 0, 1).astype(BF16)
 
 
-def make_order(place, pieces):
+def make_order(place, pieces, lows):
     rows, length = pieces[0].shape
     vmem = pl.BlockSpec(memory_space=pltpu.VMEM)
     return pl.pallas_call(
-        order_body,
+        functools.partial(order_body, lows),
         in_specs=[pl.BlockSpec(memory_space=pltpu.SMEM)] + [vmem] * len(pieces),
         out_specs=vmem,
         out_shape=jax.ShapeDtypeStruct((length, rows * len(pieces)), BF16),
@@ -258,7 +273,7 @@
     )(place, *pieces)
 
 
-def product_body(order, flips_ref, lows_ref, *refs):
+def product_body(order, place_ref, *refs):
     side_refs = refs[:len(order)]
     block_refs = refs[len(order):-3]
     out_ref, sides_ref, sum_ref = refs[-3:]
@@ -268,20 +283,20 @@
     sum_ref[...] = jnp.zeros_like(sum_ref)
     for at, ref in enumerate(block_refs):
         first = full // 2 if at == len(block_refs) - 1 else 0
-        side = sides_ref[flips_ref[at], :, first:first + ref.shape[0]]
-        sum_ref[lows_ref[at]] += jnp.dot(side, ref[...], preferred_element_type=F32)
+        side = sides_ref[place_ref[PLACES + at], :, first:first + ref.shape[0]]
+        sum_ref[place_ref[PLACES + len(block_refs) + at]] += jnp.dot(side, ref[...], preferred_element_type=F32)
     for low in range(sum_ref.shape[0]):
         out_ref[:, low * cols:(low + 1) * cols] = sum_ref[low].astype(BF16)
 
 
-def make_product(flips, lows_at, order, sides, blocks, lows):
+def make_product(place, order, sides, blocks, lows):
     length, full = sides[0].shape
     cols = blocks[0].shape[1]
     smem = pl.BlockSpec(memory_space=pltpu.SMEM)
     vmem = pl.BlockSpec(memory_space=pltpu.VMEM)
     return pl.pallas_call(
         functools.partial(product_body, order),
-        in_specs=[smem, smem] + [vmem] * (len(sides) + len(blocks)),
+        in_specs=[smem] + [vmem] * (len(sides) + len(blocks)),
         out_specs=vmem,
         out_shape=jax.ShapeDtypeStruct((length, lows * cols), BF16),
         scratch_shapes=[
@@ -289,7 +304,7 @@
             pltpu.VMEM((lows, length, cols), F32),
         ],
         name="product",
-    )(flips, lows_at, *sides, *blocks)
+    )(place, *sides, *blocks)
 
 
 def reverse_bits(value, count):
@@ -351,20 +366,6 @@
             embedding, lambda i, j: (i, (j + 2 * shift) % fsdp_count) if j == i // lows else None
         )
         across = got if across is None else across + got
-    channel_at = low_at * part + high_at * own
-    per_group = min(GROUP, own)
-    group_count = own // per_group
-    decay = lax.dynamic_slice_in_dim(decay_rates.T, channel_at // GROUP, group_count, 0)
-    weight = lax.dynamic_slice_in_dim(residue.T, channel_at // GROUP, group_count, 0)
-    filters = make_filters(decay, weight)
-    taps = lax.dynamic_slice_in_dim(short_taps, channel_at, own, 2)
-    taps = taps.reshape(taps.shape[0], 3 * own).T
-    skip = lax.dynamic_slice_in_dim(skip_weight, channel_at, own, 0)[:, None]
-    (across,) = after((across,), taps, skip, *filters)
-    holder = jnp.where(fsdp_at == high_at, embedding, across)
-    beside = move(holder, lambda i, j: (i, j ^ 1) if j % 2 == i // lows % 2 else None)
-    gain = lax.dynamic_slice_in_dim(norm_gain, high_at * columns, columns, 0)[None, :]
-
     cycle = cycle_of(fsdp_count, lows)
     spot = {ctx: at for at, ctx in enumerate(cycle)}
     moved = move(
@@ -373,6 +374,29 @@
     )
     ahead, behind = [moved], [moved]
     rounds = (ctx_count - 1) // 2
+    steps = [*range(rounds + 1), *range(-1, -rounds - 1, -1), rounds + 1, rounds + 1]
+    known = []
+    for i in range(ctx_count):
+        met = [cycle[(spot[i] - step) % ctx_count] for step in steps]
+        for j in range(fsdp_count):
+            origin = 0 if j == i // lows else 1 if (j - i // lows) % 2 == 0 else 2
+            flips = [reverse_bits(ctx // lows ^ j, fsdp_count) ^ j for ctx in met]
+            known.append([i % lows, origin, i, i // lows, *flips, *(ctx % lows for ctx in met)])
+    place = jnp.array(known, jnp.int32)[ctx_at * fsdp_count + fsdp_at]
+
+    channel_at = low_at * part + high_at * own
+    per_group = min(GROUP, own)
+    group_count = own // per_group
+    decay = lax.dynamic_slice_in_dim(decay_rates.T, channel_at // GROUP, group_count, 0)
+    weight = lax.dynamic_slice_in_dim(residue.T, channel_at // GROUP, group_count, 0)
+    taps = lax.dynamic_slice_in_dim(short_taps, channel_at, own, 2)
+    taps = taps.reshape(taps.shape[0], 3 * own).T
+    skip = lax.dynamic_slice_in_dim(skip_weight, channel_at, own, 0)[:, None]
+    gain = lax.dynamic_slice_in_dim(norm_gain, high_at * columns, columns, 0)[None, :]
+    filters = make_filters(decay, weight, taps, skip)
+    (across,) = after((across,), gain, place, *filters)
+    holder = jnp.where(fsdp_at == high_at, embedding, across)
+    beside = move(holder, lambda i, j: (i, j ^ 1) if j % 2 == i // lows % 2 else None)
 
     def turn(*others):
         low, high = after((ahead[-1], behind[-1]), *others)
@@ -380,49 +404,41 @@
         behind.append(move(high, lambda i, j: (cycle[(spot[i] - 1) % ctx_count], j)))
 
     turn()
-    origin = jnp.where(fsdp_at == high_at, 0, jnp.where((fsdp_at - high_at) % 2 == 0, 1, 2))
-    partial = make_table(
-        jnp.stack([low_at, origin]), embedding, across, beside, gain, weights, ids, fsdp_count
-    )
-    pieces = [lax.dynamic_index_in_dim(partial, high_at, 0, keepdims=False)]
+    outgoing = make_table(place, embedding, across, beside, gain, weights, ids, fsdp_count)
+    pieces = [outgoing[0]]
     for shift in range(1, fsdp_count):
-        going = lax.dynamic_index_in_dim(partial, (high_at + shift) % fsdp_count, 0, keepdims=False)
-        pieces.append(move(going, lambda i, j: ((i // lows + shift) % fsdp_count * lows + i % lows, j)))
+        pieces.append(
+            move(outgoing[shift], lambda i, j: ((i // lows + shift) % fsdp_count * lows + i % lows, j))
+        )
 
     for _ in range(1, rounds - 1):
         pieces = list(after(pieces, ahead[-1], behind[-1]))
         turn(*pieces)
-    ctx_place = jnp.stack([ctx_at, jnp.int32(lows)])
     gated = make_mixer(
-        ctx_place, columns * fsdp_count, tok_count, taps, skip, filters, pieces, ctx_count
+        place, columns * fsdp_count, short_taps.shape[0], tok_count, filters, pieces, ctx_count
     )
 
-    pieces = [lax.dynamic_slice_in_dim(gated, ctx_at * tok_count, tok_count, 1)]
+    pieces = [gated[0]]
     for shift in range(1, ctx_count):
-        going = lax.dynamic_slice_in_dim(gated, (ctx_at + shift) % ctx_count * tok_count, tok_count, 1)
-        pieces.append(move(going, lambda i, j: ((i + shift) % ctx_count, j)))
-    turn(pieces[-1])
+        pieces.append(move(gated[shift], lambda i, j: ((i + shift) % ctx_count, j)))
+    pieces = list(after(pieces, ahead[-1], behind[-1]))
+    turn(gated[0])
+    ordered = make_order(place, pieces, lows)
     middle = out_weight.shape[0] // 2
-    last_ahead = move(ahead[-1][:middle], lambda i, j: (cycle[(spot[i] + 1) % ctx_count], j))
-    last_behind = move(behind[-1][middle:], lambda i, j: (cycle[(spot[i] - 1) % ctx_count], j))
+    low, high = after((ahead[-1], behind[-1]), ordered)
+    last_ahead = move(low[:middle], lambda i, j: (cycle[(spot[i] + 1) % ctx_count], j))
+    last_behind = move(high[middle:], lambda i, j: (cycle[(spot[i] - 1) % ctx_count], j))
     blocks = ahead + behind[1:] + [last_ahead, last_behind]
-    steps = list(range(len(ahead))) + [-at for at in range(1, len(behind))] + [len(ahead)] * 2
-    from_ctx = [[cycle[(spot[ctx] - step) % ctx_count] for step in steps] for ctx in range(ctx_count)]
-    sources = jnp.array(from_ctx, jnp.int32)[ctx_at]
-    lows_from = sources % lows
-    to_flip = [
-        [reverse_bits(high ^ j, fsdp_count) ^ j for high in range(fsdp_count)] for j in range(fsdp_count)
-    ]
-    flips = jnp.array(to_flip, jnp.int32)[fsdp_at][sources // lows]
-
-    ordered = make_order(ctx_place, pieces)
     sides, order = [ordered], [0]
     reach = fsdp_count // 2
     while reach:
-        sides = sides + [move(side, lambda i, j: (i, j ^ reach)) for side in sides]
+        more = []
+        for side in sides:
+            more.append(move(side, lambda i, j: (i, j ^ reach)))
+        sides = sides + more
         order = order + [at ^ reach for at in order]
         reach //= 2
-    return make_product(flips, lows_from, tuple(order), sides, blocks, lows)
+    return make_product(place, tuple(order), sides, blocks, lows)
 
 
 def solution(mesh):

time: 147 us -> 148 us (level)
  waiting for transfers between devices: 47.5 us -> 56.5 us
  local copies, waits for them, and re-layouts: 15.4 us -> 10.2 us
  other arithmetic: 5.88 us -> 2.74 us
    ppermute x26, waiting for transfers between devices: 47.5 us -> 56.5 us  [send(): return lax.ppermute(value, AXES, pairs)]
    select_n x2 -> x0, other arithmetic: 1.92 us -> none  [the longest x1 1.22 us: body(): lows_from = sources % lows]
    dynamic_slice x1 -> x0, local copies, waits for them, and re-layouts: 1.72 us -> none  [body(): lax.dynamic_slice_in_dim(gated, (ctx_at + shift) % ctx_count * tok_count,...]
  transfers between devices with their start and end apart: 26 -> 26, of which waited for: 13 -> 14; matrix products, arithmetic and copies ran while one was open for 11% -> 5% of each run, Pallas kernels for 17% -> 15%
where the time goes in v1:
time: 148 us
  waiting for transfers between devices  56.5 us (38%)
  starting transfers between devices  47 us (32%)
  Pallas kernels  31 us (21%)
  local copies, waits for them, and re-layouts  10.2 us (7%)
  other arithmetic  2.74 us (2%)
    ppermute x26, waiting for transfers between devices, send(): return lax.ppermute(value, AXES, pairs)  56.5 us
    ppermute x26, starting transfers between devices, send(): return lax.ppermute(value, AXES, pairs)  47 us
    pallas_call x1, Pallas kernels, make_mixer(): pl.pallas_call(functools.partial(mixer_body, width, taps), in_specs=[pl.B...  12.2 us
    pallas_call x1, Pallas kernels, make_product(): pl.pallas_call(functools.partial(product_body, order), in_specs=[smem] +...  6.35 us
    pallas_call x1, Pallas kernels, make_filters(): pl.pallas_call(filter_body, in_specs=[smem, smem] + [vmem] * 4, out_specs...  5.25 us
    pallas_call x1, Pallas kernels, make_table(): pl.pallas_call(functools.partial(table_body, len(weights)), in_specs=[pl....  4.98 us
    unnamed x56, local copies, waits for them, and re-layouts  3.6 us
  transfers between devices with their start and end apart: 26, of which 14 were waited for; matrix products, arithmetic and copies ran while one was open for 5% of the time, Pallas kernels for 15%

profile of v1, /device:TPU:0, one launch (start us, length us, event | category | flops | bytes accessed | tf_op | source)
XLA Modules:
  0.0 147.9 jit_solution(3249368849082026613)
XLA Ops:
  0.0 5.1 %collective-permute-start = (bf16[512,1024]{1,0:T(8,128)(2,1)}, bf16[512,1024]{1,0:T(8,128)(2,1)S(1)}, u32[]{:S(2)}, u32[]{:S(2)}) collective-permute-start(bf16[512,1024]{1,0:T(8,128)(2,1)} %own_ref.1), channel_id=1, source_target_pairs={{0,2},{4,6},{9,11},{13,15},{18,16},{22,20},{27,25},{31,29}} | collective-permute-start | bytes 3145736 | tf_op jit(solution)/shard_map/ppermute | solution.py:29
  9.5 1.3 dynamic_slice.29
  10.8 5.3 %filters.1 = (bf16[4,256,256]{2,1,0:T(8,128)(2,1)}, bf16[4,256,32]{2,1,0:T(8,128)(2,1)}, bf16[4,48,256]{2,1,0:T(8,128)(2,1)}, f32[4,1,16]{2,1,0:T(1,128)}, f32[192,128]{1,0:T(8,128)}) custom-call(f32[4,16]{1,0:T(4,128)} %bitcast.26, f32[4,16]{1,0:T(4,128)} %bitcast.24, f32[4,1,16]{2,1,0:T(1,128)} %bitcast.27, f32[4,1,16]{2,1,0:T(1,128)} %bitcast.25, ...), custom_call_target="tpu_custom_call" | custom-call | tf_op jit(solution)/shard_map/filters/pallas_call | solution.py:75
  16.1 1.2 fusion.place_ref
  17.6 2.7 %broadcast_select_fusion = bf16[512,1024]{1,0:T(8,128)(2,1)} fusion(bf16[512,1024]{1,0:T(8,128)(2,1)} %own_ref.1, bf16[512,1024]{1,0:T(8,128)(2,1)S(1)} %collective-permute-done.across_ref, pred[]{:T(512)S(6)} %eq.6), kind=kLoop, calls=%fused_computation | loop fusion | flops 524288 | bytes 3145729 | tf_op jit(solution)/shard_map/jit(_where)/select_n | solution.py:398
  20.4 2.3 %collective-permute-start.1 = (bf16[512,1024]{1,0:T(8,128)(2,1)}, bf16[512,1024]{1,0:T(8,128)(2,1)}, u32[]{:S(2)}, u32[]{:S(2)}) collective-permute-start(bf16[512,1024]{1,0:T(8,128)(2,1)} %broadcast_select_fusion), channel_id=1, source_target_pairs={{0,1},{2,3},{4,5},{6,7},{9,8},{11,10},{13,12},{15,14},{16,17},{18,... | collective-permute-start | bytes 3145736 | tf_op jit(solution)/shard_map/ppermute | solution.py:29
  23.4 1.0 dynamic-slice_bitcast_fusion
  24.4 1.5 %collective-permute-start.2 = (bf16[3,512,256]{2,1,0:T(8,128)(2,1)S(1)}, bf16[3,512,256]{2,1,0:T(8,128)(2,1)S(1)}, u32[]{:S(2)}, u32[]{:S(2)}) collective-permute-start(bf16[3,512,256]{2,1,0:T(8,128)(2,1)S(1)} %get-tuple-element.81), channel_id=1, source_target_pairs={{0,4},{1,5},{2,6},{3,7},{4,0},{5,1},{6,2},{7,3},{8,12},{9,13},{10,... | collective-permute-start | bytes 2359304 | tf_op jit(solution)/shard_map/ppermute | solution.py:29
  25.9 12.0 %collective-permute-start.8 = (bf16[512,512]{1,0:T(8,128)(2,1)S(1)}, bf16[512,512]{1,0:T(8,128)(2,1)S(1)}, u32[]{:S(2)}, u32[]{:S(2)}) collective-permute-start(bf16[512,512]{1,0:T(8,128)(2,1)S(1)} %collective-permute-done.7.refs_4_), channel_id=1, source_target_pairs={{0,8},{1,9},{2,10},{3,11},{4,0},{5,1},{6,2},{7,3},{8,16},{9,17},{1... | collective-permute-start | bytes 1572872 | tf_op jit(solution)/shard_map/ppermute | solution.py:29
  38.0 1.5 %collective-permute-start.3 = (s32[1,512]{1,0:T(1,128)S(1)}, s32[1,512]{1,0:T(1,128)S(1)}, u32[]{:S(2)}, u32[]{:S(2)}) collective-permute-start(s32[1,512]{1,0:T(1,128)S(1)} %bitcast.30), channel_id=1, source_target_pairs={{0,4},{1,5},{2,6},{3,7},{4,0},{5,1},{6,2},{7,3},{8,12},{9,13},{10,... | collective-permute-start | bytes 6152 | tf_op jit(solution)/shard_map/ppermute | solution.py:29
  39.5 14.1 %collective-permute-done.3.refs_3_ = s32[1,512]{1,0:T(1,128)S(1)} collective-permute-done((s32[1,512]{1,0:T(1,128)S(1)}, s32[1,512]{1,0:T(1,128)S(1)}, u32[]{:S(2)}, u32[]{:S(2)}) %collective-permute-start.3) | collective-permute-done | bytes 2080 | tf_op jit(solution)/shard_map/ppermute | solution.py:29
  54.5 5.0 %table.1 = (bf16[208,512]{1,0:T(8,128)(2,1)}, bf16[208,512]{1,0:T(8,128)(2,1)}, bf16[208,512]{1,0:T(8,128)(2,1)}, bf16[208,512]{1,0:T(8,128)(2,1)}) custom-call(s32[22]{0:T(128)} %fusion.place_ref, bf16[512,1024]{1,0:T(8,128)(2,1)} %own_ref.1, bf16[512,1024]{1,0:T(8,128)(2,1)} %copy-done.1, bf16[512,1024]{1,0:T(8,128)(2,1)} %collective-permute-done.1.beside_ref, ...), custom_call_target="tpu_custom_call" | custom-call | tf_op jit(solution)/shard_map/table/pallas_call | solution.py:143
  59.5 6.2 %collective-permute-start.5 = (bf16[208,512]{1,0:T(8,128)(2,1)}, bf16[208,512]{1,0:T(8,128)(2,1)S(1)}, u32[]{:S(2)}, u32[]{:S(2)}) collective-permute-start(bf16[208,512]{1,0:T(8,128)(2,1)} %get-tuple-element.51), channel_id=1, source_target_pairs={{0,16},{1,17},{2,18},{3,19},{4,20},{5,21},{6,22},{7,23},{8,24},{9,... | collective-permute-start | bytes 638984 | tf_op jit(solution)/shard_map/ppermute | solution.py:29
  65.7 5.9 %collective-permute-done.4.refs_1_ = bf16[208,512]{1,0:T(8,128)(2,1)S(1)} collective-permute-done((bf16[208,512]{1,0:T(8,128)(2,1)}, bf16[208,512]{1,0:T(8,128)(2,1)S(1)}, u32[]{:S(2)}, u32[]{:S(2)}) %collective-permute-start.4) | collective-permute-done | bytes 213024 | tf_op jit(solution)/shard_map/ppermute | solution.py:29
  71.5 8.7 %collective-permute-done.5.refs_2_ = bf16[208,512]{1,0:T(8,128)(2,1)S(1)} collective-permute-done((bf16[208,512]{1,0:T(8,128)(2,1)}, bf16[208,512]{1,0:T(8,128)(2,1)S(1)}, u32[]{:S(2)}, u32[]{:S(2)}) %collective-permute-start.5) | collective-permute-done | bytes 213024 | tf_op jit(solution)/shard_map/ppermute | solution.py:29
  80.2 4.2 %collective-permute-start.17 = (bf16[512,512]{1,0:T(8,128)(2,1)S(1)}, bf16[512,512]{1,0:T(8,128)(2,1)S(1)}, u32[]{:S(2)}, u32[]{:S(2)}) collective-permute-start(bf16[512,512]{1,0:T(8,128)(2,1)S(1)} %collective-permute-done.8.refs_5_), channel_id=1, source_target_pairs={{0,8},{1,9},{2,10},{3,11},{4,0},{5,1},{6,2},{7,3},{8,16},{9,17},{1... | collective-permute-start | bytes 1572872 | tf_op jit(solution)/shard_map/ppermute | solution.py:29
  84.4 12.2 %mixer.1 = (bf16[64,512]{1,0:T(8,128)(2,1)}, bf16[64,512]{1,0:T(8,128)(2,1)}, bf16[64,512]{1,0:T(8,128)(2,1)}, bf16[64,512]{1,0:T(8,128)(2,1)}, bf16[64,512]{1,0...) custom-call(s32[22]{0:T(128)} %fusion.place_ref, ...), custom_call_target="tpu_custom_call" | custom-call | tf_op jit(solution)/shard_map/mixer/pallas_call | solution.py:236
  96.7 1.5 %collective-permute-start.10 = (bf16[64,512]{1,0:T(8,128)(2,1)}, bf16[64,512]{1,0:T(8,128)(2,1)S(1)}, u32[]{:S(2)}, u32[]{:S(2)}) collective-permute-start(bf16[64,512]{1,0:T(8,128)(2,1)} %get-tuple-element.60), channel_id=1, source_target_pairs={{0,4},{1,5},{2,6},{3,7},{4,8},{5,9},{6,10},{7,11},{8,12},{9,13},{1... | collective-permute-start | bytes 196616 | tf_op jit(solution)/shard_map/ppermute | solution.py:29
  98.2 2.0 %collective-permute-start.11 = (bf16[64,512]{1,0:T(8,128)(2,1)}, bf16[64,512]{1,0:T(8,128)(2,1)S(1)}, u32[]{:S(2)}, u32[]{:S(2)}) collective-permute-start(bf16[64,512]{1,0:T(8,128)(2,1)} %get-tuple-element.61), channel_id=1, source_target_pairs={{0,8},{1,9},{2,10},{3,11},{4,12},{5,13},{6,14},{7,15},{8,16},{9,17... | collective-permute-start | bytes 196616 | tf_op jit(solution)/shard_map/ppermute | solution.py:29
  100.2 4.4 %collective-permute-done.10.refs_1_ = bf16[64,512]{1,0:T(8,128)(2,1)S(1)} collective-permute-done((bf16[64,512]{1,0:T(8,128)(2,1)}, bf16[64,512]{1,0:T(8,128)(2,1)S(1)}, u32[]{:S(2)}, u32[]{:S(2)}) %collective-permute-start.10) | collective-permute-done | bytes 65568 | tf_op jit(solution)/shard_map/ppermute | solution.py:29
  104.7 2.6 %collective-permute-start.14 = (bf16[64,512]{1,0:T(8,128)(2,1)}, bf16[64,512]{1,0:T(8,128)(2,1)S(1)}, u32[]{:S(2)}, u32[]{:S(2)}) collective-permute-start(bf16[64,512]{1,0:T(8,128)(2,1)} %get-tuple-element.64), channel_id=1, source_target_pairs={{0,20},{1,21},{2,22},{3,23},{4,24},{5,25},{6,26},{7,27},{8,28},{9,... | collective-permute-start | bytes 196616 | tf_op jit(solution)/shard_map/ppermute | solution.py:29
  107.3 1.1 collective-permute-done.12.refs_3_
  108.3 2.5 %collective-permute-start.15 = (bf16[64,512]{1,0:T(8,128)(2,1)}, bf16[64,512]{1,0:T(8,128)(2,1)S(1)}, u32[]{:S(2)}, u32[]{:S(2)}) collective-permute-start(bf16[64,512]{1,0:T(8,128)(2,1)} %get-tuple-element.65), channel_id=1, source_target_pairs={{0,24},{1,25},{2,26},{3,27},{4,28},{5,29},{6,30},{7,31},{8,0},{9,1... | collective-permute-start | bytes 196616 | tf_op jit(solution)/shard_map/ppermute | solution.py:29
  112.2 1.5 %collective-permute-done.15.refs_6_ = bf16[64,512]{1,0:T(8,128)(2,1)S(1)} collective-permute-done((bf16[64,512]{1,0:T(8,128)(2,1)}, bf16[64,512]{1,0:T(8,128)(2,1)S(1)}, u32[]{:S(2)}, u32[]{:S(2)}) %collective-permute-start.15) | collective-permute-done | bytes 65568 | tf_op jit(solution)/shard_map/ppermute | solution.py:29
  113.7 2.4 %collective-permute-done.16.refs_7_ = bf16[64,512]{1,0:T(8,128)(2,1)S(1)} collective-permute-done((bf16[64,512]{1,0:T(8,128)(2,1)}, bf16[64,512]{1,0:T(8,128)(2,1)S(1)}, u32[]{:S(2)}, u32[]{:S(2)}) %collective-permute-start.16) | collective-permute-done | bytes 65568 | tf_op jit(solution)/shard_map/ppermute | solution.py:29
  116.7 2.2 %order.1.refs_0_ = bf16[512,512]{1,0:T(8,128)(2,1)} custom-call(s32[22]{0:T(128)} %fusion.place_ref, bf16[64,512]{1,0:T(8,128)(2,1)} %get-tuple-element.69.refs_0_, bf16[64,512]{1,0:T(8,128)(2,1)} %copy-done.17, bf16[64,512]{1,0:T(8,128)(2,1)} %copy-done.18, bf16[64,512]{1,0:T(8,128)(2,1)} %copy-done.19, bf16[64,512]{1,0:T(8,128)(2,1)} %copy-done.20, ...), custom_call_target="tpu_custom_call" | custom-call | tf_op jit(solution)/shard_map/order/pallas_call | solution.py:266
  119.0 2.0 %collective-permute-start.23 = (bf16[512,512]{1,0:T(8,128)(2,1)}, bf16[512,512]{1,0:T(8,128)(2,1)S(1)}, u32[]{:S(2)}, u32[]{:S(2)}) collective-permute-start(bf16[512,512]{1,0:T(8,128)(2,1)} %copy-done.10), channel_id=1, source_target_pairs={{0,4},{1,5},{2,6},{3,7},{4,12},{5,13},{6,14},{7,15},{8,0},{9,1},{1... | collective-permute-start | bytes 1572872 | tf_op jit(solution)/shard_map/ppermute | solution.py:29
  121.0 8.9 %collective-permute-done.19.refs_1_ = bf16[512,512]{1,0:T(8,128)(2,1)S(1)} collective-permute-done((bf16[512,512]{1,0:T(8,128)(2,1)}, bf16[512,512]{1,0:T(8,128)(2,1)S(1)}, u32[]{:S(2)}, u32[]{:S(2)}) %collective-permute-start.19) | collective-permute-done | bytes 524320 | tf_op jit(solution)/shard_map/ppermute | solution.py:29
  130.7 2.3 %collective-permute-start.25 = (bf16[256,512]{1,0:T(8,128)(2,1)S(1)}, bf16[256,512]{1,0:T(8,128)(2,1)S(1)}, u32[]{:S(2)}, u32[]{:S(2)}) collective-permute-start(bf16[256,512]{1,0:T(8,128)(2,1)S(1)} %slice.7), channel_id=1, source_target_pairs={{0,4},{1,5},{2,6},{3,7},{4,12},{5,13},{6,14},{7,15},{8,0},{9,1},{1... | collective-permute-start | bytes 786440 | tf_op jit(solution)/shard_map/ppermute | solution.py:29
  133.0 5.8 %collective-permute-done.25.refs_12_ = bf16[256,512]{1,0:T(8,128)(2,1)S(1)} collective-permute-done((bf16[256,512]{1,0:T(8,128)(2,1)S(1)}, bf16[256,512]{1,0:T(8,128)(2,1)S(1)}, u32[]{:S(2)}, u32[]{:S(2)}) %collective-permute-start.25) | collective-permute-done | bytes 262176 | tf_op jit(solution)/shard_map/ppermute | solution.py:29
  138.8 2.0 %collective-permute-done.24.refs_11_ = bf16[256,512]{1,0:T(8,128)(2,1)S(1)} collective-permute-done((bf16[256,512]{1,0:T(8,128)(2,1)S(1)}, bf16[256,512]{1,0:T(8,128)(2,1)S(1)}, u32[]{:S(2)}, u32[]{:S(2)}) %collective-permute-start.24) | collective-permute-done | bytes 262176 | tf_op jit(solution)/shard_map/ppermute | solution.py:29
  141.5 6.4 %product.1 = bf16[512,1024]{1,0:T(8,128)(2,1)} custom-call(s32[22]{0:T(128)} %fusion.place_ref, bf16[512,512]{1,0:T(8,128)(2,1)} %order.1.refs_0_, bf16[512,512]{1,0:T(8,128)(2,1)} %copy-done.11, bf16[512,512]{1,0:T(8,128)(2,1)} %collective-permute-done.20.refs_2_, bf16[512,512]{1,0:T(8,128)(2,1)} %collective-permute-done.21.refs_3_, ...), custom_call_target="tpu_custom_call" | custom-call | tf_op jit(solution)/shard_map/product/pallas_call | solution.py:297
  (92 shorter events, 9.8 us)
Async XLA Ops:
  0.0 17.6 %collective-permute-start = (bf16[512,1024]{1,0:T(8,128)(2,1)}, bf16[512,1024]{1,0:T(8,128)(2,1)S(1)}, u32[]{:S(2)}, u32[]{:S(2)}) collective-permute-start(bf16[512,1024]{1,0:T(8,128)(2,1)} %own_ref.1), channel_id=1, source_target_pairs={{0,2},{4,6},{9,11},{13,15},{18,16},{22,20},{27,25},{31,29}} | collective-permute-start | bytes 3145736 | tf_op jit(solution)/shard_map/ppermute | solution.py:29
  20.4 33.2 %collective-permute-start.1 = (bf16[512,1024]{1,0:T(8,128)(2,1)}, bf16[512,1024]{1,0:T(8,128)(2,1)}, u32[]{:S(2)}, u32[]{:S(2)}) collective-permute-start(bf16[512,1024]{1,0:T(8,128)(2,1)} %broadcast_select_fusion), channel_id=1, source_target_pairs={{0,1},{2,3},{4,5},{6,7},{9,8},{11,10},{13,12},{15,14},{16,17},{18,... | collective-permute-start | bytes 3145736 | tf_op jit(solution)/shard_map/ppermute | solution.py:29
  22.7 3.3 %collective-permute-start.7 = (bf16[512,512]{1,0:T(8,128)(2,1)S(1)}, bf16[512,512]{1,0:T(8,128)(2,1)S(1)}, u32[]{:S(2)}, u32[]{:S(2)}) collective-permute-start(bf16[512,512]{1,0:T(8,128)(2,1)S(1)} %copy-done.26), channel_id=1, source_target_pairs={{0,0},{1,16},{2,8},{3,24},{4,4},{5,20},{6,12},{7,28},{8,9},{9,25},... | collective-permute-start | bytes 1572872 | tf_op jit(solution)/shard_map/ppermute | solution.py:29
  23.4 14.6 %copy-start.24 = (s32[512]{0:T(512)S(1)}, s32[512]{0:T(512)}, u32[]{:S(2)}) copy-start(s32[512]{0:T(512)} %param.10) | copy-start | bytes 6148
  24.4 29.2 %collective-permute-start.2 = (bf16[3,512,256]{2,1,0:T(8,128)(2,1)S(1)}, bf16[3,512,256]{2,1,0:T(8,128)(2,1)S(1)}, u32[]{:S(2)}, u32[]{:S(2)}) collective-permute-start(bf16[3,512,256]{2,1,0:T(8,128)(2,1)S(1)} %get-tuple-element.81), channel_id=1, source_target_pairs={{0,4},{1,5},{2,6},{3,7},{4,0},{5,1},{6,2},{7,3},{8,12},{9,13},{10,... | collective-permute-start | bytes 2359304 | tf_op jit(solution)/shard_map/ppermute | solution.py:29
  25.9 114.9 %copy-start.6 = (bf16[512,512]{1,0:T(8,128)(2,1)}, bf16[512,512]{1,0:T(8,128)(2,1)S(1)}, u32[]{:S(2)}) copy-start(bf16[512,512]{1,0:T(8,128)(2,1)S(1)} %collective-permute-done.7.refs_4_) | copy-start | bytes 1572868
  25.9 39.7 %collective-permute-start.8 = (bf16[512,512]{1,0:T(8,128)(2,1)S(1)}, bf16[512,512]{1,0:T(8,128)(2,1)S(1)}, u32[]{:S(2)}, u32[]{:S(2)}) collective-permute-start(bf16[512,512]{1,0:T(8,128)(2,1)S(1)} %collective-permute-done.7.refs_4_), channel_id=1, source_target_pairs={{0,8},{1,9},{2,10},{3,11},{4,0},{5,1},{6,2},{7,3},{8,16},{9,17},{1... | collective-permute-start | bytes 1572872 | tf_op jit(solution)/shard_map/ppermute | solution.py:29
  38.0 27.7 %collective-permute-start.9 = (bf16[512,512]{1,0:T(8,128)(2,1)S(1)}, bf16[512,512]{1,0:T(8,128)(2,1)S(1)}, u32[]{:S(2)}, u32[]{:S(2)}) collective-permute-start(bf16[512,512]{1,0:T(8,128)(2,1)S(1)} %collective-permute-done.7.refs_4_), channel_id=1, source_target_pairs={{0,4},{1,5},{2,6},{3,7},{4,12},{5,13},{6,14},{7,15},{8,0},{9,1},{1... | collective-permute-start | bytes 1572872 | tf_op jit(solution)/shard_map/ppermute | solution.py:29
  38.0 15.6 %collective-permute-start.3 = (s32[1,512]{1,0:T(1,128)S(1)}, s32[1,512]{1,0:T(1,128)S(1)}, u32[]{:S(2)}, u32[]{:S(2)}) collective-permute-start(s32[1,512]{1,0:T(1,128)S(1)} %bitcast.30), channel_id=1, source_target_pairs={{0,4},{1,5},{2,6},{3,7},{4,0},{5,1},{6,2},{7,3},{8,12},{9,13},{10,... | collective-permute-start | bytes 6152 | tf_op jit(solution)/shard_map/ppermute | solution.py:29
  59.4 12.1 %collective-permute-start.4 = (bf16[208,512]{1,0:T(8,128)(2,1)}, bf16[208,512]{1,0:T(8,128)(2,1)S(1)}, u32[]{:S(2)}, u32[]{:S(2)}) collective-permute-start(bf16[208,512]{1,0:T(8,128)(2,1)} %get-tuple-element.50), channel_id=1, source_target_pairs={{0,8},{1,9},{2,10},{3,11},{4,12},{5,13},{6,14},{7,15},{8,16},{9,17... | collective-permute-start | bytes 638984 | tf_op jit(solution)/shard_map/ppermute | solution.py:29
  59.5 20.8 %collective-permute-start.5 = (bf16[208,512]{1,0:T(8,128)(2,1)}, bf16[208,512]{1,0:T(8,128)(2,1)S(1)}, u32[]{:S(2)}, u32[]{:S(2)}) collective-permute-start(bf16[208,512]{1,0:T(8,128)(2,1)} %get-tuple-element.51), channel_id=1, source_target_pairs={{0,16},{1,17},{2,18},{3,19},{4,20},{5,21},{6,22},{7,23},{8,24},{9,... | collective-permute-start | bytes 638984 | tf_op jit(solution)/shard_map/ppermute | solution.py:29
  65.6 14.6 %collective-permute-start.6 = (bf16[208,512]{1,0:T(8,128)(2,1)}, bf16[208,512]{1,0:T(8,128)(2,1)S(1)}, u32[]{:S(2)}, u32[]{:S(2)}) collective-permute-start(bf16[208,512]{1,0:T(8,128)(2,1)} %get-tuple-element.52), channel_id=1, source_target_pairs={{0,24},{1,25},{2,26},{3,27},{4,28},{5,29},{6,30},{7,31},{8,0},{9,1... | collective-permute-start | bytes 638984 | tf_op jit(solution)/shard_map/ppermute | solution.py:29
  65.7 64.8 %copy-start.7 = (bf16[512,512]{1,0:T(8,128)(2,1)}, bf16[512,512]{1,0:T(8,128)(2,1)S(1)}, u32[]{:S(2)}) copy-start(bf16[512,512]{1,0:T(8,128)(2,1)S(1)} %collective-permute-done.8.refs_5_) | copy-start | bytes 1572868
  65.7 64.8 %copy-start.8 = (bf16[512,512]{1,0:T(8,128)(2,1)}, bf16[512,512]{1,0:T(8,128)(2,1)S(1)}, u32[]{:S(2)}) copy-start(bf16[512,512]{1,0:T(8,128)(2,1)S(1)} %collective-permute-done.9.refs_8_) | copy-start | bytes 1572868
  71.5 12.9 %copy-start.14 = (bf16[208,512]{1,0:T(8,128)(2,1)}, bf16[208,512]{1,0:T(8,128)(2,1)S(1)}, u32[]{:S(2)}) copy-start(bf16[208,512]{1,0:T(8,128)(2,1)S(1)} %collective-permute-done.4.refs_1_) | copy-start | bytes 638980
  80.2 35.9 %collective-permute-start.17 = (bf16[512,512]{1,0:T(8,128)(2,1)S(1)}, bf16[512,512]{1,0:T(8,128)(2,1)S(1)}, u32[]{:S(2)}, u32[]{:S(2)}) collective-permute-start(bf16[512,512]{1,0:T(8,128)(2,1)S(1)} %collective-permute-done.8.refs_5_), channel_id=1, source_target_pairs={{0,8},{1,9},{2,10},{3,11},{4,0},{5,1},{6,2},{7,3},{8,16},{9,17},{1... | collective-permute-start | bytes 1572872 | tf_op jit(solution)/shard_map/ppermute | solution.py:29
  84.4 31.7 %collective-permute-start.18 = (bf16[512,512]{1,0:T(8,128)(2,1)S(1)}, bf16[512,512]{1,0:T(8,128)(2,1)S(1)}, u32[]{:S(2)}, u32[]{:S(2)}) collective-permute-start(bf16[512,512]{1,0:T(8,128)(2,1)S(1)} %collective-permute-done.9.refs_8_), channel_id=1, source_target_pairs={{0,4},{1,5},{2,6},{3,7},{4,12},{5,13},{6,14},{7,15},{8,0},{9,1},{1... | collective-permute-start | bytes 1572872 | tf_op jit(solution)/shard_map/ppermute | solution.py:29
  96.7 8.0 %collective-permute-start.10 = (bf16[64,512]{1,0:T(8,128)(2,1)}, bf16[64,512]{1,0:T(8,128)(2,1)S(1)}, u32[]{:S(2)}, u32[]{:S(2)}) collective-permute-start(bf16[64,512]{1,0:T(8,128)(2,1)} %get-tuple-element.60), channel_id=1, source_target_pairs={{0,4},{1,5},{2,6},{3,7},{4,8},{5,9},{6,10},{7,11},{8,12},{9,13},{1... | collective-permute-start | bytes 196616 | tf_op jit(solution)/shard_map/ppermute | solution.py:29
  98.2 6.5 %collective-permute-start.11 = (bf16[64,512]{1,0:T(8,128)(2,1)}, bf16[64,512]{1,0:T(8,128)(2,1)S(1)}, u32[]{:S(2)}, u32[]{:S(2)}) collective-permute-start(bf16[64,512]{1,0:T(8,128)(2,1)} %get-tuple-element.61), channel_id=1, source_target_pairs={{0,8},{1,9},{2,10},{3,11},{4,12},{5,13},{6,14},{7,15},{8,16},{9,17... | collective-permute-start | bytes 196616 | tf_op jit(solution)/shard_map/ppermute | solution.py:29
  100.2 8.1 %collective-permute-start.12 = (bf16[64,512]{1,0:T(8,128)(2,1)}, bf16[64,512]{1,0:T(8,128)(2,1)S(1)}, u32[]{:S(2)}, u32[]{:S(2)}) collective-permute-start(bf16[64,512]{1,0:T(8,128)(2,1)} %get-tuple-element.62), channel_id=1, source_target_pairs={{0,12},{1,13},{2,14},{3,15},{4,16},{5,17},{6,18},{7,19},{8,20},{9,... | collective-permute-start | bytes 196616 | tf_op jit(solution)/shard_map/ppermute | solution.py:29
  104.6 7.0 %collective-permute-start.13 = (bf16[64,512]{1,0:T(8,128)(2,1)}, bf16[64,512]{1,0:T(8,128)(2,1)S(1)}, u32[]{:S(2)}, u32[]{:S(2)}) collective-permute-start(bf16[64,512]{1,0:T(8,128)(2,1)} %get-tuple-element.63), channel_id=1, source_target_pairs={{0,16},{1,17},{2,18},{3,19},{4,20},{5,21},{6,22},{7,23},{8,24},{9,... | collective-permute-start | bytes 196616 | tf_op jit(solution)/shard_map/ppermute | solution.py:29
  104.7 7.5 %collective-permute-start.14 = (bf16[64,512]{1,0:T(8,128)(2,1)}, bf16[64,512]{1,0:T(8,128)(2,1)S(1)}, u32[]{:S(2)}, u32[]{:S(2)}) collective-permute-start(bf16[64,512]{1,0:T(8,128)(2,1)} %get-tuple-element.64), channel_id=1, source_target_pairs={{0,20},{1,21},{2,22},{3,23},{4,24},{5,25},{6,26},{7,27},{8,28},{9,... | collective-permute-start | bytes 196616 | tf_op jit(solution)/shard_map/ppermute | solution.py:29
  108.3 5.4 %collective-permute-start.15 = (bf16[64,512]{1,0:T(8,128)(2,1)}, bf16[64,512]{1,0:T(8,128)(2,1)S(1)}, u32[]{:S(2)}, u32[]{:S(2)}) collective-permute-start(bf16[64,512]{1,0:T(8,128)(2,1)} %get-tuple-element.65), channel_id=1, source_target_pairs={{0,24},{1,25},{2,26},{3,27},{4,28},{5,29},{6,30},{7,31},{8,0},{9,1... | collective-permute-start | bytes 196616 | tf_op jit(solution)/shard_map/ppermute | solution.py:29
  111.6 4.5 %collective-permute-start.16 = (bf16[64,512]{1,0:T(8,128)(2,1)}, bf16[64,512]{1,0:T(8,128)(2,1)S(1)}, u32[]{:S(2)}, u32[]{:S(2)}) collective-permute-start(bf16[64,512]{1,0:T(8,128)(2,1)} %get-tuple-element.66), channel_id=1, source_target_pairs={{0,28},{1,29},{2,30},{3,31},{4,0},{5,1},{6,2},{7,3},{8,4},{9,5},{1... | collective-permute-start | bytes 196616 | tf_op jit(solution)/shard_map/ppermute | solution.py:29
  116.1 24.7 %copy-start.9 = (bf16[512,512]{1,0:T(8,128)(2,1)}, bf16[512,512]{1,0:T(8,128)(2,1)S(1)}, u32[]{:S(2)}) copy-start(bf16[512,512]{1,0:T(8,128)(2,1)S(1)} %collective-permute-done.17.refs_6_) | copy-start | bytes 1572868
  118.9 11.0 %collective-permute-start.19 = (bf16[512,512]{1,0:T(8,128)(2,1)}, bf16[512,512]{1,0:T(8,128)(2,1)S(1)}, u32[]{:S(2)}, u32[]{:S(2)}) collective-permute-start(bf16[512,512]{1,0:T(8,128)(2,1)} %order.1.refs_0_), channel_id=1, source_target_pairs={{0,2},{1,3},{2,0},{3,1},{4,6},{5,7},{6,4},{7,5},{8,10},{9,11},{10,... | collective-permute-start | bytes 1572872 | tf_op jit(solution)/shard_map/ppermute | solution.py:29
  118.9 11.4 %collective-permute-start.22 = (bf16[512,512]{1,0:T(8,128)(2,1)S(1)}, bf16[512,512]{1,0:T(8,128)(2,1)S(1)}, u32[]{:S(2)}, u32[]{:S(2)}) collective-permute-start(bf16[512,512]{1,0:T(8,128)(2,1)S(1)} %collective-permute-done.17.refs_6_), channel_id=1, source_target_pairs={{0,8},{1,9},{2,10},{3,11},{4,0},{5,1},{6,2},{7,3},{8,16},{9,17},{1... | collective-permute-start | bytes 1572872 | tf_op jit(solution)/shard_map/ppermute | solution.py:29
  119.0 11.5 %collective-permute-start.23 = (bf16[512,512]{1,0:T(8,128)(2,1)}, bf16[512,512]{1,0:T(8,128)(2,1)S(1)}, u32[]{:S(2)}, u32[]{:S(2)}) collective-permute-start(bf16[512,512]{1,0:T(8,128)(2,1)} %copy-done.10), channel_id=1, source_target_pairs={{0,4},{1,5},{2,6},{3,7},{4,12},{5,13},{6,14},{7,15},{8,0},{9,1},{1... | collective-permute-start | bytes 1572872 | tf_op jit(solution)/shard_map/ppermute | solution.py:29
  121.0 12.0 %collective-permute-start.20 = (bf16[512,512]{1,0:T(8,128)(2,1)}, bf16[512,512]{1,0:T(8,128)(2,1)}, u32[]{:S(2)}, u32[]{:S(2)}) collective-permute-start(bf16[512,512]{1,0:T(8,128)(2,1)} %order.1.refs_0_), channel_id=1, source_target_pairs={{0,1},{1,0},{2,3},{3,2},{4,5},{5,4},{6,7},{7,6},{8,9},{9,8},{10,11... | collective-permute-start | bytes 1572872 | tf_op jit(solution)/shard_map/ppermute | solution.py:29
  129.9 10.9 %collective-permute-start.21 = (bf16[512,512]{1,0:T(8,128)(2,1)S(1)}, bf16[512,512]{1,0:T(8,128)(2,1)}, u32[]{:S(2)}, u32[]{:S(2)}) collective-permute-start(bf16[512,512]{1,0:T(8,128)(2,1)S(1)} %collective-permute-done.19.refs_1_), channel_id=1, source_target_pairs={{0,1},{1,0},{2,3},{3,2},{4,5},{5,4},{6,7},{7,6},{8,9},{9,8},{10,11... | collective-permute-start | bytes 1572872 | tf_op jit(solution)/shard_map/ppermute | solution.py:29
  130.7 8.1 %collective-permute-start.25 = (bf16[256,512]{1,0:T(8,128)(2,1)S(1)}, bf16[256,512]{1,0:T(8,128)(2,1)S(1)}, u32[]{:S(2)}, u32[]{:S(2)}) collective-permute-start(bf16[256,512]{1,0:T(8,128)(2,1)S(1)} %slice.7), channel_id=1, source_target_pairs={{0,4},{1,5},{2,6},{3,7},{4,12},{5,13},{6,14},{7,15},{8,0},{9,1},{1... | collective-permute-start | bytes 786440 | tf_op jit(solution)/shard_map/ppermute | solution.py:29
  133.0 7.8 %collective-permute-start.24 = (bf16[256,512]{1,0:T(8,128)(2,1)S(1)}, bf16[256,512]{1,0:T(8,128)(2,1)S(1)}, u32[]{:S(2)}, u32[]{:S(2)}) collective-permute-start(bf16[256,512]{1,0:T(8,128)(2,1)S(1)} %slice.6), channel_id=1, source_target_pairs={{0,8},{1,9},{2,10},{3,11},{4,0},{5,1},{6,2},{7,3},{8,16},{9,17},{1... | collective-permute-start | bytes 786440 | tf_op jit(solution)/shard_map/ppermute | solution.py:29
  (21 other events, 101.8 us)

commit v2 on v1

--- a/solution.py
+++ b/solution.py
@@ -31,6 +31,10 @@
 
 def after(values, *others):
     return lax.optimization_barrier((tuple(values), others))[0]
+
+
+def near(*values):
+    return [pltpu.with_memory_space_constraint(value, pltpu.VMEM) for value in values]
 
 
 def split_high_low(value):
@@ -144,7 +148,7 @@
         functools.partial(table_body, len(weights)),
         in_specs=[pl.BlockSpec(memory_space=pltpu.SMEM)] + [vmem] * (4 + len(weights) + len(tokens)),
         out_specs=[vmem] * pieces,
-        out_shape=[jax.ShapeDtypeStruct((EXTRA + 3 * channels // pieces, vocab), BF16)] * pieces,
+        out_shape=[pltpu.VMEM((EXTRA + 3 * channels // pieces, vocab), BF16)] * pieces,
         scratch_shapes=[
             pltpu.VMEM(own.shape, F32),
             pltpu.VMEM(own.shape, BF16),
@@ -237,7 +241,7 @@
         functools.partial(mixer_body, width, taps),
         in_specs=[pl.BlockSpec(memory_space=pltpu.SMEM)] + [vmem] * (5 + len(pieces)),
         out_specs=[vmem] * blocks,
-        out_shape=[jax.ShapeDtypeStruct((channels, block), BF16)] * blocks,
+        out_shape=[pltpu.VMEM((channels, block), BF16)] * blocks,
         scratch_shapes=[
             pltpu.VMEM((channels, length), F32),
             pltpu.VMEM((channels, length), F32),
@@ -246,7 +250,7 @@
             pltpu.VMEM((blocks, channels, block), BF16),
         ],
         name="mixer",
-    )(place, *filters, *pieces)
+    )(place, *filters, *near(*pieces))
 
 
 def order_body(lows, place_ref, *refs):
@@ -267,24 +271,34 @@
         functools.partial(order_body, lows),
         in_specs=[pl.BlockSpec(memory_space=pltpu.SMEM)] + [vmem] * len(pieces),
         out_specs=vmem,
-        out_shape=jax.ShapeDtypeStruct((length, rows * len(pieces)), BF16),
+        out_shape=pltpu.VMEM((length, rows * len(pieces)), BF16),
         scratch_shapes=[pltpu.VMEM((rows * len(pieces), length), F32)],
         name="order",
-    )(place, *pieces)
+    )(place, *near(*pieces))
 
 
 def product_body(order, place_ref, *refs):
     side_refs = refs[:len(order)]
-    block_refs = refs[len(order):-3]
-    out_ref, sides_ref, sum_ref = refs[-3:]
+    out_ref, sides_ref, sum_ref, wide_ref, arrived = refs[-5:]
+    block_refs = refs[len(order):-5]
+    full, cols = block_refs[0].shape
+    copies = []
+    for at, ref in enumerate(block_refs):
+        copies.append(
+            pltpu.make_async_copy(ref, wide_ref.at[at, :ref.shape[0]], arrived.at[at])
+        )
+        copies[-1].start()
     for flip, ref in zip(order, side_refs):
         sides_ref[flip] = ref[...]
-    full, cols = block_refs[0].shape
     sum_ref[...] = jnp.zeros_like(sum_ref)
     for at, ref in enumerate(block_refs):
+        rows = ref.shape[0]
         first = full // 2 if at == len(block_refs) - 1 else 0
-        side = sides_ref[place_ref[PLACES + at], :, first:first + ref.shape[0]]
-        sum_ref[place_ref[PLACES + len(block_refs) + at]] += jnp.dot(side, ref[...], preferred_element_type=F32)
+        copies[at].wait()
+        side = sides_ref[place_ref[PLACES + at], :, first:first + rows]
+        sum_ref[place_ref[PLACES + len(block_refs) + at]] += jnp.dot(
+            side, wide_ref[at, :rows], preferred_element_type=F32
+        )
     for low in range(sum_ref.shape[0]):
         out_ref[:, low * cols:(low + 1) * cols] = sum_ref[low].astype(BF16)
 
@@ -292,19 +306,23 @@
 def make_product(place, order, sides, blocks, lows):
     length, full = sides[0].shape
     cols = blocks[0].shape[1]
-    smem = pl.BlockSpec(memory_space=pltpu.SMEM)
+    rows = blocks[0].shape[0]
     vmem = pl.BlockSpec(memory_space=pltpu.VMEM)
     return pl.pallas_call(
         functools.partial(product_body, order),
-        in_specs=[smem] + [vmem] * (len(sides) + len(blocks)),
+        in_specs=[pl.BlockSpec(memory_space=pltpu.SMEM)]
+        + [vmem] * len(sides)
+        + [pl.BlockSpec(memory_space=pl.ANY)] * len(blocks),
         out_specs=vmem,
         out_shape=jax.ShapeDtypeStruct((length, lows * cols), BF16),
         scratch_shapes=[
             pltpu.VMEM((len(sides), length, full), BF16),
             pltpu.VMEM((lows, length, cols), F32),
+            pltpu.VMEM((len(blocks), rows, cols), BF16),
+            pltpu.SemaphoreType.DMA((len(blocks),)),
         ],
         name="product",
-    )(place, *sides, *blocks)
+    )(place, *near(*sides), *blocks)
 
 
 def reverse_bits(value, count):
@@ -349,8 +367,7 @@
         return send(value, ctx_count, fsdp_count, target)
 
     by_kind = jnp.swapaxes(in_weight, 0, 1)
-    weights = [lax.dynamic_slice_in_dim(by_kind, low_at * part, part, 2)]
-    ids = [tokens[None, :]]
+    weights, ids = [], [tokens[None, :]]
     for shift in range(1, lows):
         def neighbour(i, j):
             return (i // lows * lows + (i % lows - shift) % lows, j)
@@ -358,6 +375,9 @@
         going = lax.dynamic_slice_in_dim(by_kind, (low_at - shift) % lows * part, part, 2)
         weights.append(move(going, neighbour))
         ids.append(move(tokens[None, :], neighbour))
+
+    (by_kind,) = after((by_kind,), going)
+    weights.insert(0, lax.dynamic_slice_in_dim(by_kind, low_at * part, part, 2))
 
     chips = fsdp_count // 2
     across = None
@@ -453,4 +473,6 @@
         P("fsdp"),
         P("fsdp", "ctx"),
     )
-    return jax.shard_map(body, mesh=mesh, in_specs=placed, out_specs=P("ctx", "fsdp"), check_vma=False)
+    return jax.shard_map(
+        body, mesh=mesh, in_specs=placed, out_specs=P("ctx", "fsdp"), check_vma=False
+    )

time: 148 us -> 146 us (0.986)
  waiting for transfers between devices: 56.5 us -> 59.6 us
  Pallas kernels: 31 us -> 28 us
  starting transfers between devices: 47 us -> 44 us
    ppermute x26, waiting for transfers between devices: 56.5 us -> 59.6 us  [send(): return lax.ppermute(value, AXES, pairs)]
    ppermute x26, starting transfers between devices: 47 us -> 44 us  [send(): return lax.ppermute(value, AXES, pairs)]
    unnamed x56 -> x24, local copies, waits for them, and re-layouts: 3.6 us -> 2.93 us
  transfers between devices with their start and end apart: 26 -> 26, of which waited for: 14 -> 13; matrix products, arithmetic and copies ran while one was open for 5% -> 6% of each run, Pallas kernels for 15% -> 14%
where the time goes in v2:
time: 146 us; the launch traced here: 145 us
  waiting for transfers between devices  59.6 us (41%)
  starting transfers between devices  44 us (30%)
  Pallas kernels  28 us (19%)
  local copies, waits for them, and re-layouts  10.4 us (7%)
  other arithmetic  2.73 us (2%)
    ppermute x26, waiting for transfers between devices, send(): return lax.ppermute(value, AXES, pairs)  59.6 us
    ppermute x26, starting transfers between devices, send(): return lax.ppermute(value, AXES, pairs)  44 us
    pallas_call x1, Pallas kernels, make_mixer(): pl.pallas_call(functools.partial(mixer_body, width, taps), in_specs=[pl.B...  11.2 us
    pallas_call x1, Pallas kernels, make_product(): pl.pallas_call(functools.partial(product_body, order), in_specs=[pl.Block...  6.54 us
    pallas_call x1, Pallas kernels, make_filters(): pl.pallas_call(filter_body, in_specs=[smem, smem] + [vmem] * 4, out_specs...  5.27 us
    pallas_call x1, Pallas kernels, make_table(): pl.pallas_call(functools.partial(table_body, len(weights)), in_specs=[pl....  4.07 us
    unnamed x24, local copies, waits for them, and re-layouts  2.93 us
  transfers between devices with their start and end apart: 26, of which 13 were waited for; matrix products, arithmetic and copies ran while one was open for 6% of the time, Pallas kernels for 14%

profile of v2, /device:TPU:0, one launch (start us, length us, event | category | flops | bytes accessed | tf_op | source)
XLA Modules:
  0.0 145.2 jit_solution(4022609091060462272)
XLA Ops:
  0.0 5.1 %collective-permute-start = (bf16[512,1024]{1,0:T(8,128)(2,1)}, bf16[512,1024]{1,0:T(8,128)(2,1)S(1)}, u32[]{:S(2)}, u32[]{:S(2)}) collective-permute-start(bf16[512,1024]{1,0:T(8,128)(2,1)} %own_ref.1), channel_id=1, source_target_pairs={{0,2},{4,6},{9,11},{13,15},{18,16},{22,20},{27,25},{31,29}} | collective-permute-start | bytes 3145736 | tf_op jit(solution)/shard_map/ppermute | solution.py:29
  9.5 1.3 dynamic_slice.29
  10.8 5.3 %filters.1 = (bf16[4,256,256]{2,1,0:T(8,128)(2,1)}, bf16[4,256,32]{2,1,0:T(8,128)(2,1)}, bf16[4,48,256]{2,1,0:T(8,128)(2,1)}, f32[4,1,16]{2,1,0:T(1,128)}, f32[192,128]{1,0:T(8,128)}) custom-call(f32[4,16]{1,0:T(4,128)} %bitcast.26, f32[4,16]{1,0:T(4,128)} %bitcast.24, f32[4,1,16]{2,1,0:T(1,128)} %bitcast.27, f32[4,1,16]{2,1,0:T(1,128)} %bitcast.25, ...), custom_call_target="tpu_custom_call" | custom-call | tf_op jit(solution)/shard_map/filters/pallas_call | solution.py:79
  16.1 1.2 fusion.place_ref
  17.6 2.7 %broadcast_select_fusion = bf16[512,1024]{1,0:T(8,128)(2,1)} fusion(bf16[512,1024]{1,0:T(8,128)(2,1)} %own_ref.1, bf16[512,1024]{1,0:T(8,128)(2,1)S(1)} %collective-permute-done.across_ref, pred[]{:T(512)S(6)} %eq.6), kind=kLoop, calls=%fused_computation | loop fusion | flops 524288 | bytes 3145729 | tf_op jit(solution)/shard_map/jit(_where)/select_n | solution.py:418
  20.4 2.4 %collective-permute-start.1 = (bf16[512,1024]{1,0:T(8,128)(2,1)}, bf16[512,1024]{1,0:T(8,128)(2,1)}, u32[]{:S(2)}, u32[]{:S(2)}) collective-permute-start(bf16[512,1024]{1,0:T(8,128)(2,1)} %broadcast_select_fusion), channel_id=1, source_target_pairs={{0,1},{2,3},{4,5},{6,7},{9,8},{11,10},{13,12},{15,14},{16,17},{18,... | collective-permute-start | bytes 3145736 | tf_op jit(solution)/shard_map/ppermute | solution.py:29
  22.8 1.7 %collective-permute-start.7 = (bf16[512,512]{1,0:T(8,128)(2,1)}, bf16[512,512]{1,0:T(8,128)(2,1)S(1)}, u32[]{:S(2)}, u32[]{:S(2)}) collective-permute-start(bf16[512,512]{1,0:T(8,128)(2,1)} %param.18), channel_id=1, source_target_pairs={{0,0},{1,16},{2,8},{3,24},{4,4},{5,20},{6,12},{7,28},{8,9},{9,25},... | collective-permute-start | bytes 1572872 | tf_op jit(solution)/shard_map/ppermute | solution.py:29
  25.4 1.5 %collective-permute-start.2 = (bf16[3,512,256]{2,1,0:T(8,128)(2,1)}, bf16[3,512,256]{2,1,0:T(8,128)(2,1)S(1)}, u32[]{:S(2)}, u32[]{:S(2)}) collective-permute-start(bf16[3,512,256]{2,1,0:T(8,128)(2,1)} %dynamic-slice_bitcast_fusion), channel_id=1, source_target_pairs={{0,4},{1,5},{2,6},{3,7},{4,0},{5,1},{6,2},{7,3},{8,12},{9,13},{10,... | collective-permute-start | bytes 2359304 | tf_op jit(solution)/shard_map/ppermute | solution.py:29
  26.9 11.3 %collective-permute-start.8 = (bf16[512,512]{1,0:T(8,128)(2,1)S(1)}, bf16[512,512]{1,0:T(8,128)(2,1)}, u32[]{:S(2)}, u32[]{:S(2)}) collective-permute-start(bf16[512,512]{1,0:T(8,128)(2,1)S(1)} %collective-permute-done.7.refs_4_), channel_id=1, source_target_pairs={{0,8},{1,9},{2,10},{3,11},{4,0},{5,1},{6,2},{7,3},{8,16},{9,17},{1... | collective-permute-start | bytes 1572872 | tf_op jit(solution)/shard_map/ppermute | solution.py:29
  38.2 1.5 %collective-permute-start.3 = (s32[1,512]{1,0:T(1,128)S(1)}, s32[1,512]{1,0:T(1,128)S(1)}, u32[]{:S(2)}, u32[]{:S(2)}) collective-permute-start(s32[1,512]{1,0:T(1,128)S(1)} %bitcast.30), channel_id=1, source_target_pairs={{0,4},{1,5},{2,6},{3,7},{4,0},{5,1},{6,2},{7,3},{8,12},{9,13},{10,... | collective-permute-start | bytes 6152 | tf_op jit(solution)/shard_map/ppermute | solution.py:29
  40.7 15.2 %collective-permute-done.3.refs_3_ = s32[1,512]{1,0:T(1,128)S(1)} collective-permute-done((s32[1,512]{1,0:T(1,128)S(1)}, s32[1,512]{1,0:T(1,128)S(1)}, u32[]{:S(2)}, u32[]{:S(2)}) %collective-permute-start.3) | collective-permute-done | bytes 2080 | tf_op jit(solution)/shard_map/ppermute | solution.py:29
  56.8 4.1 %table.1 = (bf16[208,512]{1,0:T(8,128)(2,1)S(1)}, bf16[208,512]{1,0:T(8,128)(2,1)S(1)}, bf16[208,512]{1,0:T(8,128)(2,1)S(1)}, bf16[208,512]{1,0:T(8,128)(2,1)S(1)}) custom-call(s32[22]{0:T(128)} %fusion.place_ref, bf16[512,1024]{1,0:T(8,128)(2,1)} %own_ref.1, bf16[512,1024]{1,0:T(8,128)(2,1)} %copy-done.1, ...), custom_call_target="tpu_custom_call" | custom-call | tf_op jit(solution)/shard_map/table/pallas_call | solution.py:147
  60.9 4.0 %collective-permute-start.5 = (bf16[208,512]{1,0:T(8,128)(2,1)S(1)}, bf16[208,512]{1,0:T(8,128)(2,1)S(1)}, u32[]{:S(2)}, u32[]{:S(2)}) collective-permute-start(bf16[208,512]{1,0:T(8,128)(2,1)S(1)} %get-tuple-element.53), channel_id=1, source_target_pairs={{0,16},{1,17},{2,18},{3,19},{4,20},{5,21},{6,22},{7,23},{8,24},{9,... | collective-permute-start | bytes 638984 | tf_op jit(solution)/shard_map/ppermute | solution.py:29
  65.0 5.7 %collective-permute-done.4.refs_1_ = bf16[208,512]{1,0:T(8,128)(2,1)S(1)} collective-permute-done((bf16[208,512]{1,0:T(8,128)(2,1)S(1)}, bf16[208,512]{1,0:T(8,128)(2,1)S(1)}, u32[]{:S(2)}, u32[]{:S(2)}) %collective-permute-start.4) | collective-permute-done | bytes 213024 | tf_op jit(solution)/shard_map/ppermute | solution.py:29
  70.7 9.4 %collective-permute-done.5.refs_2_ = bf16[208,512]{1,0:T(8,128)(2,1)S(1)} collective-permute-done((bf16[208,512]{1,0:T(8,128)(2,1)S(1)}, bf16[208,512]{1,0:T(8,128)(2,1)S(1)}, u32[]{:S(2)}, u32[]{:S(2)}) %collective-permute-start.5) | collective-permute-done | bytes 213024 | tf_op jit(solution)/shard_map/ppermute | solution.py:29
  80.1 4.5 %collective-permute-start.17 = (bf16[512,512]{1,0:T(8,128)(2,1)}, bf16[512,512]{1,0:T(8,128)(2,1)}, u32[]{:S(2)}, u32[]{:S(2)}) collective-permute-start(bf16[512,512]{1,0:T(8,128)(2,1)} %collective-permute-done.8.refs_5_), channel_id=1, source_target_pairs={{0,8},{1,9},{2,10},{3,11},{4,0},{5,1},{6,2},{7,3},{8,16},{9,17},{1... | collective-permute-start | bytes 1572872 | tf_op jit(solution)/shard_map/ppermute | solution.py:29
  84.7 11.2 %mixer.1 = (bf16[64,512]{1,0:T(8,128)(2,1)S(1)}, bf16[64,512]{1,0:T(8,128)(2,1)S(1)}, bf16[64,512]{1,0:T(8,128)(2,1)S(1)}, bf16[64,512]{1,0:T(8,128)(2,1)S(1)}, ...) custom-call(s32[22]{0:T(128)} %fusion.place_ref, ...), custom_call_target="tpu_custom_call" | custom-call | tf_op jit(solution)/shard_map/mixer/pallas_call | solution.py:240
  95.8 1.6 %collective-permute-start.10 = (bf16[64,512]{1,0:T(8,128)(2,1)S(1)}, bf16[64,512]{1,0:T(8,128)(2,1)S(1)}, u32[]{:S(2)}, u32[]{:S(2)}) collective-permute-start(bf16[64,512]{1,0:T(8,128)(2,1)S(1)} %get-tuple-element.62), channel_id=1, source_target_pairs={{0,4},{1,5},{2,6},{3,7},{4,8},{5,9},{6,10},{7,11},{8,12},{9,13},{1... | collective-permute-start | bytes 196616 | tf_op jit(solution)/shard_map/ppermute | solution.py:29
  97.4 2.0 %collective-permute-start.11 = (bf16[64,512]{1,0:T(8,128)(2,1)S(1)}, bf16[64,512]{1,0:T(8,128)(2,1)S(1)}, u32[]{:S(2)}, u32[]{:S(2)}) collective-permute-start(bf16[64,512]{1,0:T(8,128)(2,1)S(1)} %get-tuple-element.63), channel_id=1, source_target_pairs={{0,8},{1,9},{2,10},{3,11},{4,12},{5,13},{6,14},{7,15},{8,16},{9,17... | collective-permute-start | bytes 196616 | tf_op jit(solution)/shard_map/ppermute | solution.py:29
  99.4 4.2 %collective-permute-done.10.refs_1_ = bf16[64,512]{1,0:T(8,128)(2,1)S(1)} collective-permute-done((bf16[64,512]{1,0:T(8,128)(2,1)S(1)}, bf16[64,512]{1,0:T(8,128)(2,1)S(1)}, u32[]{:S(2)}, u32[]{:S(2)}) %collective-permute-start.10) | collective-permute-done | bytes 65568 | tf_op jit(solution)/shard_map/ppermute | solution.py:29
  104.5 3.2 %collective-permute-done.12.refs_3_ = bf16[64,512]{1,0:T(8,128)(2,1)S(1)} collective-permute-done((bf16[64,512]{1,0:T(8,128)(2,1)S(1)}, bf16[64,512]{1,0:T(8,128)(2,1)S(1)}, u32[]{:S(2)}, u32[]{:S(2)}) %collective-permute-start.12) | collective-permute-done | bytes 65568 | tf_op jit(solution)/shard_map/ppermute | solution.py:29
  107.7 2.2 %collective-permute-start.15 = (bf16[64,512]{1,0:T(8,128)(2,1)S(1)}, bf16[64,512]{1,0:T(8,128)(2,1)S(1)}, u32[]{:S(2)}, u32[]{:S(2)}) collective-permute-start(bf16[64,512]{1,0:T(8,128)(2,1)S(1)} %get-tuple-element.67), channel_id=1, source_target_pairs={{0,24},{1,25},{2,26},{3,27},{4,28},{5,29},{6,30},{7,31},{8,0},{9,1... | collective-permute-start | bytes 196616 | tf_op jit(solution)/shard_map/ppermute | solution.py:29
  110.1 1.1 collective-permute-start.16
  111.2 1.0 collective-permute-done.15.refs_6_
  112.2 2.2 %collective-permute-done.16.refs_7_ = bf16[64,512]{1,0:T(8,128)(2,1)S(1)} collective-permute-done((bf16[64,512]{1,0:T(8,128)(2,1)S(1)}, bf16[64,512]{1,0:T(8,128)(2,1)S(1)}, u32[]{:S(2)}, u32[]{:S(2)}) %collective-permute-start.16) | collective-permute-done | bytes 65568 | tf_op jit(solution)/shard_map/ppermute | solution.py:29
  114.4 1.0 order.1.refs_0_
  115.5 2.0 %collective-permute-start.23 = (bf16[512,512]{1,0:T(8,128)(2,1)}, bf16[512,512]{1,0:T(8,128)(2,1)S(1)}, u32[]{:S(2)}, u32[]{:S(2)}) collective-permute-start(bf16[512,512]{1,0:T(8,128)(2,1)} %collective-permute-done.18.refs_9_), channel_id=1, source_target_pairs={{0,4},{1,5},{2,6},{3,7},{4,12},{5,13},{6,14},{7,15},{8,0},{9,1},{1... | collective-permute-start | bytes 1572872 | tf_op jit(solution)/shard_map/ppermute | solution.py:29
  117.5 9.3 %collective-permute-done.19.refs_1_ = bf16[512,512]{1,0:T(8,128)(2,1)S(1)} collective-permute-done((bf16[512,512]{1,0:T(8,128)(2,1)S(1)}, bf16[512,512]{1,0:T(8,128)(2,1)S(1)}, u32[]{:S(2)}, u32[]{:S(2)}) %collective-permute-start.19) | collective-permute-done | bytes 524320 | tf_op jit(solution)/shard_map/ppermute | solution.py:29
  127.7 1.9 %collective-permute-start.25 = (bf16[256,512]{1,0:T(8,128)(2,1)S(1)}, bf16[256,512]{1,0:T(8,128)(2,1)S(1)}, u32[]{:S(2)}, u32[]{:S(2)}) collective-permute-start(bf16[256,512]{1,0:T(8,128)(2,1)S(1)} %slice.7), channel_id=1, source_target_pairs={{0,4},{1,5},{2,6},{3,7},{4,12},{5,13},{6,14},{7,15},{8,0},{9,1},{1... | collective-permute-start | bytes 786440 | tf_op jit(solution)/shard_map/ppermute | solution.py:29
  129.8 5.8 %collective-permute-done.25.refs_12_ = bf16[256,512]{1,0:T(8,128)(2,1)S(1)} collective-permute-done((bf16[256,512]{1,0:T(8,128)(2,1)S(1)}, bf16[256,512]{1,0:T(8,128)(2,1)S(1)}, u32[]{:S(2)}, u32[]{:S(2)}) %collective-permute-start.25) | collective-permute-done | bytes 262176 | tf_op jit(solution)/shard_map/ppermute | solution.py:29
  135.6 2.1 %collective-permute-done.24.refs_11_ = bf16[256,512]{1,0:T(8,128)(2,1)S(1)} collective-permute-done((bf16[256,512]{1,0:T(8,128)(2,1)S(1)}, bf16[256,512]{1,0:T(8,128)(2,1)S(1)}, u32[]{:S(2)}, u32[]{:S(2)}) %collective-permute-start.24) | collective-permute-done | bytes 262176 | tf_op jit(solution)/shard_map/ppermute | solution.py:29
  138.4 6.5 %product.1 = bf16[512,1024]{1,0:T(8,128)(2,1)} custom-call(s32[22]{0:T(128)} %fusion.place_ref, bf16[512,512]{1,0:T(8,128)(2,1)S(1)} %order.1.refs_0_, bf16[512,512]{1,0:T(8,128)(2,1)S(1)} %collective-permute-done.19.refs_1_, bf16[512,512]{1,0:T(8,128)(2,1)S(1)} %collective-permute-done.20.refs_2_, bf16[512,512]{1,0:T(8,128)(2,1)S(1)} %collective-permute-done.21.refs_3_, ...), custom_call_target="tpu_custom_call" | custom-call | tf_op jit(solution)/shard_map/product/pallas_call | solution.py:311
  (61 shorter events, 10.7 us)
Async XLA Ops:
  0.0 8.7 %copy-start = (f32[7,3,512]{2,0,1:T(8,128)S(1)}, f32[7,3,512]{2,0,1:T(8,128)}, u32[]{:S(2)}) copy-start(f32[7,3,512]{2,0,1:T(8,128)} %param.14) | copy-start | bytes 129028
  0.0 17.6 %collective-permute-start = (bf16[512,1024]{1,0:T(8,128)(2,1)}, bf16[512,1024]{1,0:T(8,128)(2,1)S(1)}, u32[]{:S(2)}, u32[]{:S(2)}) collective-permute-start(bf16[512,1024]{1,0:T(8,128)(2,1)} %own_ref.1), channel_id=1, source_target_pairs={{0,2},{4,6},{9,11},{13,15},{18,16},{22,20},{27,25},{31,29}} | collective-permute-start | bytes 3145736 | tf_op jit(solution)/shard_map/ppermute | solution.py:29
  17.6 6.8 %copy-start.2 = (bf16[512,3,512]{2,0,1:T(8,128)(2,1)S(1)}, bf16[512,3,512]{2,0,1:T(8,128)(2,1)}, u32[]{:S(2)}) copy-start(bf16[512,3,512]{2,0,1:T(8,128)(2,1)} %param.13) | copy-start | bytes 4718596
  20.4 17.8 %copy-start.9 = (s32[512]{0:T(512)S(1)}, s32[512]{0:T(512)}, u32[]{:S(2)}) copy-start(s32[512]{0:T(512)} %param.10) | copy-start | bytes 6148
  20.4 35.5 %collective-permute-start.1 = (bf16[512,1024]{1,0:T(8,128)(2,1)}, bf16[512,1024]{1,0:T(8,128)(2,1)}, u32[]{:S(2)}, u32[]{:S(2)}) collective-permute-start(bf16[512,1024]{1,0:T(8,128)(2,1)} %broadcast_select_fusion), channel_id=1, source_target_pairs={{0,1},{2,3},{4,5},{6,7},{9,8},{11,10},{13,12},{15,14},{16,17},{18,... | collective-permute-start | bytes 3145736 | tf_op jit(solution)/shard_map/ppermute | solution.py:29
  22.8 4.1 %collective-permute-start.7 = (bf16[512,512]{1,0:T(8,128)(2,1)}, bf16[512,512]{1,0:T(8,128)(2,1)S(1)}, u32[]{:S(2)}, u32[]{:S(2)}) collective-permute-start(bf16[512,512]{1,0:T(8,128)(2,1)} %param.18), channel_id=1, source_target_pairs={{0,0},{1,16},{2,8},{3,24},{4,4},{5,20},{6,12},{7,28},{8,9},{9,25},... | collective-permute-start | bytes 1572872 | tf_op jit(solution)/shard_map/ppermute | solution.py:29
  25.4 30.5 %collective-permute-start.2 = (bf16[3,512,256]{2,1,0:T(8,128)(2,1)}, bf16[3,512,256]{2,1,0:T(8,128)(2,1)S(1)}, u32[]{:S(2)}, u32[]{:S(2)}) collective-permute-start(bf16[3,512,256]{2,1,0:T(8,128)(2,1)} %dynamic-slice_bitcast_fusion), channel_id=1, source_target_pairs={{0,4},{1,5},{2,6},{3,7},{4,0},{5,1},{6,2},{7,3},{8,12},{9,13},{10,... | collective-permute-start | bytes 2359304 | tf_op jit(solution)/shard_map/ppermute | solution.py:29
  26.9 34.0 %copy-start.6 = (bf16[512,512]{1,0:T(8,128)(2,1)}, bf16[512,512]{1,0:T(8,128)(2,1)S(1)}, u32[]{:S(2)}) copy-start(bf16[512,512]{1,0:T(8,128)(2,1)S(1)} %collective-permute-done.7.refs_4_) | copy-start | bytes 1572868
  26.9 38.1 %collective-permute-start.8 = (bf16[512,512]{1,0:T(8,128)(2,1)S(1)}, bf16[512,512]{1,0:T(8,128)(2,1)}, u32[]{:S(2)}, u32[]{:S(2)}) collective-permute-start(bf16[512,512]{1,0:T(8,128)(2,1)S(1)} %collective-permute-done.7.refs_4_), channel_id=1, source_target_pairs={{0,8},{1,9},{2,10},{3,11},{4,0},{5,1},{6,2},{7,3},{8,16},{9,17},{1... | collective-permute-start | bytes 1572872 | tf_op jit(solution)/shard_map/ppermute | solution.py:29
  38.2 26.8 %collective-permute-start.9 = (bf16[512,512]{1,0:T(8,128)(2,1)S(1)}, bf16[512,512]{1,0:T(8,128)(2,1)}, u32[]{:S(2)}, u32[]{:S(2)}) collective-permute-start(bf16[512,512]{1,0:T(8,128)(2,1)S(1)} %collective-permute-done.7.refs_4_), channel_id=1, source_target_pairs={{0,4},{1,5},{2,6},{3,7},{4,12},{5,13},{6,14},{7,15},{8,0},{9,1},{1... | collective-permute-start | bytes 1572872 | tf_op jit(solution)/shard_map/ppermute | solution.py:29
  38.2 17.7 %collective-permute-start.3 = (s32[1,512]{1,0:T(1,128)S(1)}, s32[1,512]{1,0:T(1,128)S(1)}, u32[]{:S(2)}, u32[]{:S(2)}) collective-permute-start(s32[1,512]{1,0:T(1,128)S(1)} %bitcast.30), channel_id=1, source_target_pairs={{0,4},{1,5},{2,6},{3,7},{4,0},{5,1},{6,2},{7,3},{8,12},{9,13},{10,... | collective-permute-start | bytes 6152 | tf_op jit(solution)/shard_map/ppermute | solution.py:29
  60.9 9.8 %collective-permute-start.4 = (bf16[208,512]{1,0:T(8,128)(2,1)S(1)}, bf16[208,512]{1,0:T(8,128)(2,1)S(1)}, u32[]{:S(2)}, u32[]{:S(2)}) collective-permute-start(bf16[208,512]{1,0:T(8,128)(2,1)S(1)} %get-tuple-element.52), channel_id=1, source_target_pairs={{0,8},{1,9},{2,10},{3,11},{4,12},{5,13},{6,14},{7,15},{8,16},{9,17... | collective-permute-start | bytes 638984 | tf_op jit(solution)/shard_map/ppermute | solution.py:29
  60.9 19.2 %collective-permute-start.5 = (bf16[208,512]{1,0:T(8,128)(2,1)S(1)}, bf16[208,512]{1,0:T(8,128)(2,1)S(1)}, u32[]{:S(2)}, u32[]{:S(2)}) collective-permute-start(bf16[208,512]{1,0:T(8,128)(2,1)S(1)} %get-tuple-element.53), channel_id=1, source_target_pairs={{0,16},{1,17},{2,18},{3,19},{4,20},{5,21},{6,22},{7,23},{8,24},{9,... | collective-permute-start | bytes 638984 | tf_op jit(solution)/shard_map/ppermute | solution.py:29
  65.0 15.1 %collective-permute-start.6 = (bf16[208,512]{1,0:T(8,128)(2,1)S(1)}, bf16[208,512]{1,0:T(8,128)(2,1)S(1)}, u32[]{:S(2)}, u32[]{:S(2)}) collective-permute-start(bf16[208,512]{1,0:T(8,128)(2,1)S(1)} %get-tuple-element.54), channel_id=1, source_target_pairs={{0,24},{1,25},{2,26},{3,27},{4,28},{5,29},{6,30},{7,31},{8,0},{9,1... | collective-permute-start | bytes 638984 | tf_op jit(solution)/shard_map/ppermute | solution.py:29
  80.1 34.3 %collective-permute-start.17 = (bf16[512,512]{1,0:T(8,128)(2,1)}, bf16[512,512]{1,0:T(8,128)(2,1)}, u32[]{:S(2)}, u32[]{:S(2)}) collective-permute-start(bf16[512,512]{1,0:T(8,128)(2,1)} %collective-permute-done.8.refs_5_), channel_id=1, source_target_pairs={{0,8},{1,9},{2,10},{3,11},{4,0},{5,1},{6,2},{7,3},{8,16},{9,17},{1... | collective-permute-start | bytes 1572872 | tf_op jit(solution)/shard_map/ppermute | solution.py:29
  84.6 29.8 %collective-permute-start.18 = (bf16[512,512]{1,0:T(8,128)(2,1)}, bf16[512,512]{1,0:T(8,128)(2,1)}, u32[]{:S(2)}, u32[]{:S(2)}) collective-permute-start(bf16[512,512]{1,0:T(8,128)(2,1)} %collective-permute-done.9.refs_8_), channel_id=1, source_target_pairs={{0,4},{1,5},{2,6},{3,7},{4,12},{5,13},{6,14},{7,15},{8,0},{9,1},{1... | collective-permute-start | bytes 1572872 | tf_op jit(solution)/shard_map/ppermute | solution.py:29
  95.8 7.8 %collective-permute-start.10 = (bf16[64,512]{1,0:T(8,128)(2,1)S(1)}, bf16[64,512]{1,0:T(8,128)(2,1)S(1)}, u32[]{:S(2)}, u32[]{:S(2)}) collective-permute-start(bf16[64,512]{1,0:T(8,128)(2,1)S(1)} %get-tuple-element.62), channel_id=1, source_target_pairs={{0,4},{1,5},{2,6},{3,7},{4,8},{5,9},{6,10},{7,11},{8,12},{9,13},{1... | collective-permute-start | bytes 196616 | tf_op jit(solution)/shard_map/ppermute | solution.py:29
  97.4 6.2 %collective-permute-start.11 = (bf16[64,512]{1,0:T(8,128)(2,1)S(1)}, bf16[64,512]{1,0:T(8,128)(2,1)S(1)}, u32[]{:S(2)}, u32[]{:S(2)}) collective-permute-start(bf16[64,512]{1,0:T(8,128)(2,1)S(1)} %get-tuple-element.63), channel_id=1, source_target_pairs={{0,8},{1,9},{2,10},{3,11},{4,12},{5,13},{6,14},{7,15},{8,16},{9,17... | collective-permute-start | bytes 196616 | tf_op jit(solution)/shard_map/ppermute | solution.py:29
  99.4 8.3 %collective-permute-start.12 = (bf16[64,512]{1,0:T(8,128)(2,1)S(1)}, bf16[64,512]{1,0:T(8,128)(2,1)S(1)}, u32[]{:S(2)}, u32[]{:S(2)}) collective-permute-start(bf16[64,512]{1,0:T(8,128)(2,1)S(1)} %get-tuple-element.64), channel_id=1, source_target_pairs={{0,12},{1,13},{2,14},{3,15},{4,16},{5,17},{6,18},{7,19},{8,20},{9,... | collective-permute-start | bytes 196616 | tf_op jit(solution)/shard_map/ppermute | solution.py:29
  103.6 6.5 %collective-permute-start.13 = (bf16[64,512]{1,0:T(8,128)(2,1)S(1)}, bf16[64,512]{1,0:T(8,128)(2,1)S(1)}, u32[]{:S(2)}, u32[]{:S(2)}) collective-permute-start(bf16[64,512]{1,0:T(8,128)(2,1)S(1)} %get-tuple-element.65), channel_id=1, source_target_pairs={{0,16},{1,17},{2,18},{3,19},{4,20},{5,21},{6,22},{7,23},{8,24},{9,... | collective-permute-start | bytes 196616 | tf_op jit(solution)/shard_map/ppermute | solution.py:29
  103.7 7.5 %collective-permute-start.14 = (bf16[64,512]{1,0:T(8,128)(2,1)S(1)}, bf16[64,512]{1,0:T(8,128)(2,1)S(1)}, u32[]{:S(2)}, u32[]{:S(2)}) collective-permute-start(bf16[64,512]{1,0:T(8,128)(2,1)S(1)} %get-tuple-element.66), channel_id=1, source_target_pairs={{0,20},{1,21},{2,22},{3,23},{4,24},{5,25},{6,26},{7,27},{8,28},{9,... | collective-permute-start | bytes 196616 | tf_op jit(solution)/shard_map/ppermute | solution.py:29
  107.7 4.6 %collective-permute-start.15 = (bf16[64,512]{1,0:T(8,128)(2,1)S(1)}, bf16[64,512]{1,0:T(8,128)(2,1)S(1)}, u32[]{:S(2)}, u32[]{:S(2)}) collective-permute-start(bf16[64,512]{1,0:T(8,128)(2,1)S(1)} %get-tuple-element.67), channel_id=1, source_target_pairs={{0,24},{1,25},{2,26},{3,27},{4,28},{5,29},{6,30},{7,31},{8,0},{9,1... | collective-permute-start | bytes 196616 | tf_op jit(solution)/shard_map/ppermute | solution.py:29
  110.1 4.3 %collective-permute-start.16 = (bf16[64,512]{1,0:T(8,128)(2,1)S(1)}, bf16[64,512]{1,0:T(8,128)(2,1)S(1)}, u32[]{:S(2)}, u32[]{:S(2)}) collective-permute-start(bf16[64,512]{1,0:T(8,128)(2,1)S(1)} %get-tuple-element.68), channel_id=1, source_target_pairs={{0,28},{1,29},{2,30},{3,31},{4,0},{5,1},{6,2},{7,3},{8,4},{9,5},{1... | collective-permute-start | bytes 196616 | tf_op jit(solution)/shard_map/ppermute | solution.py:29
  115.4 11.4 %collective-permute-start.19 = (bf16[512,512]{1,0:T(8,128)(2,1)S(1)}, bf16[512,512]{1,0:T(8,128)(2,1)S(1)}, u32[]{:S(2)}, u32[]{:S(2)}) collective-permute-start(bf16[512,512]{1,0:T(8,128)(2,1)S(1)} %order.1.refs_0_), channel_id=1, source_target_pairs={{0,2},{1,3},{2,0},{3,1},{4,6},{5,7},{6,4},{7,5},{8,10},{9,11},{10,... | collective-permute-start | bytes 1572872 | tf_op jit(solution)/shard_map/ppermute | solution.py:29
  115.4 12.2 %collective-permute-start.22 = (bf16[512,512]{1,0:T(8,128)(2,1)}, bf16[512,512]{1,0:T(8,128)(2,1)S(1)}, u32[]{:S(2)}, u32[]{:S(2)}) collective-permute-start(bf16[512,512]{1,0:T(8,128)(2,1)} %collective-permute-done.17.refs_6_), channel_id=1, source_target_pairs={{0,8},{1,9},{2,10},{3,11},{4,0},{5,1},{6,2},{7,3},{8,16},{9,17},{1... | collective-permute-start | bytes 1572872 | tf_op jit(solution)/shard_map/ppermute | solution.py:29
  115.5 12.2 %collective-permute-start.23 = (bf16[512,512]{1,0:T(8,128)(2,1)}, bf16[512,512]{1,0:T(8,128)(2,1)S(1)}, u32[]{:S(2)}, u32[]{:S(2)}) collective-permute-start(bf16[512,512]{1,0:T(8,128)(2,1)} %collective-permute-done.18.refs_9_), channel_id=1, source_target_pairs={{0,4},{1,5},{2,6},{3,7},{4,12},{5,13},{6,14},{7,15},{8,0},{9,1},{1... | collective-permute-start | bytes 1572872 | tf_op jit(solution)/shard_map/ppermute | solution.py:29
  117.5 12.3 %collective-permute-start.20 = (bf16[512,512]{1,0:T(8,128)(2,1)S(1)}, bf16[512,512]{1,0:T(8,128)(2,1)S(1)}, u32[]{:S(2)}, u32[]{:S(2)}) collective-permute-start(bf16[512,512]{1,0:T(8,128)(2,1)S(1)} %order.1.refs_0_), channel_id=1, source_target_pairs={{0,1},{1,0},{2,3},{3,2},{4,5},{5,4},{6,7},{7,6},{8,9},{9,8},{10,11... | collective-permute-start | bytes 1572872 | tf_op jit(solution)/shard_map/ppermute | solution.py:29
  126.8 11.6 %collective-permute-start.21 = (bf16[512,512]{1,0:T(8,128)(2,1)S(1)}, bf16[512,512]{1,0:T(8,128)(2,1)S(1)}, u32[]{:S(2)}, u32[]{:S(2)}) collective-permute-start(bf16[512,512]{1,0:T(8,128)(2,1)S(1)} %collective-permute-done.19.refs_1_), channel_id=1, source_target_pairs={{0,1},{1,0},{2,3},{3,2},{4,5},{5,4},{6,7},{7,6},{8,9},{9,8},{10,11... | collective-permute-start | bytes 1572872 | tf_op jit(solution)/shard_map/ppermute | solution.py:29
  127.7 10.7 %copy-start.3 = (bf16[512,512]{1,0:T(8,128)(2,1)}, bf16[512,512]{1,0:T(8,128)(2,1)S(1)}, u32[]{:S(2)}) copy-start(bf16[512,512]{1,0:T(8,128)(2,1)S(1)} %collective-permute-done.22.refs_7_) | copy-start | bytes 1572868
  127.7 10.7 %copy-start.4 = (bf16[512,512]{1,0:T(8,128)(2,1)}, bf16[512,512]{1,0:T(8,128)(2,1)S(1)}, u32[]{:S(2)}) copy-start(bf16[512,512]{1,0:T(8,128)(2,1)S(1)} %collective-permute-done.23.refs_10_) | copy-start | bytes 1572868
  127.7 7.9 %collective-permute-start.25 = (bf16[256,512]{1,0:T(8,128)(2,1)S(1)}, bf16[256,512]{1,0:T(8,128)(2,1)S(1)}, u32[]{:S(2)}, u32[]{:S(2)}) collective-permute-start(bf16[256,512]{1,0:T(8,128)(2,1)S(1)} %slice.7), channel_id=1, source_target_pairs={{0,4},{1,5},{2,6},{3,7},{4,12},{5,13},{6,14},{7,15},{8,0},{9,1},{1... | collective-permute-start | bytes 786440 | tf_op jit(solution)/shard_map/ppermute | solution.py:29
  129.6 8.1 %collective-permute-start.24 = (bf16[256,512]{1,0:T(8,128)(2,1)S(1)}, bf16[256,512]{1,0:T(8,128)(2,1)S(1)}, u32[]{:S(2)}, u32[]{:S(2)}) collective-permute-start(bf16[256,512]{1,0:T(8,128)(2,1)S(1)} %slice.6), channel_id=1, source_target_pairs={{0,8},{1,9},{2,10},{3,11},{4,0},{5,1},{6,2},{7,3},{8,16},{9,17},{1... | collective-permute-start | bytes 786440 | tf_op jit(solution)/shard_map/ppermute | solution.py:29
  (5 other events, 7.7 us)

commit v3 on v2

--- a/solution.py
+++ b/solution.py
@@ -279,28 +279,30 @@
 
 def product_body(order, place_ref, *refs):
     side_refs = refs[:len(order)]
-    out_ref, sides_ref, sum_ref, wide_ref, arrived = refs[-5:]
-    block_refs = refs[len(order):-5]
+    out_ref, sides_ref, wide_ref, arrived = refs[-4:]
+    block_refs = refs[len(order):-4]
+    count = len(block_refs)
     full, cols = block_refs[0].shape
     copies = []
     for at, ref in enumerate(block_refs):
+        first = full // 2 if at == count - 1 else 0
+        start = pl.multiple_of(place_ref[PLACES + at] * full + first, full // 2)
         copies.append(
-            pltpu.make_async_copy(ref, wide_ref.at[at, :ref.shape[0]], arrived.at[at])
+            pltpu.make_async_copy(
+                ref,
+                wide_ref.at[place_ref[PLACES + count + at], pl.ds(start, ref.shape[0])],
+                arrived.at[at],
+            )
         )
         copies[-1].start()
     for flip, ref in zip(order, side_refs):
-        sides_ref[flip] = ref[...]
-    sum_ref[...] = jnp.zeros_like(sum_ref)
-    for at, ref in enumerate(block_refs):
-        rows = ref.shape[0]
-        first = full // 2 if at == len(block_refs) - 1 else 0
-        copies[at].wait()
-        side = sides_ref[place_ref[PLACES + at], :, first:first + rows]
-        sum_ref[place_ref[PLACES + len(block_refs) + at]] += jnp.dot(
-            side, wide_ref[at, :rows], preferred_element_type=F32
-        )
-    for low in range(sum_ref.shape[0]):
-        out_ref[:, low * cols:(low + 1) * cols] = sum_ref[low].astype(BF16)
+        sides_ref[:, flip * full:(flip + 1) * full] = ref[...]
+    for copy in copies:
+        copy.wait()
+    for low in range(wide_ref.shape[0]):
+        out_ref[:, low * cols:(low + 1) * cols] = jnp.dot(
+            sides_ref[...], wide_ref[low], preferred_element_type=F32
+        ).astype(BF16)
 
 
 def make_product(place, order, sides, blocks, lows):
@@ -316,9 +318,8 @@
         out_specs=vmem,
         out_shape=jax.ShapeDtypeStruct((length, lows * cols), BF16),
         scratch_shapes=[
-            pltpu.VMEM((len(sides), length, full), BF16),
-            pltpu.VMEM((lows, length, cols), F32),
-            pltpu.VMEM((len(blocks), rows, cols), BF16),
+            pltpu.VMEM((length, len(sides) * full), BF16),
+            pltpu.VMEM((lows, len(sides) * rows, cols), BF16),
             pltpu.SemaphoreType.DMA((len(blocks),)),
         ],
         name="product",
@@ -413,8 +414,7 @@
     taps = taps.reshape(taps.shape[0], 3 * own).T
     skip = lax.dynamic_slice_in_dim(skip_weight, channel_at, own, 0)[:, None]
     gain = lax.dynamic_slice_in_dim(norm_gain, high_at * columns, columns, 0)[None, :]
-    filters = make_filters(decay, weight, taps, skip)
-    (across,) = after((across,), gain, place, *filters)
+    (across,) = after((across,), gain, place, weights[0])
     holder = jnp.where(fsdp_at == high_at, embedding, across)
     beside = move(holder, lambda i, j: (i, j ^ 1) if j % 2 == i // lows % 2 else None)
 
@@ -431,6 +431,7 @@
             move(outgoing[shift], lambda i, j: ((i // lows + shift) % fsdp_count * lows + i % lows, j))
         )
 
+    filters = make_filters(*after((decay, weight, taps, skip), *outgoing))
     for _ in range(1, rounds - 1):
         pieces = list(after(pieces, ahead[-1], behind[-1]))
         turn(*pieces)

time: 146 us -> 152 us (1.041)
  waiting for transfers between devices: 59.6 us -> 67.3 us
  local copies, waits for them, and re-layouts: 10.4 us -> 14 us
  other arithmetic: 2.73 us -> 0.11 us
  starting transfers between devices: 44 us -> 41.9 us
    ppermute x26, waiting for transfers between devices: 59.6 us -> 67.3 us  [send(): return lax.ppermute(value, AXES, pairs)]
    select_n x1, other arithmetic: 2.73 us -> 0.11 us  [body(): holder = jnp.where(fsdp_at == high_at, embedding, across)]
    ppermute x26, starting transfers between devices: 44 us -> 41.9 us  [send(): return lax.ppermute(value, AXES, pairs)]
    unnamed x24 -> x32, local copies, waits for them, and re-layouts: 2.93 us -> 4.78 us
  transfers between devices with their start and end apart: 26 -> 26, of which waited for: 13 -> 14; matrix products, arithmetic and copies ran while one was open for 6% -> 7% of each run, Pallas kernels for 14% -> 14%
where the time goes in v3:
time: 152 us
  waiting for transfers between devices  67.3 us (44%)
  starting transfers between devices  41.9 us (28%)
  Pallas kernels  27.8 us (18%)
  local copies, waits for them, and re-layouts  14 us (9%)
    ppermute x26, waiting for transfers between devices, send(): return lax.ppermute(value, AXES, pairs)  67.3 us
    ppermute x26, starting transfers between devices, send(): return lax.ppermute(value, AXES, pairs)  41.9 us
    pallas_call x1, Pallas kernels, make_mixer(): pl.pallas_call(functools.partial(mixer_body, width, taps), in_specs=[pl.B...  11.4 us
    pallas_call x1, Pallas kernels, make_product(): pl.pallas_call(functools.partial(product_body, order), in_specs=[pl.Block...  6.19 us
    pallas_call x1, Pallas kernels, make_filters(): pl.pallas_call(filter_body, in_specs=[smem, smem] + [vmem] * 4, out_specs...  5.24 us
    unnamed x32, local copies, waits for them, and re-layouts  4.78 us
    pallas_call x1, Pallas kernels, make_table(): pl.pallas_call(functools.partial(table_body, len(weights)), in_specs=[pl....  4.06 us
  transfers between devices with their start and end apart: 26, of which 14 were waited for; matrix products, arithmetic and copies ran while one was open for 7% of the time, Pallas kernels for 14%

profile of v3, /device:TPU:0, one launch (start us, length us, event | category | flops | bytes accessed | tf_op | source)
XLA Modules:
  0.0 151.6 jit_solution(5372811702361160122)
XLA Ops:
  0.0 5.1 %collective-permute-start = (bf16[512,1024]{1,0:T(8,128)(2,1)}, bf16[512,1024]{1,0:T(8,128)(2,1)S(1)}, u32[]{:S(2)}, u32[]{:S(2)}) collective-permute-start(bf16[512,1024]{1,0:T(8,128)(2,1)} %own_ref.1), channel_id=1, source_target_pairs={{0,2},{4,6},{9,11},{13,15},{18,16},{22,20},{27,25},{31,29}} | collective-permute-start | bytes 3145736 | tf_op jit(solution)/shard_map/ppermute | solution.py:29
  5.1 2.2 %dynamic-slice_bitcast_fusion = bf16[3,512,256]{2,1,0:T(8,128)(2,1)} fusion(bf16[512,3,512]{2,0,1:T(8,128)(2,1)} %param.13, s32[]{:T(128)S(6)} %select_n.55), kind=kLoop, calls=%fused_computation.1 | loop fusion | bytes 1572868 | tf_op jit(solution)/shard_map/dynamic_slice | solution.py:376
  7.3 1.3 dynamic_slice.29
  8.6 1.3 fusion.place_ref
  9.9 2.1 %constant_dynamic-slice_fusion.refs_0_ = bf16[3,512,256]{2,1,0:T(8,128)(2,1)} fusion(bf16[3,512,512]{2,1,0:T(8,128)(2,1)} %bitcast.20, s32[]{:T(128)S(6)} %select_n.56), kind=kLoop, calls=%fused_computation.2 | loop fusion | bytes 1572868 | tf_op jit(solution)/shard_map/dynamic_slice | solution.py:381
  11.9 5.7 %collective-permute-done.across_ref = bf16[512,1024]{1,0:T(8,128)(2,1)S(1)} collective-permute-done((bf16[512,1024]{1,0:T(8,128)(2,1)}, bf16[512,1024]{1,0:T(8,128)(2,1)S(1)}, u32[]{:S(2)}, u32[]{:S(2)}) %collective-permute-start) | collective-permute-done | bytes 1048608 | tf_op jit(solution)/shard_map/ppermute | solution.py:29
  18.6 1.3 collective-permute-start.1
  20.0 1.5 collective-permute-start.7
  21.4 1.5 %collective-permute-start.2 = (bf16[3,512,256]{2,1,0:T(8,128)(2,1)S(1)}, bf16[3,512,256]{2,1,0:T(8,128)(2,1)S(1)}, u32[]{:S(2)}, u32[]{:S(2)}) collective-permute-start(bf16[3,512,256]{2,1,0:T(8,128)(2,1)S(1)} %copy-done.7), channel_id=1, source_target_pairs={{0,4},{1,5},{2,6},{3,7},{4,0},{5,1},{6,2},{7,3},{8,12},{9,13},{10,... | collective-permute-start | bytes 2359304 | tf_op jit(solution)/shard_map/ppermute | solution.py:29
  23.0 10.0 %collective-permute-start.8 = (bf16[512,512]{1,0:T(8,128)(2,1)}, bf16[512,512]{1,0:T(8,128)(2,1)}, u32[]{:S(2)}, u32[]{:S(2)}) collective-permute-start(bf16[512,512]{1,0:T(8,128)(2,1)} %collective-permute-done.7.refs_4_), channel_id=1, source_target_pairs={{0,8},{1,9},{2,10},{3,11},{4,0},{5,1},{6,2},{7,3},{8,16},{9,17},{1... | collective-permute-start | bytes 1572872 | tf_op jit(solution)/shard_map/ppermute | solution.py:29
  33.0 1.5 collective-permute-start.3
  34.5 15.6 %collective-permute-done.3.refs_3_ = s32[1,512]{1,0:T(1,128)S(1)} collective-permute-done((s32[1,512]{1,0:T(1,128)S(1)}, s32[1,512]{1,0:T(1,128)S(1)}, u32[]{:S(2)}, u32[]{:S(2)}) %collective-permute-start.3) | collective-permute-done | bytes 2080 | tf_op jit(solution)/shard_map/ppermute | solution.py:29
  51.9 4.1 %table.1 = (bf16[208,512]{1,0:T(8,128)(2,1)S(1)}, bf16[208,512]{1,0:T(8,128)(2,1)S(1)}, bf16[208,512]{1,0:T(8,128)(2,1)S(1)}, bf16[208,512]{1,0:T(8,128)(2,1)S(1)}) custom-call(s32[22]{0:T(128)} %fusion.place_ref, bf16[512,1024]{1,0:T(8,128)(2,1)} %own_ref.1, bf16[512,1024]{1,0:T(8,128)(2,1)} %copy-done.2, bf16[512,1024]{1,0:T(8,128)(2,1)} %copy-done.5, ...), custom_call_target="tpu_custom_call" | custom-call | tf_op jit(solution)/shard_map/table/pallas_call | solution.py:147
  56.1 6.1 %collective-permute-start.5 = (bf16[208,512]{1,0:T(8,128)(2,1)S(1)}, bf16[208,512]{1,0:T(8,128)(2,1)S(1)}, u32[]{:S(2)}, u32[]{:S(2)}) collective-permute-start(bf16[208,512]{1,0:T(8,128)(2,1)S(1)} %get-tuple-element.52), channel_id=1, source_target_pairs={{0,16},{1,17},{2,18},{3,19},{4,20},{5,21},{6,22},{7,23},{8,24},{9,... | collective-permute-start | bytes 638984 | tf_op jit(solution)/shard_map/ppermute | solution.py:29
  62.1 5.4 %collective-permute-done.4.refs_1_ = bf16[208,512]{1,0:T(8,128)(2,1)S(1)} collective-permute-done((bf16[208,512]{1,0:T(8,128)(2,1)S(1)}, bf16[208,512]{1,0:T(8,128)(2,1)S(1)}, u32[]{:S(2)}, u32[]{:S(2)}) %collective-permute-start.4) | collective-permute-done | bytes 213024 | tf_op jit(solution)/shard_map/ppermute | solution.py:29
  67.6 9.3 %collective-permute-done.5.refs_2_ = bf16[208,512]{1,0:T(8,128)(2,1)S(1)} collective-permute-done((bf16[208,512]{1,0:T(8,128)(2,1)S(1)}, bf16[208,512]{1,0:T(8,128)(2,1)S(1)}, u32[]{:S(2)}, u32[]{:S(2)}) %collective-permute-start.5) | collective-permute-done | bytes 213024 | tf_op jit(solution)/shard_map/ppermute | solution.py:29
  76.9 5.1 %collective-permute-start.17 = (bf16[512,512]{1,0:T(8,128)(2,1)}, bf16[512,512]{1,0:T(8,128)(2,1)}, u32[]{:S(2)}, u32[]{:S(2)}) collective-permute-start(bf16[512,512]{1,0:T(8,128)(2,1)} %collective-permute-done.8.refs_5_), channel_id=1, source_target_pairs={{0,8},{1,9},{2,10},{3,11},{4,0},{5,1},{6,2},{7,3},{8,16},{9,17},{1... | collective-permute-start | bytes 1572872 | tf_op jit(solution)/shard_map/ppermute | solution.py:29
  85.7 5.2 %filters.1 = (bf16[4,256,256]{2,1,0:T(8,128)(2,1)}, bf16[4,256,32]{2,1,0:T(8,128)(2,1)}, bf16[4,48,256]{2,1,0:T(8,128)(2,1)}, f32[4,1,16]{2,1,0:T(1,128)}, f32[192,128]{1,0:T(8,128)}) custom-call(f32[4,16]{1,0:T(4,128)} %bitcast.24, f32[4,16]{1,0:T(4,128)} %bitcast.22, f32[4,1,16]{2,1,0:T(1,128)} %bitcast.25, f32[4,1,16]{2,1,0:T(1,128)} %bitcast.23, ...), custom_call_target="tpu_custom_call" | custom-call | tf_op jit(solution)/shard_map/filters/pallas_call | solution.py:79
  90.9 11.4 %mixer.1 = (bf16[64,512]{1,0:T(8,128)(2,1)S(1)}, bf16[64,512]{1,0:T(8,128)(2,1)S(1)}, bf16[64,512]{1,0:T(8,128)(2,1)S(1)}, bf16[64,512]{1,0:T(8,128)(2,1)S(1)}, ...) custom-call(s32[22]{0:T(128)} %fusion.place_ref, ...), custom_call_target="tpu_custom_call" | custom-call | tf_op jit(solution)/shard_map/mixer/pallas_call | solution.py:240
  102.3 1.6 %collective-permute-start.10 = (bf16[64,512]{1,0:T(8,128)(2,1)S(1)}, bf16[64,512]{1,0:T(8,128)(2,1)S(1)}, u32[]{:S(2)}, u32[]{:S(2)}) collective-permute-start(bf16[64,512]{1,0:T(8,128)(2,1)S(1)} %get-tuple-element.70), channel_id=1, source_target_pairs={{0,4},{1,5},{2,6},{3,7},{4,8},{5,9},{6,10},{7,11},{8,12},{9,13},{1... | collective-permute-start | bytes 196616 | tf_op jit(solution)/shard_map/ppermute | solution.py:29
  103.9 2.0 %collective-permute-start.11 = (bf16[64,512]{1,0:T(8,128)(2,1)S(1)}, bf16[64,512]{1,0:T(8,128)(2,1)S(1)}, u32[]{:S(2)}, u32[]{:S(2)}) collective-permute-start(bf16[64,512]{1,0:T(8,128)(2,1)S(1)} %get-tuple-element.71), channel_id=1, source_target_pairs={{0,8},{1,9},{2,10},{3,11},{4,12},{5,13},{6,14},{7,15},{8,16},{9,17... | collective-permute-start | bytes 196616 | tf_op jit(solution)/shard_map/ppermute | solution.py:29
  105.9 3.9 %collective-permute-done.10.refs_1_ = bf16[64,512]{1,0:T(8,128)(2,1)S(1)} collective-permute-done((bf16[64,512]{1,0:T(8,128)(2,1)S(1)}, bf16[64,512]{1,0:T(8,128)(2,1)S(1)}, u32[]{:S(2)}, u32[]{:S(2)}) %collective-permute-start.10) | collective-permute-done | bytes 65568 | tf_op jit(solution)/shard_map/ppermute | solution.py:29
  110.7 3.7 %collective-permute-done.12.refs_3_ = bf16[64,512]{1,0:T(8,128)(2,1)S(1)} collective-permute-done((bf16[64,512]{1,0:T(8,128)(2,1)S(1)}, bf16[64,512]{1,0:T(8,128)(2,1)S(1)}, u32[]{:S(2)}, u32[]{:S(2)}) %collective-permute-start.12) | collective-permute-done | bytes 65568 | tf_op jit(solution)/shard_map/ppermute | solution.py:29
  115.2 1.8 %collective-permute-done.13.refs_4_ = bf16[64,512]{1,0:T(8,128)(2,1)S(1)} collective-permute-done((bf16[64,512]{1,0:T(8,128)(2,1)S(1)}, bf16[64,512]{1,0:T(8,128)(2,1)S(1)}, u32[]{:S(2)}, u32[]{:S(2)}) %collective-permute-start.13) | collective-permute-done | bytes 65568 | tf_op jit(solution)/shard_map/ppermute | solution.py:29
  118.0 1.1 collective-permute-done.15.refs_6_
  119.1 2.2 %collective-permute-done.16.refs_7_ = bf16[64,512]{1,0:T(8,128)(2,1)S(1)} collective-permute-done((bf16[64,512]{1,0:T(8,128)(2,1)S(1)}, bf16[64,512]{1,0:T(8,128)(2,1)S(1)}, u32[]{:S(2)}, u32[]{:S(2)}) %collective-permute-start.16) | collective-permute-done | bytes 65568 | tf_op jit(solution)/shard_map/ppermute | solution.py:29
  122.4 2.0 %collective-permute-start.23 = (bf16[512,512]{1,0:T(8,128)(2,1)}, bf16[512,512]{1,0:T(8,128)(2,1)S(1)}, u32[]{:S(2)}, u32[]{:S(2)}) collective-permute-start(bf16[512,512]{1,0:T(8,128)(2,1)} %collective-permute-done.18.refs_9_), channel_id=1, source_target_pairs={{0,4},{1,5},{2,6},{3,7},{4,12},{5,13},{6,14},{7,15},{8,0},{9,1},{1... | collective-permute-start | bytes 1572872 | tf_op jit(solution)/shard_map/ppermute | solution.py:29
  124.4 9.1 %collective-permute-done.19.refs_1_ = bf16[512,512]{1,0:T(8,128)(2,1)S(1)} collective-permute-done((bf16[512,512]{1,0:T(8,128)(2,1)S(1)}, bf16[512,512]{1,0:T(8,128)(2,1)S(1)}, u32[]{:S(2)}, u32[]{:S(2)}) %collective-permute-start.19) | collective-permute-done | bytes 524320 | tf_op jit(solution)/shard_map/ppermute | solution.py:29
  134.5 1.9 %collective-permute-start.25 = (bf16[256,512]{1,0:T(8,128)(2,1)S(1)}, bf16[256,512]{1,0:T(8,128)(2,1)S(1)}, u32[]{:S(2)}, u32[]{:S(2)}) collective-permute-start(bf16[256,512]{1,0:T(8,128)(2,1)S(1)} %slice.7), channel_id=1, source_target_pairs={{0,4},{1,5},{2,6},{3,7},{4,12},{5,13},{6,14},{7,15},{8,0},{9,1},{1... | collective-permute-start | bytes 786440 | tf_op jit(solution)/shard_map/ppermute | solution.py:29
  136.6 5.8 %collective-permute-done.25.refs_12_ = bf16[256,512]{1,0:T(8,128)(2,1)S(1)} collective-permute-done((bf16[256,512]{1,0:T(8,128)(2,1)S(1)}, bf16[256,512]{1,0:T(8,128)(2,1)S(1)}, u32[]{:S(2)}, u32[]{:S(2)}) %collective-permute-start.25) | collective-permute-done | bytes 262176 | tf_op jit(solution)/shard_map/ppermute | solution.py:29
  142.4 2.1 %collective-permute-done.24.refs_11_ = bf16[256,512]{1,0:T(8,128)(2,1)S(1)} collective-permute-done((bf16[256,512]{1,0:T(8,128)(2,1)S(1)}, bf16[256,512]{1,0:T(8,128)(2,1)S(1)}, u32[]{:S(2)}, u32[]{:S(2)}) %collective-permute-start.24) | collective-permute-done | bytes 262176 | tf_op jit(solution)/shard_map/ppermute | solution.py:29
  145.2 6.2 %product.1 = bf16[512,1024]{1,0:T(8,128)(2,1)} custom-call(s32[22]{0:T(128)} %fusion.place_ref, bf16[512,512]{1,0:T(8,128)(2,1)S(1)} %order.1.refs_0_, bf16[512,512]{1,0:T(8,128)(2,1)S(1)} %collective-permute-done.19.refs_1_, bf16[512,512]{1,0:T(8,128)(2,1)S(1)} %collective-permute-done.20.refs_2_, bf16[512,512]{1,0:T(8,128)(2,1)S(1)} %collective-permute-done.21.refs_3_, ...), custom_call_target="tpu_custom_call" | custom-call | tf_op jit(solution)/shard_map/product/pallas_call | solution.py:313
  (69 shorter events, 12.3 us)
Async XLA Ops:
  0.0 83.4 %copy-start = (f32[7,3,512]{2,0,1:T(8,128)S(1)}, f32[7,3,512]{2,0,1:T(8,128)}, u32[]{:S(2)}) copy-start(f32[7,3,512]{2,0,1:T(8,128)} %param.14) | copy-start | bytes 129028
  0.0 17.6 %collective-permute-start = (bf16[512,1024]{1,0:T(8,128)(2,1)}, bf16[512,1024]{1,0:T(8,128)(2,1)S(1)}, u32[]{:S(2)}, u32[]{:S(2)}) collective-permute-start(bf16[512,1024]{1,0:T(8,128)(2,1)} %own_ref.1), channel_id=1, source_target_pairs={{0,2},{4,6},{9,11},{13,15},{18,16},{22,20},{27,25},{31,29}} | collective-permute-start | bytes 3145736 | tf_op jit(solution)/shard_map/ppermute | solution.py:29
  5.1 12.5 %copy-start.1 = (bf16[512,1024]{1,0:T(8,128)(2,1)S(1)}, bf16[512,1024]{1,0:T(8,128)(2,1)}, u32[]{:S(2)}) copy-start(bf16[512,1024]{1,0:T(8,128)(2,1)} %own_ref.1) | copy-start | bytes 3145732
  17.6 15.3 %copy-start.12 = (s32[512]{0:T(512)S(1)}, s32[512]{0:T(512)}, u32[]{:S(2)}) copy-start(s32[512]{0:T(512)} %param.10) | copy-start | bytes 6148
  18.6 31.5 %collective-permute-start.1 = (bf16[512,1024]{1,0:T(8,128)(2,1)S(1)}, bf16[512,1024]{1,0:T(8,128)(2,1)S(1)}, u32[]{:S(2)}, u32[]{:S(2)}) collective-permute-start(bf16[512,1024]{1,0:T(8,128)(2,1)S(1)} %broadcast_select_fusion), channel_id=1, source_target_pairs={{0,1},{2,3},{4,5},{6,7},{9,8},{11,10},{13,12},{15,14},{16,17},{18,... | collective-permute-start | bytes 3145736 | tf_op jit(solution)/shard_map/ppermute | solution.py:29
  20.0 3.0 %collective-permute-start.7 = (bf16[512,512]{1,0:T(8,128)(2,1)S(1)}, bf16[512,512]{1,0:T(8,128)(2,1)}, u32[]{:S(2)}, u32[]{:S(2)}) collective-permute-start(bf16[512,512]{1,0:T(8,128)(2,1)S(1)} %copy-done.14), channel_id=1, source_target_pairs={{0,0},{1,16},{2,8},{3,24},{4,4},{5,20},{6,12},{7,28},{8,9},{9,25},... | collective-permute-start | bytes 1572872 | tf_op jit(solution)/shard_map/ppermute | solution.py:29
  21.4 28.6 %collective-permute-start.2 = (bf16[3,512,256]{2,1,0:T(8,128)(2,1)S(1)}, bf16[3,512,256]{2,1,0:T(8,128)(2,1)S(1)}, u32[]{:S(2)}, u32[]{:S(2)}) collective-permute-start(bf16[3,512,256]{2,1,0:T(8,128)(2,1)S(1)} %copy-done.7), channel_id=1, source_target_pairs={{0,4},{1,5},{2,6},{3,7},{4,0},{5,1},{6,2},{7,3},{8,12},{9,13},{10,... | collective-permute-start | bytes 2359304 | tf_op jit(solution)/shard_map/ppermute | solution.py:29
  23.0 39.2 %collective-permute-start.8 = (bf16[512,512]{1,0:T(8,128)(2,1)}, bf16[512,512]{1,0:T(8,128)(2,1)}, u32[]{:S(2)}, u32[]{:S(2)}) collective-permute-start(bf16[512,512]{1,0:T(8,128)(2,1)} %collective-permute-done.7.refs_4_), channel_id=1, source_target_pairs={{0,8},{1,9},{2,10},{3,11},{4,0},{5,1},{6,2},{7,3},{8,16},{9,17},{1... | collective-permute-start | bytes 1572872 | tf_op jit(solution)/shard_map/ppermute | solution.py:29
  33.0 29.2 %collective-permute-start.9 = (bf16[512,512]{1,0:T(8,128)(2,1)}, bf16[512,512]{1,0:T(8,128)(2,1)}, u32[]{:S(2)}, u32[]{:S(2)}) collective-permute-start(bf16[512,512]{1,0:T(8,128)(2,1)} %collective-permute-done.7.refs_4_), channel_id=1, source_target_pairs={{0,4},{1,5},{2,6},{3,7},{4,12},{5,13},{6,14},{7,15},{8,0},{9,1},{1... | collective-permute-start | bytes 1572872 | tf_op jit(solution)/shard_map/ppermute | solution.py:29
  33.0 49.0 %copy-start.10 = (f32[16,32]{1,0:T(8,128)S(1)}, f32[16,32]{1,0:T(8,128)}, u32[]{:S(2)}) copy-start(f32[16,32]{1,0:T(8,128)} %param.16) | copy-start | bytes 6148
  33.0 49.0 %copy-start.11 = (f32[16,32]{1,0:T(8,128)S(1)}, f32[16,32]{1,0:T(8,128)}, u32[]{:S(2)}) copy-start(f32[16,32]{1,0:T(8,128)} %param.15) | copy-start | bytes 6148
  33.0 17.1 %collective-permute-start.3 = (s32[1,512]{1,0:T(1,128)S(1)}, s32[1,512]{1,0:T(1,128)S(1)}, u32[]{:S(2)}, u32[]{:S(2)}) collective-permute-start(s32[1,512]{1,0:T(1,128)S(1)} %bitcast.28), channel_id=1, source_target_pairs={{0,4},{1,5},{2,6},{3,7},{4,0},{5,1},{6,2},{7,3},{8,12},{9,13},{10,... | collective-permute-start | bytes 6152 | tf_op jit(solution)/shard_map/ppermute | solution.py:29
  56.0 11.6 %collective-permute-start.4 = (bf16[208,512]{1,0:T(8,128)(2,1)S(1)}, bf16[208,512]{1,0:T(8,128)(2,1)S(1)}, u32[]{:S(2)}, u32[]{:S(2)}) collective-permute-start(bf16[208,512]{1,0:T(8,128)(2,1)S(1)} %get-tuple-element.51), channel_id=1, source_target_pairs={{0,8},{1,9},{2,10},{3,11},{4,12},{5,13},{6,14},{7,15},{8,16},{9,17... | collective-permute-start | bytes 638984 | tf_op jit(solution)/shard_map/ppermute | solution.py:29
  56.1 20.8 %collective-permute-start.5 = (bf16[208,512]{1,0:T(8,128)(2,1)S(1)}, bf16[208,512]{1,0:T(8,128)(2,1)S(1)}, u32[]{:S(2)}, u32[]{:S(2)}) collective-permute-start(bf16[208,512]{1,0:T(8,128)(2,1)S(1)} %get-tuple-element.52), channel_id=1, source_target_pairs={{0,16},{1,17},{2,18},{3,19},{4,20},{5,21},{6,22},{7,23},{8,24},{9,... | collective-permute-start | bytes 638984 | tf_op jit(solution)/shard_map/ppermute | solution.py:29
  62.1 14.7 %collective-permute-start.6 = (bf16[208,512]{1,0:T(8,128)(2,1)S(1)}, bf16[208,512]{1,0:T(8,128)(2,1)S(1)}, u32[]{:S(2)}, u32[]{:S(2)}) collective-permute-start(bf16[208,512]{1,0:T(8,128)(2,1)S(1)} %get-tuple-element.53), channel_id=1, source_target_pairs={{0,24},{1,25},{2,26},{3,27},{4,28},{5,29},{6,30},{7,31},{8,0},{9,1... | collective-permute-start | bytes 638984 | tf_op jit(solution)/shard_map/ppermute | solution.py:29
  76.9 44.4 %collective-permute-start.17 = (bf16[512,512]{1,0:T(8,128)(2,1)}, bf16[512,512]{1,0:T(8,128)(2,1)}, u32[]{:S(2)}, u32[]{:S(2)}) collective-permute-start(bf16[512,512]{1,0:T(8,128)(2,1)} %collective-permute-done.8.refs_5_), channel_id=1, source_target_pairs={{0,8},{1,9},{2,10},{3,11},{4,0},{5,1},{6,2},{7,3},{8,16},{9,17},{1... | collective-permute-start | bytes 1572872 | tf_op jit(solution)/shard_map/ppermute | solution.py:29
  82.0 39.3 %collective-permute-start.18 = (bf16[512,512]{1,0:T(8,128)(2,1)}, bf16[512,512]{1,0:T(8,128)(2,1)}, u32[]{:S(2)}, u32[]{:S(2)}) collective-permute-start(bf16[512,512]{1,0:T(8,128)(2,1)} %collective-permute-done.9.refs_8_), channel_id=1, source_target_pairs={{0,4},{1,5},{2,6},{3,7},{4,12},{5,13},{6,14},{7,15},{8,0},{9,1},{1... | collective-permute-start | bytes 1572872 | tf_op jit(solution)/shard_map/ppermute | solution.py:29
  102.3 7.5 %collective-permute-start.10 = (bf16[64,512]{1,0:T(8,128)(2,1)S(1)}, bf16[64,512]{1,0:T(8,128)(2,1)S(1)}, u32[]{:S(2)}, u32[]{:S(2)}) collective-permute-start(bf16[64,512]{1,0:T(8,128)(2,1)S(1)} %get-tuple-element.70), channel_id=1, source_target_pairs={{0,4},{1,5},{2,6},{3,7},{4,8},{5,9},{6,10},{7,11},{8,12},{9,13},{1... | collective-permute-start | bytes 196616 | tf_op jit(solution)/shard_map/ppermute | solution.py:29
  103.9 6.6 %collective-permute-start.11 = (bf16[64,512]{1,0:T(8,128)(2,1)S(1)}, bf16[64,512]{1,0:T(8,128)(2,1)S(1)}, u32[]{:S(2)}, u32[]{:S(2)}) collective-permute-start(bf16[64,512]{1,0:T(8,128)(2,1)S(1)} %get-tuple-element.71), channel_id=1, source_target_pairs={{0,8},{1,9},{2,10},{3,11},{4,12},{5,13},{6,14},{7,15},{8,16},{9,17... | collective-permute-start | bytes 196616 | tf_op jit(solution)/shard_map/ppermute | solution.py:29
  105.9 8.5 %collective-permute-start.12 = (bf16[64,512]{1,0:T(8,128)(2,1)S(1)}, bf16[64,512]{1,0:T(8,128)(2,1)S(1)}, u32[]{:S(2)}, u32[]{:S(2)}) collective-permute-start(bf16[64,512]{1,0:T(8,128)(2,1)S(1)} %get-tuple-element.72), channel_id=1, source_target_pairs={{0,12},{1,13},{2,14},{3,15},{4,16},{5,17},{6,18},{7,19},{8,20},{9,... | collective-permute-start | bytes 196616 | tf_op jit(solution)/shard_map/ppermute | solution.py:29
  109.8 7.2 %collective-permute-start.13 = (bf16[64,512]{1,0:T(8,128)(2,1)S(1)}, bf16[64,512]{1,0:T(8,128)(2,1)S(1)}, u32[]{:S(2)}, u32[]{:S(2)}) collective-permute-start(bf16[64,512]{1,0:T(8,128)(2,1)S(1)} %get-tuple-element.73), channel_id=1, source_target_pairs={{0,16},{1,17},{2,18},{3,19},{4,20},{5,21},{6,22},{7,23},{8,24},{9,... | collective-permute-start | bytes 196616 | tf_op jit(solution)/shard_map/ppermute | solution.py:29
  110.5 7.5 %collective-permute-start.14 = (bf16[64,512]{1,0:T(8,128)(2,1)S(1)}, bf16[64,512]{1,0:T(8,128)(2,1)S(1)}, u32[]{:S(2)}, u32[]{:S(2)}) collective-permute-start(bf16[64,512]{1,0:T(8,128)(2,1)S(1)} %get-tuple-element.74), channel_id=1, source_target_pairs={{0,20},{1,21},{2,22},{3,23},{4,24},{5,25},{6,26},{7,27},{8,28},{9,... | collective-permute-start | bytes 196616 | tf_op jit(solution)/shard_map/ppermute | solution.py:29
  114.4 4.7 %collective-permute-start.15 = (bf16[64,512]{1,0:T(8,128)(2,1)S(1)}, bf16[64,512]{1,0:T(8,128)(2,1)S(1)}, u32[]{:S(2)}, u32[]{:S(2)}) collective-permute-start(bf16[64,512]{1,0:T(8,128)(2,1)S(1)} %get-tuple-element.75), channel_id=1, source_target_pairs={{0,24},{1,25},{2,26},{3,27},{4,28},{5,29},{6,30},{7,31},{8,0},{9,1... | collective-permute-start | bytes 196616 | tf_op jit(solution)/shard_map/ppermute | solution.py:29
  117.0 4.3 %collective-permute-start.16 = (bf16[64,512]{1,0:T(8,128)(2,1)S(1)}, bf16[64,512]{1,0:T(8,128)(2,1)S(1)}, u32[]{:S(2)}, u32[]{:S(2)}) collective-permute-start(bf16[64,512]{1,0:T(8,128)(2,1)S(1)} %get-tuple-element.76), channel_id=1, source_target_pairs={{0,28},{1,29},{2,30},{3,31},{4,0},{5,1},{6,2},{7,3},{8,4},{9,5},{1... | collective-permute-start | bytes 196616 | tf_op jit(solution)/shard_map/ppermute | solution.py:29
  122.3 11.3 %collective-permute-start.19 = (bf16[512,512]{1,0:T(8,128)(2,1)S(1)}, bf16[512,512]{1,0:T(8,128)(2,1)S(1)}, u32[]{:S(2)}, u32[]{:S(2)}) collective-permute-start(bf16[512,512]{1,0:T(8,128)(2,1)S(1)} %order.1.refs_0_), channel_id=1, source_target_pairs={{0,2},{1,3},{2,0},{3,1},{4,6},{5,7},{6,4},{7,5},{8,10},{9,11},{10,... | collective-permute-start | bytes 1572872 | tf_op jit(solution)/shard_map/ppermute | solution.py:29
  122.4 12.1 %collective-permute-start.22 = (bf16[512,512]{1,0:T(8,128)(2,1)}, bf16[512,512]{1,0:T(8,128)(2,1)S(1)}, u32[]{:S(2)}, u32[]{:S(2)}) collective-permute-start(bf16[512,512]{1,0:T(8,128)(2,1)} %collective-permute-done.17.refs_6_), channel_id=1, source_target_pairs={{0,8},{1,9},{2,10},{3,11},{4,0},{5,1},{6,2},{7,3},{8,16},{9,17},{1... | collective-permute-start | bytes 1572872 | tf_op jit(solution)/shard_map/ppermute | solution.py:29
  122.4 12.0 %collective-permute-start.23 = (bf16[512,512]{1,0:T(8,128)(2,1)}, bf16[512,512]{1,0:T(8,128)(2,1)S(1)}, u32[]{:S(2)}, u32[]{:S(2)}) collective-permute-start(bf16[512,512]{1,0:T(8,128)(2,1)} %collective-permute-done.18.refs_9_), channel_id=1, source_target_pairs={{0,4},{1,5},{2,6},{3,7},{4,12},{5,13},{6,14},{7,15},{8,0},{9,1},{1... | collective-permute-start | bytes 1572872 | tf_op jit(solution)/shard_map/ppermute | solution.py:29
  124.4 12.2 %collective-permute-start.20 = (bf16[512,512]{1,0:T(8,128)(2,1)S(1)}, bf16[512,512]{1,0:T(8,128)(2,1)S(1)}, u32[]{:S(2)}, u32[]{:S(2)}) collective-permute-start(bf16[512,512]{1,0:T(8,128)(2,1)S(1)} %order.1.refs_0_), channel_id=1, source_target_pairs={{0,1},{1,0},{2,3},{3,2},{4,5},{5,4},{6,7},{7,6},{8,9},{9,8},{10,11... | collective-permute-start | bytes 1572872 | tf_op jit(solution)/shard_map/ppermute | solution.py:29
  133.5 11.7 %collective-permute-start.21 = (bf16[512,512]{1,0:T(8,128)(2,1)S(1)}, bf16[512,512]{1,0:T(8,128)(2,1)S(1)}, u32[]{:S(2)}, u32[]{:S(2)}) collective-permute-start(bf16[512,512]{1,0:T(8,128)(2,1)S(1)} %collective-permute-done.19.refs_1_), channel_id=1, source_target_pairs={{0,1},{1,0},{2,3},{3,2},{4,5},{5,4},{6,7},{7,6},{8,9},{9,8},{10,11... | collective-permute-start | bytes 1572872 | tf_op jit(solution)/shard_map/ppermute | solution.py:29
  134.4 10.8 %copy-start.3 = (bf16[512,512]{1,0:T(8,128)(2,1)}, bf16[512,512]{1,0:T(8,128)(2,1)S(1)}, u32[]{:S(2)}) copy-start(bf16[512,512]{1,0:T(8,128)(2,1)S(1)} %collective-permute-done.22.refs_7_) | copy-start | bytes 1572868
  134.5 7.9 %collective-permute-start.25 = (bf16[256,512]{1,0:T(8,128)(2,1)S(1)}, bf16[256,512]{1,0:T(8,128)(2,1)S(1)}, u32[]{:S(2)}, u32[]{:S(2)}) collective-permute-start(bf16[256,512]{1,0:T(8,128)(2,1)S(1)} %slice.7), channel_id=1, source_target_pairs={{0,4},{1,5},{2,6},{3,7},{4,12},{5,13},{6,14},{7,15},{8,0},{9,1},{1... | collective-permute-start | bytes 786440 | tf_op jit(solution)/shard_map/ppermute | solution.py:29
  136.4 8.1 %collective-permute-start.24 = (bf16[256,512]{1,0:T(8,128)(2,1)S(1)}, bf16[256,512]{1,0:T(8,128)(2,1)S(1)}, u32[]{:S(2)}, u32[]{:S(2)}) collective-permute-start(bf16[256,512]{1,0:T(8,128)(2,1)S(1)} %slice.6), channel_id=1, source_target_pairs={{0,8},{1,9},{2,10},{3,11},{4,0},{5,1},{6,2},{7,3},{8,16},{9,17},{1... | collective-permute-start | bytes 786440 | tf_op jit(solution)/shard_map/ppermute | solution.py:29
  (9 other events, 23.1 us)

commit v4 on v3

--- a/solution.py
+++ b/solution.py
@@ -160,10 +160,10 @@
 
 
 def mixer_body(width, taps, place_ref, near_ref, into_ref, outof_ref, step_ref, taps_ref, *refs):
-    query_ref, drive_ref, conv_ref, token_ref, stage_ref = refs[-5:]
+    query_ref, drive_ref, conv_ref, token_ref, stage_ref, found_ref, tap_ref = refs[-7:]
     ctx_at = place_ref[2]
-    out_refs = refs[-5 - token_ref.shape[0]:-5]
-    piece_refs = refs[:-5 - token_ref.shape[0]]
+    out_refs = refs[-7 - token_ref.shape[0]:-7]
+    piece_refs = refs[:-7 - token_ref.shape[0]]
     rows, vocab = piece_refs[0].shape
     rows -= EXTRA
     channels = rows // 3
@@ -184,21 +184,39 @@
         part = ref[EXTRA:, :].astype(F32)
         total = part if total is None else total + part
     table = (total * lax.rsqrt(squares * (1.0 / width) + 1e-05)).astype(BF16)
+    for lag in range(taps):
+        tap_ref[lag] = jnp.broadcast_to(taps_ref[:rows, lag:lag + 1], (rows, 128))
     ids = lax.broadcasted_iota(jnp.int32, (vocab, TILE), 0)
-    halo = jnp.zeros((rows, 128), F32)
-    for tile in range(length // TILE):
+    wide = TILE // 128
+    tiles = length // TILE
+
+    def look_up(tile):
         at = tile * TILE
         inside = at % block
         tokens = token_ref[at // block][:, inside:inside + TILE]
         hot = jnp.where(ids == tokens, 1.0, 0.0).astype(BF16)
-        projected = jnp.dot(table, hot, preferred_element_type=F32)
-        extended = jnp.concatenate([halo, projected], axis=1)
-        halo = projected[:, TILE - 128:]
-        short = taps_ref[:, 0:1] * projected
-        for lag in range(1, taps):
-            short += taps_ref[:, lag:lag + 1] * pltpu.roll(extended, lag, 1)[:, 128:]
-        query_ref[:, at:at + TILE] = short[:channels]
-        drive_ref[:, at:at + TILE] = short[channels:2 * channels] * short[2 * channels:]
+        here_ref = found_ref.at[tile % 2]
+        if tile == 0:
+            here_ref[:, :128] = jnp.zeros((rows, 128), F32)
+        else:
+            here_ref[:, :128] = found_ref[(tile - 1) % 2, :, TILE:]
+        here_ref[:, 128:] = jnp.dot(table, hot, preferred_element_type=F32)
+
+    def combine(tile, row):
+        extended = found_ref[tile % 2, row:row + 8, :]
+        short = None
+        for lag in range(taps):
+            moved = (pltpu.roll(extended, lag, 1) if lag else extended)[:, 128:]
+            term = jnp.concatenate([tap_ref[lag, row:row + 8]] * wide, axis=1) * moved
+            short = term if short is None else short + term
+        return short
+
+    for tile in range(tiles):
+        look_up(tile)
+        at = tile * TILE
+        for row in range(0, channels, 8):
+            query_ref[row:row + 8, at:at + TILE] = combine(tile, row)
+            drive_ref[row:row + 8, at:at + TILE] = combine(tile, channels + row) * combine(tile, 2 * channels + row)
     groups = near_ref.shape[0]
     per = channels // groups
     modes = step_ref.shape[2]
@@ -248,6 +266,8 @@
             pltpu.VMEM((length // CHUNK * (channels // groups), CHUNK), F32),
             pltpu.VMEM((blocks, 1, block), jnp.int32),
             pltpu.VMEM((blocks, channels, block), BF16),
+            pltpu.VMEM((2, rows, TILE + 128), F32),
+            pltpu.VMEM((taps, rows, 128), F32),
         ],
         name="mixer",
     )(place, *filters, *near(*pieces))

time: 152 us -> 149 us (0.980)
  Pallas kernels: 27.8 us -> 25.2 us
    pallas_call x1, Pallas kernels: 11.4 us -> 8.79 us  [make_mixer(): pl.pallas_call(functools.partial(mixer_body, width, taps), in_specs=[pl.B...]
  transfers between devices with their start and end apart: 26 -> 26, of which waited for: 14 -> 14; matrix products, arithmetic and copies ran while one was open for 7% -> 7% of each run, Pallas kernels for 14% -> 12%
where the time goes in v4:
time: 149 us
  waiting for transfers between devices  67.3 us (45%)
  starting transfers between devices  41.9 us (28%)
  Pallas kernels  25.2 us (17%)
  local copies, waits for them, and re-layouts  14 us (9%)
    ppermute x26, waiting for transfers between devices, send(): return lax.ppermute(value, AXES, pairs)  67.3 us
    ppermute x26, starting transfers between devices, send(): return lax.ppermute(value, AXES, pairs)  41.9 us
    pallas_call x1, Pallas kernels, make_mixer(): pl.pallas_call(functools.partial(mixer_body, width, taps), in_specs=[pl.B...  8.79 us
    pallas_call x1, Pallas kernels, make_product(): pl.pallas_call(functools.partial(product_body, order), in_specs=[pl.Block...  6.19 us
    pallas_call x1, Pallas kernels, make_filters(): pl.pallas_call(filter_body, in_specs=[smem, smem] + [vmem] * 4, out_specs...  5.24 us
    unnamed x32, local copies, waits for them, and re-layouts  4.78 us
    pallas_call x1, Pallas kernels, make_table(): pl.pallas_call(functools.partial(table_body, len(weights)), in_specs=[pl....  4.06 us
  transfers between devices with their start and end apart: 26, of which 14 were waited for; matrix products, arithmetic and copies ran while one was open for 7% of the time, Pallas kernels for 12%

profile of v4, /device:TPU:0, one launch (start us, length us, event | category | flops | bytes accessed | tf_op | source)
XLA Modules:
  0.0 149.0 jit_solution(7339907822535104295)
XLA Ops:
  0.0 5.1 %collective-permute-start = (bf16[512,1024]{1,0:T(8,128)(2,1)}, bf16[512,1024]{1,0:T(8,128)(2,1)S(1)}, u32[]{:S(2)}, u32[]{:S(2)}) collective-permute-start(bf16[512,1024]{1,0:T(8,128)(2,1)} %own_ref.1), channel_id=1, source_target_pairs={{0,2},{4,6},{9,11},{13,15},{18,16},{22,20},{27,25},{31,29}} | collective-permute-start | bytes 3145736 | tf_op jit(solution)/shard_map/ppermute | solution.py:29
  5.1 2.2 %dynamic-slice_bitcast_fusion = bf16[3,512,256]{2,1,0:T(8,128)(2,1)} fusion(bf16[512,3,512]{2,0,1:T(8,128)(2,1)} %param.13, s32[]{:T(128)S(6)} %select_n.55), kind=kLoop, calls=%fused_computation.1 | loop fusion | bytes 1572868 | tf_op jit(solution)/shard_map/dynamic_slice | solution.py:396
  7.3 1.3 dynamic_slice.29
  8.6 1.3 fusion.place_ref
  9.9 2.1 %constant_dynamic-slice_fusion.refs_0_ = bf16[3,512,256]{2,1,0:T(8,128)(2,1)} fusion(bf16[3,512,512]{2,1,0:T(8,128)(2,1)} %bitcast.20, s32[]{:T(128)S(6)} %select_n.56), kind=kLoop, calls=%fused_computation.2 | loop fusion | bytes 1572868 | tf_op jit(solution)/shard_map/dynamic_slice | solution.py:401
  11.9 5.7 %collective-permute-done.across_ref = bf16[512,1024]{1,0:T(8,128)(2,1)S(1)} collective-permute-done((bf16[512,1024]{1,0:T(8,128)(2,1)}, bf16[512,1024]{1,0:T(8,128)(2,1)S(1)}, u32[]{:S(2)}, u32[]{:S(2)}) %collective-permute-start) | collective-permute-done | bytes 1048608 | tf_op jit(solution)/shard_map/ppermute | solution.py:29
  18.6 1.3 collective-permute-start.1
  20.0 1.5 collective-permute-start.7
  21.4 1.5 %collective-permute-start.2 = (bf16[3,512,256]{2,1,0:T(8,128)(2,1)S(1)}, bf16[3,512,256]{2,1,0:T(8,128)(2,1)S(1)}, u32[]{:S(2)}, u32[]{:S(2)}) collective-permute-start(bf16[3,512,256]{2,1,0:T(8,128)(2,1)S(1)} %copy-done.7), channel_id=1, source_target_pairs={{0,4},{1,5},{2,6},{3,7},{4,0},{5,1},{6,2},{7,3},{8,12},{9,13},{10,... | collective-permute-start | bytes 2359304 | tf_op jit(solution)/shard_map/ppermute | solution.py:29
  23.0 10.0 %collective-permute-start.8 = (bf16[512,512]{1,0:T(8,128)(2,1)}, bf16[512,512]{1,0:T(8,128)(2,1)}, u32[]{:S(2)}, u32[]{:S(2)}) collective-permute-start(bf16[512,512]{1,0:T(8,128)(2,1)} %collective-permute-done.7.refs_4_), channel_id=1, source_target_pairs={{0,8},{1,9},{2,10},{3,11},{4,0},{5,1},{6,2},{7,3},{8,16},{9,17},{1... | collective-permute-start | bytes 1572872 | tf_op jit(solution)/shard_map/ppermute | solution.py:29
  33.0 1.5 %collective-permute-start.3 = (s32[1,512]{1,0:T(1,128)S(1)}, s32[1,512]{1,0:T(1,128)S(1)}, u32[]{:S(2)}, u32[]{:S(2)}) collective-permute-start(s32[1,512]{1,0:T(1,128)S(1)} %bitcast.28), channel_id=1, source_target_pairs={{0,4},{1,5},{2,6},{3,7},{4,0},{5,1},{6,2},{7,3},{8,12},{9,13},{10,... | collective-permute-start | bytes 6152 | tf_op jit(solution)/shard_map/ppermute | solution.py:29
  34.5 15.6 %collective-permute-done.3.refs_3_ = s32[1,512]{1,0:T(1,128)S(1)} collective-permute-done((s32[1,512]{1,0:T(1,128)S(1)}, s32[1,512]{1,0:T(1,128)S(1)}, u32[]{:S(2)}, u32[]{:S(2)}) %collective-permute-start.3) | collective-permute-done | bytes 2080 | tf_op jit(solution)/shard_map/ppermute | solution.py:29
  51.9 4.1 %table.1 = (bf16[208,512]{1,0:T(8,128)(2,1)S(1)}, bf16[208,512]{1,0:T(8,128)(2,1)S(1)}, bf16[208,512]{1,0:T(8,128)(2,1)S(1)}, bf16[208,512]{1,0:T(8,128)(2,1)S(1)}) custom-call(s32[22]{0:T(128)} %fusion.place_ref, bf16[512,1024]{1,0:T(8,128)(2,1)} %own_ref.1, bf16[512,1024]{1,0:T(8,128)(2,1)} %copy-done.2, bf16[512,1024]{1,0:T(8,128)(2,1)} %copy-done.5, ...), custom_call_target="tpu_custom_call" | custom-call | tf_op jit(solution)/shard_map/table/pallas_call | solution.py:147
  56.1 6.1 %collective-permute-start.5 = (bf16[208,512]{1,0:T(8,128)(2,1)S(1)}, bf16[208,512]{1,0:T(8,128)(2,1)S(1)}, u32[]{:S(2)}, u32[]{:S(2)}) collective-permute-start(bf16[208,512]{1,0:T(8,128)(2,1)S(1)} %get-tuple-element.52), channel_id=1, source_target_pairs={{0,16},{1,17},{2,18},{3,19},{4,20},{5,21},{6,22},{7,23},{8,24},{9,... | collective-permute-start | bytes 638984 | tf_op jit(solution)/shard_map/ppermute | solution.py:29
  62.1 5.4 %collective-permute-done.4.refs_1_ = bf16[208,512]{1,0:T(8,128)(2,1)S(1)} collective-permute-done((bf16[208,512]{1,0:T(8,128)(2,1)S(1)}, bf16[208,512]{1,0:T(8,128)(2,1)S(1)}, u32[]{:S(2)}, u32[]{:S(2)}) %collective-permute-start.4) | collective-permute-done | bytes 213024 | tf_op jit(solution)/shard_map/ppermute | solution.py:29
  67.6 9.3 %collective-permute-done.5.refs_2_ = bf16[208,512]{1,0:T(8,128)(2,1)S(1)} collective-permute-done((bf16[208,512]{1,0:T(8,128)(2,1)S(1)}, bf16[208,512]{1,0:T(8,128)(2,1)S(1)}, u32[]{:S(2)}, u32[]{:S(2)}) %collective-permute-start.5) | collective-permute-done | bytes 213024 | tf_op jit(solution)/shard_map/ppermute | solution.py:29
  76.9 5.1 %collective-permute-start.17 = (bf16[512,512]{1,0:T(8,128)(2,1)}, bf16[512,512]{1,0:T(8,128)(2,1)}, u32[]{:S(2)}, u32[]{:S(2)}) collective-permute-start(bf16[512,512]{1,0:T(8,128)(2,1)} %collective-permute-done.8.refs_5_), channel_id=1, source_target_pairs={{0,8},{1,9},{2,10},{3,11},{4,0},{5,1},{6,2},{7,3},{8,16},{9,17},{1... | collective-permute-start | bytes 1572872 | tf_op jit(solution)/shard_map/ppermute | solution.py:29
  85.7 5.2 %filters.1 = (bf16[4,256,256]{2,1,0:T(8,128)(2,1)}, bf16[4,256,32]{2,1,0:T(8,128)(2,1)}, bf16[4,48,256]{2,1,0:T(8,128)(2,1)}, f32[4,1,16]{2,1,0:T(1,128)}, f32[192,128]{1,0:T(8,128)}) custom-call(f32[4,16]{1,0:T(4,128)} %bitcast.24, f32[4,16]{1,0:T(4,128)} %bitcast.22, f32[4,1,16]{2,1,0:T(1,128)} %bitcast.25, f32[4,1,16]{2,1,0:T(1,128)} %bitcast.23, ...), custom_call_target="tpu_custom_call" | custom-call | tf_op jit(solution)/shard_map/filters/pallas_call | solution.py:79
  90.9 8.8 %mixer.1 = (bf16[64,512]{1,0:T(8,128)(2,1)S(1)}, bf16[64,512]{1,0:T(8,128)(2,1)S(1)}, bf16[64,512]{1,0:T(8,128)(2,1)S(1)}, bf16[64,512]{1,0:T(8,128)(2,1)S(1)}, ...) custom-call(s32[22]{0:T(128)} %fusion.place_ref, ...), custom_call_target="tpu_custom_call" | custom-call | tf_op jit(solution)/shard_map/mixer/pallas_call | solution.py:258
  99.7 1.6 %collective-permute-start.10 = (bf16[64,512]{1,0:T(8,128)(2,1)S(1)}, bf16[64,512]{1,0:T(8,128)(2,1)S(1)}, u32[]{:S(2)}, u32[]{:S(2)}) collective-permute-start(bf16[64,512]{1,0:T(8,128)(2,1)S(1)} %get-tuple-element.70), channel_id=1, source_target_pairs={{0,4},{1,5},{2,6},{3,7},{4,8},{5,9},{6,10},{7,11},{8,12},{9,13},{1... | collective-permute-start | bytes 196616 | tf_op jit(solution)/shard_map/ppermute | solution.py:29
  101.3 2.0 %collective-permute-start.11 = (bf16[64,512]{1,0:T(8,128)(2,1)S(1)}, bf16[64,512]{1,0:T(8,128)(2,1)S(1)}, u32[]{:S(2)}, u32[]{:S(2)}) collective-permute-start(bf16[64,512]{1,0:T(8,128)(2,1)S(1)} %get-tuple-element.71), channel_id=1, source_target_pairs={{0,8},{1,9},{2,10},{3,11},{4,12},{5,13},{6,14},{7,15},{8,16},{9,17... | collective-permute-start | bytes 196616 | tf_op jit(solution)/shard_map/ppermute | solution.py:29
  103.3 3.9 %collective-permute-done.10.refs_1_ = bf16[64,512]{1,0:T(8,128)(2,1)S(1)} collective-permute-done((bf16[64,512]{1,0:T(8,128)(2,1)S(1)}, bf16[64,512]{1,0:T(8,128)(2,1)S(1)}, u32[]{:S(2)}, u32[]{:S(2)}) %collective-permute-start.10) | collective-permute-done | bytes 65568 | tf_op jit(solution)/shard_map/ppermute | solution.py:29
  108.1 3.7 %collective-permute-done.12.refs_3_ = bf16[64,512]{1,0:T(8,128)(2,1)S(1)} collective-permute-done((bf16[64,512]{1,0:T(8,128)(2,1)S(1)}, bf16[64,512]{1,0:T(8,128)(2,1)S(1)}, u32[]{:S(2)}, u32[]{:S(2)}) %collective-permute-start.12) | collective-permute-done | bytes 65568 | tf_op jit(solution)/shard_map/ppermute | solution.py:29
  112.6 1.8 %collective-permute-done.13.refs_4_ = bf16[64,512]{1,0:T(8,128)(2,1)S(1)} collective-permute-done((bf16[64,512]{1,0:T(8,128)(2,1)S(1)}, bf16[64,512]{1,0:T(8,128)(2,1)S(1)}, u32[]{:S(2)}, u32[]{:S(2)}) %collective-permute-start.13) | collective-permute-done | bytes 65568 | tf_op jit(solution)/shard_map/ppermute | solution.py:29
  115.4 1.1 collective-permute-done.15.refs_6_
  116.5 2.2 %collective-permute-done.16.refs_7_ = bf16[64,512]{1,0:T(8,128)(2,1)S(1)} collective-permute-done((bf16[64,512]{1,0:T(8,128)(2,1)S(1)}, bf16[64,512]{1,0:T(8,128)(2,1)S(1)}, u32[]{:S(2)}, u32[]{:S(2)}) %collective-permute-start.16) | collective-permute-done | bytes 65568 | tf_op jit(solution)/shard_map/ppermute | solution.py:29
  119.8 2.0 %collective-permute-start.23 = (bf16[512,512]{1,0:T(8,128)(2,1)}, bf16[512,512]{1,0:T(8,128)(2,1)S(1)}, u32[]{:S(2)}, u32[]{:S(2)}) collective-permute-start(bf16[512,512]{1,0:T(8,128)(2,1)} %collective-permute-done.18.refs_9_), channel_id=1, source_target_pairs={{0,4},{1,5},{2,6},{3,7},{4,12},{5,13},{6,14},{7,15},{8,0},{9,1},{1... | collective-permute-start | bytes 1572872 | tf_op jit(solution)/shard_map/ppermute | solution.py:29
  121.8 9.1 %collective-permute-done.19.refs_1_ = bf16[512,512]{1,0:T(8,128)(2,1)S(1)} collective-permute-done((bf16[512,512]{1,0:T(8,128)(2,1)S(1)}, bf16[512,512]{1,0:T(8,128)(2,1)S(1)}, u32[]{:S(2)}, u32[]{:S(2)}) %collective-permute-start.19) | collective-permute-done | bytes 524320 | tf_op jit(solution)/shard_map/ppermute | solution.py:29
  131.9 1.9 %collective-permute-start.25 = (bf16[256,512]{1,0:T(8,128)(2,1)S(1)}, bf16[256,512]{1,0:T(8,128)(2,1)S(1)}, u32[]{:S(2)}, u32[]{:S(2)}) collective-permute-start(bf16[256,512]{1,0:T(8,128)(2,1)S(1)} %slice.7), channel_id=1, source_target_pairs={{0,4},{1,5},{2,6},{3,7},{4,12},{5,13},{6,14},{7,15},{8,0},{9,1},{1... | collective-permute-start | bytes 786440 | tf_op jit(solution)/shard_map/ppermute | solution.py:29
  134.0 5.8 %collective-permute-done.25.refs_12_ = bf16[256,512]{1,0:T(8,128)(2,1)S(1)} collective-permute-done((bf16[256,512]{1,0:T(8,128)(2,1)S(1)}, bf16[256,512]{1,0:T(8,128)(2,1)S(1)}, u32[]{:S(2)}, u32[]{:S(2)}) %collective-permute-start.25) | collective-permute-done | bytes 262176 | tf_op jit(solution)/shard_map/ppermute | solution.py:29
  139.8 2.1 %collective-permute-done.24.refs_11_ = bf16[256,512]{1,0:T(8,128)(2,1)S(1)} collective-permute-done((bf16[256,512]{1,0:T(8,128)(2,1)S(1)}, bf16[256,512]{1,0:T(8,128)(2,1)S(1)}, u32[]{:S(2)}, u32[]{:S(2)}) %collective-permute-start.24) | collective-permute-done | bytes 262176 | tf_op jit(solution)/shard_map/ppermute | solution.py:29
  142.6 6.2 %product.1 = bf16[512,1024]{1,0:T(8,128)(2,1)} custom-call(s32[22]{0:T(128)} %fusion.place_ref, bf16[512,512]{1,0:T(8,128)(2,1)S(1)} %order.1.refs_0_, bf16[512,512]{1,0:T(8,128)(2,1)S(1)} %collective-permute-done.19.refs_1_, bf16[512,512]{1,0:T(8,128)(2,1)S(1)} %collective-permute-done.20.refs_2_, bf16[512,512]{1,0:T(8,128)(2,1)S(1)} %collective-permute-done.21.refs_3_, ...), custom_call_target="tpu_custom_call" | custom-call | tf_op jit(solution)/shard_map/product/pallas_call | solution.py:333
  (69 shorter events, 12.3 us)
Async XLA Ops:
  0.0 83.4 %copy-start = (f32[7,3,512]{2,0,1:T(8,128)S(1)}, f32[7,3,512]{2,0,1:T(8,128)}, u32[]{:S(2)}) copy-start(f32[7,3,512]{2,0,1:T(8,128)} %param.14) | copy-start | bytes 129028
  0.0 17.6 %collective-permute-start = (bf16[512,1024]{1,0:T(8,128)(2,1)}, bf16[512,1024]{1,0:T(8,128)(2,1)S(1)}, u32[]{:S(2)}, u32[]{:S(2)}) collective-permute-start(bf16[512,1024]{1,0:T(8,128)(2,1)} %own_ref.1), channel_id=1, source_target_pairs={{0,2},{4,6},{9,11},{13,15},{18,16},{22,20},{27,25},{31,29}} | collective-permute-start | bytes 3145736 | tf_op jit(solution)/shard_map/ppermute | solution.py:29
  5.1 12.5 %copy-start.1 = (bf16[512,1024]{1,0:T(8,128)(2,1)S(1)}, bf16[512,1024]{1,0:T(8,128)(2,1)}, u32[]{:S(2)}) copy-start(bf16[512,1024]{1,0:T(8,128)(2,1)} %own_ref.1) | copy-start | bytes 3145732
  17.6 15.3 %copy-start.12 = (s32[512]{0:T(512)S(1)}, s32[512]{0:T(512)}, u32[]{:S(2)}) copy-start(s32[512]{0:T(512)} %param.10) | copy-start | bytes 6148
  18.6 31.5 %collective-permute-start.1 = (bf16[512,1024]{1,0:T(8,128)(2,1)S(1)}, bf16[512,1024]{1,0:T(8,128)(2,1)S(1)}, u32[]{:S(2)}, u32[]{:S(2)}) collective-permute-start(bf16[512,1024]{1,0:T(8,128)(2,1)S(1)} %broadcast_select_fusion), channel_id=1, source_target_pairs={{0,1},{2,3},{4,5},{6,7},{9,8},{11,10},{13,12},{15,14},{16,17},{18,... | collective-permute-start | bytes 3145736 | tf_op jit(solution)/shard_map/ppermute | solution.py:29
  20.0 3.0 %collective-permute-start.7 = (bf16[512,512]{1,0:T(8,128)(2,1)S(1)}, bf16[512,512]{1,0:T(8,128)(2,1)}, u32[]{:S(2)}, u32[]{:S(2)}) collective-permute-start(bf16[512,512]{1,0:T(8,128)(2,1)S(1)} %copy-done.14), channel_id=1, source_target_pairs={{0,0},{1,16},{2,8},{3,24},{4,4},{5,20},{6,12},{7,28},{8,9},{9,25},... | collective-permute-start | bytes 1572872 | tf_op jit(solution)/shard_map/ppermute | solution.py:29
  21.4 28.6 %collective-permute-start.2 = (bf16[3,512,256]{2,1,0:T(8,128)(2,1)S(1)}, bf16[3,512,256]{2,1,0:T(8,128)(2,1)S(1)}, u32[]{:S(2)}, u32[]{:S(2)}) collective-permute-start(bf16[3,512,256]{2,1,0:T(8,128)(2,1)S(1)} %copy-done.7), channel_id=1, source_target_pairs={{0,4},{1,5},{2,6},{3,7},{4,0},{5,1},{6,2},{7,3},{8,12},{9,13},{10,... | collective-permute-start | bytes 2359304 | tf_op jit(solution)/shard_map/ppermute | solution.py:29
  23.0 39.2 %collective-permute-start.8 = (bf16[512,512]{1,0:T(8,128)(2,1)}, bf16[512,512]{1,0:T(8,128)(2,1)}, u32[]{:S(2)}, u32[]{:S(2)}) collective-permute-start(bf16[512,512]{1,0:T(8,128)(2,1)} %collective-permute-done.7.refs_4_), channel_id=1, source_target_pairs={{0,8},{1,9},{2,10},{3,11},{4,0},{5,1},{6,2},{7,3},{8,16},{9,17},{1... | collective-permute-start | bytes 1572872 | tf_op jit(solution)/shard_map/ppermute | solution.py:29
  33.0 29.2 %collective-permute-start.9 = (bf16[512,512]{1,0:T(8,128)(2,1)}, bf16[512,512]{1,0:T(8,128)(2,1)}, u32[]{:S(2)}, u32[]{:S(2)}) collective-permute-start(bf16[512,512]{1,0:T(8,128)(2,1)} %collective-permute-done.7.refs_4_), channel_id=1, source_target_pairs={{0,4},{1,5},{2,6},{3,7},{4,12},{5,13},{6,14},{7,15},{8,0},{9,1},{1... | collective-permute-start | bytes 1572872 | tf_op jit(solution)/shard_map/ppermute | solution.py:29
  33.0 49.0 %copy-start.10 = (f32[16,32]{1,0:T(8,128)S(1)}, f32[16,32]{1,0:T(8,128)}, u32[]{:S(2)}) copy-start(f32[16,32]{1,0:T(8,128)} %param.16) | copy-start | bytes 6148
  33.0 49.0 %copy-start.11 = (f32[16,32]{1,0:T(8,128)S(1)}, f32[16,32]{1,0:T(8,128)}, u32[]{:S(2)}) copy-start(f32[16,32]{1,0:T(8,128)} %param.15) | copy-start | bytes 6148
  33.0 17.1 %collective-permute-start.3 = (s32[1,512]{1,0:T(1,128)S(1)}, s32[1,512]{1,0:T(1,128)S(1)}, u32[]{:S(2)}, u32[]{:S(2)}) collective-permute-start(s32[1,512]{1,0:T(1,128)S(1)} %bitcast.28), channel_id=1, source_target_pairs={{0,4},{1,5},{2,6},{3,7},{4,0},{5,1},{6,2},{7,3},{8,12},{9,13},{10,... | collective-permute-start | bytes 6152 | tf_op jit(solution)/shard_map/ppermute | solution.py:29
  56.0 11.6 %collective-permute-start.4 = (bf16[208,512]{1,0:T(8,128)(2,1)S(1)}, bf16[208,512]{1,0:T(8,128)(2,1)S(1)}, u32[]{:S(2)}, u32[]{:S(2)}) collective-permute-start(bf16[208,512]{1,0:T(8,128)(2,1)S(1)} %get-tuple-element.51), channel_id=1, source_target_pairs={{0,8},{1,9},{2,10},{3,11},{4,12},{5,13},{6,14},{7,15},{8,16},{9,17... | collective-permute-start | bytes 638984 | tf_op jit(solution)/shard_map/ppermute | solution.py:29
  56.1 20.8 %collective-permute-start.5 = (bf16[208,512]{1,0:T(8,128)(2,1)S(1)}, bf16[208,512]{1,0:T(8,128)(2,1)S(1)}, u32[]{:S(2)}, u32[]{:S(2)}) collective-permute-start(bf16[208,512]{1,0:T(8,128)(2,1)S(1)} %get-tuple-element.52), channel_id=1, source_target_pairs={{0,16},{1,17},{2,18},{3,19},{4,20},{5,21},{6,22},{7,23},{8,24},{9,... | collective-permute-start | bytes 638984 | tf_op jit(solution)/shard_map/ppermute | solution.py:29
  62.1 14.7 %collective-permute-start.6 = (bf16[208,512]{1,0:T(8,128)(2,1)S(1)}, bf16[208,512]{1,0:T(8,128)(2,1)S(1)}, u32[]{:S(2)}, u32[]{:S(2)}) collective-permute-start(bf16[208,512]{1,0:T(8,128)(2,1)S(1)} %get-tuple-element.53), channel_id=1, source_target_pairs={{0,24},{1,25},{2,26},{3,27},{4,28},{5,29},{6,30},{7,31},{8,0},{9,1... | collective-permute-start | bytes 638984 | tf_op jit(solution)/shard_map/ppermute | solution.py:29
  76.9 41.8 %collective-permute-start.17 = (bf16[512,512]{1,0:T(8,128)(2,1)}, bf16[512,512]{1,0:T(8,128)(2,1)}, u32[]{:S(2)}, u32[]{:S(2)}) collective-permute-start(bf16[512,512]{1,0:T(8,128)(2,1)} %collective-permute-done.8.refs_5_), channel_id=1, source_target_pairs={{0,8},{1,9},{2,10},{3,11},{4,0},{5,1},{6,2},{7,3},{8,16},{9,17},{1... | collective-permute-start | bytes 1572872 | tf_op jit(solution)/shard_map/ppermute | solution.py:29
  82.0 36.7 %collective-permute-start.18 = (bf16[512,512]{1,0:T(8,128)(2,1)}, bf16[512,512]{1,0:T(8,128)(2,1)}, u32[]{:S(2)}, u32[]{:S(2)}) collective-permute-start(bf16[512,512]{1,0:T(8,128)(2,1)} %collective-permute-done.9.refs_8_), channel_id=1, source_target_pairs={{0,4},{1,5},{2,6},{3,7},{4,12},{5,13},{6,14},{7,15},{8,0},{9,1},{1... | collective-permute-start | bytes 1572872 | tf_op jit(solution)/shard_map/ppermute | solution.py:29
  99.7 7.5 %collective-permute-start.10 = (bf16[64,512]{1,0:T(8,128)(2,1)S(1)}, bf16[64,512]{1,0:T(8,128)(2,1)S(1)}, u32[]{:S(2)}, u32[]{:S(2)}) collective-permute-start(bf16[64,512]{1,0:T(8,128)(2,1)S(1)} %get-tuple-element.70), channel_id=1, source_target_pairs={{0,4},{1,5},{2,6},{3,7},{4,8},{5,9},{6,10},{7,11},{8,12},{9,13},{1... | collective-permute-start | bytes 196616 | tf_op jit(solution)/shard_map/ppermute | solution.py:29
  101.3 6.6 %collective-permute-start.11 = (bf16[64,512]{1,0:T(8,128)(2,1)S(1)}, bf16[64,512]{1,0:T(8,128)(2,1)S(1)}, u32[]{:S(2)}, u32[]{:S(2)}) collective-permute-start(bf16[64,512]{1,0:T(8,128)(2,1)S(1)} %get-tuple-element.71), channel_id=1, source_target_pairs={{0,8},{1,9},{2,10},{3,11},{4,12},{5,13},{6,14},{7,15},{8,16},{9,17... | collective-permute-start | bytes 196616 | tf_op jit(solution)/shard_map/ppermute | solution.py:29
  103.3 8.5 %collective-permute-start.12 = (bf16[64,512]{1,0:T(8,128)(2,1)S(1)}, bf16[64,512]{1,0:T(8,128)(2,1)S(1)}, u32[]{:S(2)}, u32[]{:S(2)}) collective-permute-start(bf16[64,512]{1,0:T(8,128)(2,1)S(1)} %get-tuple-element.72), channel_id=1, source_target_pairs={{0,12},{1,13},{2,14},{3,15},{4,16},{5,17},{6,18},{7,19},{8,20},{9,... | collective-permute-start | bytes 196616 | tf_op jit(solution)/shard_map/ppermute | solution.py:29
  107.2 7.2 %collective-permute-start.13 = (bf16[64,512]{1,0:T(8,128)(2,1)S(1)}, bf16[64,512]{1,0:T(8,128)(2,1)S(1)}, u32[]{:S(2)}, u32[]{:S(2)}) collective-permute-start(bf16[64,512]{1,0:T(8,128)(2,1)S(1)} %get-tuple-element.73), channel_id=1, source_target_pairs={{0,16},{1,17},{2,18},{3,19},{4,20},{5,21},{6,22},{7,23},{8,24},{9,... | collective-permute-start | bytes 196616 | tf_op jit(solution)/shard_map/ppermute | solution.py:29
  107.9 7.5 %collective-permute-start.14 = (bf16[64,512]{1,0:T(8,128)(2,1)S(1)}, bf16[64,512]{1,0:T(8,128)(2,1)S(1)}, u32[]{:S(2)}, u32[]{:S(2)}) collective-permute-start(bf16[64,512]{1,0:T(8,128)(2,1)S(1)} %get-tuple-element.74), channel_id=1, source_target_pairs={{0,20},{1,21},{2,22},{3,23},{4,24},{5,25},{6,26},{7,27},{8,28},{9,... | collective-permute-start | bytes 196616 | tf_op jit(solution)/shard_map/ppermute | solution.py:29
  111.8 4.7 %collective-permute-start.15 = (bf16[64,512]{1,0:T(8,128)(2,1)S(1)}, bf16[64,512]{1,0:T(8,128)(2,1)S(1)}, u32[]{:S(2)}, u32[]{:S(2)}) collective-permute-start(bf16[64,512]{1,0:T(8,128)(2,1)S(1)} %get-tuple-element.75), channel_id=1, source_target_pairs={{0,24},{1,25},{2,26},{3,27},{4,28},{5,29},{6,30},{7,31},{8,0},{9,1... | collective-permute-start | bytes 196616 | tf_op jit(solution)/shard_map/ppermute | solution.py:29
  114.4 4.3 %collective-permute-start.16 = (bf16[64,512]{1,0:T(8,128)(2,1)S(1)}, bf16[64,512]{1,0:T(8,128)(2,1)S(1)}, u32[]{:S(2)}, u32[]{:S(2)}) collective-permute-start(bf16[64,512]{1,0:T(8,128)(2,1)S(1)} %get-tuple-element.76), channel_id=1, source_target_pairs={{0,28},{1,29},{2,30},{3,31},{4,0},{5,1},{6,2},{7,3},{8,4},{9,5},{1... | collective-permute-start | bytes 196616 | tf_op jit(solution)/shard_map/ppermute | solution.py:29
  119.7 11.3 %collective-permute-start.19 = (bf16[512,512]{1,0:T(8,128)(2,1)S(1)}, bf16[512,512]{1,0:T(8,128)(2,1)S(1)}, u32[]{:S(2)}, u32[]{:S(2)}) collective-permute-start(bf16[512,512]{1,0:T(8,128)(2,1)S(1)} %order.1.refs_0_), channel_id=1, source_target_pairs={{0,2},{1,3},{2,0},{3,1},{4,6},{5,7},{6,4},{7,5},{8,10},{9,11},{10,... | collective-permute-start | bytes 1572872 | tf_op jit(solution)/shard_map/ppermute | solution.py:29
  119.8 12.1 %collective-permute-start.22 = (bf16[512,512]{1,0:T(8,128)(2,1)}, bf16[512,512]{1,0:T(8,128)(2,1)S(1)}, u32[]{:S(2)}, u32[]{:S(2)}) collective-permute-start(bf16[512,512]{1,0:T(8,128)(2,1)} %collective-permute-done.17.refs_6_), channel_id=1, source_target_pairs={{0,8},{1,9},{2,10},{3,11},{4,0},{5,1},{6,2},{7,3},{8,16},{9,17},{1... | collective-permute-start | bytes 1572872 | tf_op jit(solution)/shard_map/ppermute | solution.py:29
  119.8 12.0 %collective-permute-start.23 = (bf16[512,512]{1,0:T(8,128)(2,1)}, bf16[512,512]{1,0:T(8,128)(2,1)S(1)}, u32[]{:S(2)}, u32[]{:S(2)}) collective-permute-start(bf16[512,512]{1,0:T(8,128)(2,1)} %collective-permute-done.18.refs_9_), channel_id=1, source_target_pairs={{0,4},{1,5},{2,6},{3,7},{4,12},{5,13},{6,14},{7,15},{8,0},{9,1},{1... | collective-permute-start | bytes 1572872 | tf_op jit(solution)/shard_map/ppermute | solution.py:29
  121.8 12.2 %collective-permute-start.20 = (bf16[512,512]{1,0:T(8,128)(2,1)S(1)}, bf16[512,512]{1,0:T(8,128)(2,1)S(1)}, u32[]{:S(2)}, u32[]{:S(2)}) collective-permute-start(bf16[512,512]{1,0:T(8,128)(2,1)S(1)} %order.1.refs_0_), channel_id=1, source_target_pairs={{0,1},{1,0},{2,3},{3,2},{4,5},{5,4},{6,7},{7,6},{8,9},{9,8},{10,11... | collective-permute-start | bytes 1572872 | tf_op jit(solution)/shard_map/ppermute | solution.py:29
  130.9 11.7 %collective-permute-start.21 = (bf16[512,512]{1,0:T(8,128)(2,1)S(1)}, bf16[512,512]{1,0:T(8,128)(2,1)S(1)}, u32[]{:S(2)}, u32[]{:S(2)}) collective-permute-start(bf16[512,512]{1,0:T(8,128)(2,1)S(1)} %collective-permute-done.19.refs_1_), channel_id=1, source_target_pairs={{0,1},{1,0},{2,3},{3,2},{4,5},{5,4},{6,7},{7,6},{8,9},{9,8},{10,11... | collective-permute-start | bytes 1572872 | tf_op jit(solution)/shard_map/ppermute | solution.py:29
  131.8 10.8 %copy-start.3 = (bf16[512,512]{1,0:T(8,128)(2,1)}, bf16[512,512]{1,0:T(8,128)(2,1)S(1)}, u32[]{:S(2)}) copy-start(bf16[512,512]{1,0:T(8,128)(2,1)S(1)} %collective-permute-done.22.refs_7_) | copy-start | bytes 1572868
  131.9 7.9 %collective-permute-start.25 = (bf16[256,512]{1,0:T(8,128)(2,1)S(1)}, bf16[256,512]{1,0:T(8,128)(2,1)S(1)}, u32[]{:S(2)}, u32[]{:S(2)}) collective-permute-start(bf16[256,512]{1,0:T(8,128)(2,1)S(1)} %slice.7), channel_id=1, source_target_pairs={{0,4},{1,5},{2,6},{3,7},{4,12},{5,13},{6,14},{7,15},{8,0},{9,1},{1... | collective-permute-start | bytes 786440 | tf_op jit(solution)/shard_map/ppermute | solution.py:29
  133.8 8.1 %collective-permute-start.24 = (bf16[256,512]{1,0:T(8,128)(2,1)S(1)}, bf16[256,512]{1,0:T(8,128)(2,1)S(1)}, u32[]{:S(2)}, u32[]{:S(2)}) collective-permute-start(bf16[256,512]{1,0:T(8,128)(2,1)S(1)} %slice.6), channel_id=1, source_target_pairs={{0,8},{1,9},{2,10},{3,11},{4,0},{5,1},{6,2},{7,3},{8,16},{9,17},{1... | collective-permute-start | bytes 786440 | tf_op jit(solution)/shard_map/ppermute | solution.py:29
  (9 other events, 23.1 us)
